TPU v7x, 512 devices: a whole 4x8x8 slice. The times are simulated.
512 devices in a mesh: segment: 4 (over x), chan: 16 (over y, core), dp: 8 (over z).
Axes of the slice: x: 4, y: 8, z: 8, core: 2. Of those that a mesh axis runs over, the one named last changes fastest.
Arguments:
- grad_top: bfloat16 [8, 1536, 256], P('dp', None, 'chan'), may hold values from -6 to 6
- inputs_one: bfloat16 [4, 8, 1536, 256], P('segment', 'dp', 'chan'), may hold values from -6 to 6
- conv_one: bfloat16 [4, 8, 1536, 256], P('segment', 'dp', 'chan'), may hold values from -130 to 130
- inputs_two: bfloat16 [4, 8, 1536, 256], P('segment', 'dp', 'chan'), may hold values from -6 to 6
- conv_two: bfloat16 [4, 8, 1536, 256], P('segment', 'dp', 'chan'), may hold values from -130 to 130
- proj_weight: bfloat16 [4, 2, 1536, 1536], P('segment', None, 'chan'), may hold values from -0.15625 to 0.15625
- conv_weight: bfloat16 [4, 2, 1536, 432], P('segment', None, 'chan'), may hold values from -0.3125 to 0.3125
- norm_gain: float32 [4, 2, 1536], P('segment', None, 'chan'), may hold values from 0.1 to 1.9
- norm_bias: float32 [4, 2, 1536], P('segment', None, 'chan'), may hold values from -4 to 4
Outputs:
- grad_latent: bfloat16 [4, 8, 1536, 256], P('segment', 'dp', None, 'chan')
- grad_proj: float32 [4, 2, 1536, 1536], P('segment', None, 'chan')
- grad_conv: float32 [4, 2, 1536, 432], P('segment', None, 'chan')
- grad_gain: float32 [4, 2, 1536], P('segment', None, 'chan')
- grad_bias: float32 [4, 2, 1536], P('segment', None, 'chan')
All inputs are finite; a program needn't handle non-finite values.
Results may differ from a plain program's by a relative error of at most 0.009.
Values may be sent and summed in bfloat16 or wider, within the bound.
No kernel may reach another device: no remote copies, remote signals or barrier semaphores. Data moves between devices by JAX's collectives and lax.ppermute only.
A program may use at most 64 MiB of HBM per device.

v0:
```python
import jax
import jax.numpy as jnp
from jax import lax
from jax.sharding import PartitionSpec as P

GS = 48
WW = 64


NORM_EPS = 1e-05


def passed_along(block, axis, distance):
    devices = range(lax.axis_size(axis))
    route = [(i - distance, i) for i in devices if i - distance in devices]
    return lax.ppermute(block, axis, route)


def shifted_cells(values, step_row, step_col, img_width):
    length = values.shape[2]
    margin = img_width + 1
    padded = jnp.pad(values, ((0, 0), (0, 0), (margin, margin)))
    start_at = margin + step_row * img_width + step_col
    part_view = lax.slice_in_dim(padded, start_at, start_at + length, axis=2)
    column = jnp.arange(length, dtype=jnp.int32) % img_width
    inside = (column + step_col >= 0) & (column + step_col < img_width)
    return jnp.where(inside, part_view, jnp.zeros((), values.dtype))


def norm_forward(saved_pre, gain_vec, bias_vec):
    chans, positions = saved_pre.shape
    groups_here = chans // GS
    pre = saved_pre.astype(jnp.float32).reshape(groups_here, GS, positions)
    centre = jnp.mean(pre, axis=(1, 2), keepdims=True)
    varied = jnp.mean(jnp.square(pre - centre), axis=(1, 2), keepdims=True)
    inv_std = lax.rsqrt(varied + NORM_EPS)
    normed = (pre - centre) * inv_std
    gain_grid = gain_vec.reshape(groups_here, GS, 1)
    scaled = normed * gain_grid + bias_vec.reshape(groups_here, GS, 1)
    gate_vals = jax.nn.sigmoid(scaled)
    act_bf = (scaled * gate_vals).astype(jnp.bfloat16).reshape(chans, positions)
    return (normed, scaled, gate_vals, inv_std, gain_grid, act_bf)


def conv_backward(grad_act, norm_state, saved_in, w_conv):
    normed, scaled, gate_vals, inv_std, gain_grid, act_bf = norm_state
    groups_here, _, positions = normed.shape
    chans = groups_here * GS
    grad_act = grad_act.reshape(groups_here, GS, positions)
    grad_norm = grad_act * (gate_vals * (1.0 + scaled * (1.0 - gate_vals)))
    gain_grad = jnp.sum(grad_norm * normed, axis=2).reshape(chans)
    bias_grad = jnp.sum(grad_norm, axis=2).reshape(chans)
    weighted = grad_norm * gain_grid
    first_mean = jnp.mean(weighted, axis=(1, 2), keepdims=True)
    second_mean = jnp.mean(weighted * normed, axis=(1, 2), keepdims=True)
    grad_pre = (inv_std * (weighted - first_mean - normed * second_mean)).astype(jnp.bfloat16)
    saved_grid = saved_in.reshape(groups_here, GS, positions)
    taps_w = w_conv.reshape(groups_here, GS, 9, GS)
    conv_parts = []
    back_sum = jnp.zeros((groups_here, GS, positions), jnp.float32)
    for tap_row in (-1, 0, 1):
        for tap_col in (-1, 0, 1):
            tap_at = 3 * (tap_row + 1) + tap_col + 1
            source = shifted_cells(saved_grid, tap_row, tap_col, WW)
            conv_parts.append(
                jnp.einsum("gop,gjp->goj", grad_pre, source, preferred_element_type=jnp.float32)
            )
            spread_back = jnp.einsum(
                "goj,gop->gjp",
                taps_w[:, :, tap_at, :],
                grad_pre,
                preferred_element_type=jnp.float32,
            )
            back_sum = back_sum + shifted_cells(spread_back, -tap_row, -tap_col, WW)
    conv_grad = jnp.stack(conv_parts, axis=2).reshape(chans, 9 * GS)
    branch = back_sum.reshape(chans, positions).astype(jnp.bfloat16)
    return (branch, conv_grad, gain_grad, bias_grad)


def block_sharded(grad_slab, saved_in, saved_pre, w_proj, w_conv, gain_vec, bias_vec):
    norm_state = norm_forward(saved_pre, gain_vec, bias_vec)
    act_bf = norm_state[5]
    grad_piece = lax.all_gather(grad_slab, "chan", axis=1, tiled=True)
    fresh = jnp.dot(w_proj, grad_piece, preferred_element_type=jnp.float32)
    weight_acc = lax.dot_general(
        act_bf, grad_piece, (((1,), (1,)), ((), ())), preferred_element_type=jnp.float32
    )
    branch, conv_grad, gain_grad, bias_grad = conv_backward(fresh, norm_state, saved_in, w_conv)
    returned = lax.all_to_all(branch, "chan", split_axis=1, concat_axis=0, tiled=True)
    out_slab = (grad_slab.astype(jnp.float32) + returned.astype(jnp.float32)).astype(jnp.bfloat16)
    return (out_slab, (weight_acc, conv_grad, gain_grad, bias_grad))


def take_micro(saved_all, index_at):
    return lax.dynamic_index_in_dim(saved_all[0], index_at, 0, keepdims=False)


def per_device(
    grad_top,
    inputs_one,
    conv_one,
    inputs_two,
    conv_two,
    proj_weight,
    conv_weight,
    norm_gain,
    norm_bias,
):
    segments = lax.axis_size("segment")
    segment_at = lax.axis_index("segment")
    local_mb = grad_top.shape[0]
    chans = conv_one.shape[2]
    width_all = proj_weight.shape[3]
    ticks = local_mb + segments - 1
    initial = (
        jnp.zeros(grad_top.shape[1:], jnp.bfloat16),
        jnp.zeros((1,) + grad_top.shape, jnp.bfloat16),
        jnp.zeros((2, chans, width_all), jnp.float32),
        jnp.zeros((2, chans, 9 * GS), jnp.float32),
        jnp.zeros((2, chans), jnp.float32),
        jnp.zeros((2, chans), jnp.float32),
    )

    def one_tick(tick_at, running):
        received, latent, proj_acc, conv_acc, gain_acc, bias_acc = running
        micro_at = tick_at - (segments - 1 - segment_at)
        is_valid = (micro_at >= 0) & (micro_at < local_mb)
        safe_mb = jnp.clip(micro_at, 0, local_mb - 1)
        top_grad = lax.dynamic_index_in_dim(grad_top, safe_mb, 0, keepdims=False)
        entering = jnp.where(segment_at == segments - 1, top_grad, received)
        mid_grad, grads_two = block_sharded(
            entering,
            take_micro(inputs_two, safe_mb),
            take_micro(conv_two, safe_mb),
            proj_weight[0, 1],
            conv_weight[0, 1],
            norm_gain[0, 1],
            norm_bias[0, 1],
        )
        out_grad, grads_one = block_sharded(
            mid_grad,
            take_micro(inputs_one, safe_mb),
            take_micro(conv_one, safe_mb),
            proj_weight[0, 0],
            conv_weight[0, 0],
            norm_gain[0, 0],
            norm_bias[0, 0],
        )
        weight_mask = is_valid.astype(jnp.float32)
        proj_acc = proj_acc + weight_mask * jnp.stack((grads_one[0], grads_two[0]))
        conv_acc = conv_acc + weight_mask * jnp.stack((grads_one[1], grads_two[1]))
        gain_acc = gain_acc + weight_mask * jnp.stack((grads_one[2], grads_two[2]))
        bias_acc = bias_acc + weight_mask * jnp.stack((grads_one[3], grads_two[3]))
        current = lax.dynamic_index_in_dim(latent[0], safe_mb, 0, keepdims=False)
        kept = jnp.where(is_valid, out_grad, current)
        latent = lax.dynamic_update_index_in_dim(latent, kept[None, None], safe_mb, 1)
        received = passed_along(out_grad, "segment", -1)
        return (received, latent, proj_acc, conv_acc, gain_acc, bias_acc)

    final = lax.fori_loop(0, ticks, one_tick, initial)
    latent = final[1]
    proj_sum, conv_sum, gain_sum, bias_sum = lax.psum(
        (final[2], final[3], final[4], final[5]), "dp"
    )
    return (latent, proj_sum[None], conv_sum[None], gain_sum[None], bias_sum[None])


def solution(mesh):
    return jax.shard_map(
        per_device,
        mesh=mesh,
        in_specs=(
            P("dp", None, "chan"),
            P("segment", "dp", "chan", None),
            P("segment", "dp", "chan", None),
            P("segment", "dp", "chan", None),
            P("segment", "dp", "chan", None),
            P("segment", None, "chan", None),
            P("segment", None, "chan", None),
            P("segment", None, "chan"),
            P("segment", None, "chan"),
        ),
        out_specs=(
            P("segment", "dp", None, "chan"),
            P("segment", None, "chan", None),
            P("segment", None, "chan", None),
            P("segment", None, "chan"),
            P("segment", None, "chan"),
        ),
        check_vma=False,
    )
```

profile of v0, /device:TPU:6, one launch (start us, length us, event | category | flops | bytes accessed | tf_op | source)
XLA Modules:
  0.0 469.3 jit_solution(2428649469921807830)
XLA Ops:
  7.3 1.8 copy.64
  9.6 356.3 %while.26 = (s32[]{:T(128)}, bf16[1536,16]{0,1:T(8,128)(2,1)S(1)}, bf16[1,1,1536,16]{2,3,1,0:T(8,128)(2,1)}, f32[2,96,1536]{2,1,0:T(8,128)S(1)}, f32[2,96,432]{1...) while((s32[]{:T(128)}, bf16[1536,16]{0,1:T(8,128)(2,1)S(1)}, ...), condition=%wide.region_21.22_spmd.clone, body=%wide.region_0.21_spmd.clone.sunk | while | flops 392720768 | bytes 27672152 | solution.py:160
  11.2 0.9 convert_reduce_fusion.5
  12.5 1.0 multiply_reduce_fusion.13
  14.7 19.7 %all_gather.24 = bf16[1536,256]{0,1:T(8,128)(2,1)S(1)} all-gather(bf16[1536,16]{0,1:T(8,128)(2,1)S(1)} %bitcast_select_fusion.3), channel_id=1, replica_groups=mesh['segment'=4,'chan'=16,'dp'=8] {'chan'}, dimensions={1}, use_global_device_ids=true | all-gather | bytes 835584 | tf_op jit(solution)/shard_map/while/body/eval_jaxpr/all_gather | solution.py:83
  34.4 2.0 multiply_reduce_fusion.14
  37.0 1.0 fusion.353
  40.7 4.4 all-to-all-start
  52.0 1.0 all-to-all-done
  53.2 18.4 %all_gather.25 = bf16[1536,256]{0,1:T(8,128)(2,1)S(1)} all-gather(bf16[1536,16]{0,1:T(8,128)(2,1)S(1)} %add_convert_fusion.4), channel_id=1, replica_groups=mesh['segment'=4,'chan'=16,'dp'=8] {'chan'}, dimensions={1}, use_global_device_ids=true | all-gather | bytes 835584 | tf_op jit(solution)/shard_map/while/body/eval_jaxpr/all_gather | solution.py:83
  71.6 2.0 multiply_reduce_fusion.15
  76.8 4.6 all-to-all-start.1
  81.5 0.8 fusion.369
  88.9 1.2 copy.167
  91.7 1.4 fusion.358
  93.2 2.7 collective-permute-start
  96.0 1.6 collective-permute-done
  99.2 0.9 convert_reduce_fusion.5
  100.5 1.0 multiply_reduce_fusion.13
  102.7 19.4 %all_gather.24 = bf16[1536,256]{0,1:T(8,128)(2,1)S(1)} all-gather(bf16[1536,16]{0,1:T(8,128)(2,1)S(1)} %bitcast_select_fusion.3), channel_id=1, replica_groups=mesh['segment'=4,'chan'=16,'dp'=8] {'chan'}, dimensions={1}, use_global_device_ids=true | all-gather | bytes 835584 | tf_op jit(solution)/shard_map/while/body/eval_jaxpr/all_gather | solution.py:83
  122.1 2.0 multiply_reduce_fusion.14
  124.7 1.0 fusion.353
  128.4 4.6 all-to-all-start
  139.9 1.0 all-to-all-done
  141.1 18.4 %all_gather.25 = bf16[1536,256]{0,1:T(8,128)(2,1)S(1)} all-gather(bf16[1536,16]{0,1:T(8,128)(2,1)S(1)} %add_convert_fusion.4), channel_id=1, replica_groups=mesh['segment'=4,'chan'=16,'dp'=8] {'chan'}, dimensions={1}, use_global_device_ids=true | all-gather | bytes 835584 | tf_op jit(solution)/shard_map/while/body/eval_jaxpr/all_gather | solution.py:83
  159.5 2.0 multiply_reduce_fusion.15
  164.7 4.6 all-to-all-start.1
  169.4 0.8 fusion.369
  176.8 1.2 copy.167
  179.6 1.4 fusion.358
  181.1 4.3 collective-permute-start
  185.4 1.6 collective-permute-done
  188.7 0.9 convert_reduce_fusion.5
  190.0 1.0 multiply_reduce_fusion.13
  192.1 19.4 %all_gather.24 = bf16[1536,256]{0,1:T(8,128)(2,1)S(1)} all-gather(bf16[1536,16]{0,1:T(8,128)(2,1)S(1)} %bitcast_select_fusion.3), channel_id=1, replica_groups=mesh['segment'=4,'chan'=16,'dp'=8] {'chan'}, dimensions={1}, use_global_device_ids=true | all-gather | bytes 835584 | tf_op jit(solution)/shard_map/while/body/eval_jaxpr/all_gather | solution.py:83
  211.5 2.0 multiply_reduce_fusion.14
  214.1 1.0 fusion.353
  217.8 4.6 all-to-all-start
  229.3 1.0 all-to-all-done
  230.5 18.4 %all_gather.25 = bf16[1536,256]{0,1:T(8,128)(2,1)S(1)} all-gather(bf16[1536,16]{0,1:T(8,128)(2,1)S(1)} %add_convert_fusion.4), channel_id=1, replica_groups=mesh['segment'=4,'chan'=16,'dp'=8] {'chan'}, dimensions={1}, use_global_device_ids=true | all-gather | bytes 835584 | tf_op jit(solution)/shard_map/while/body/eval_jaxpr/all_gather | solution.py:83
  249.0 2.0 multiply_reduce_fusion.15
  254.2 4.6 all-to-all-start.1
  266.2 1.2 copy.167
  269.1 1.4 fusion.358
  270.5 4.3 collective-permute-start
  274.9 1.6 collective-permute-done
  278.1 0.9 convert_reduce_fusion.5
  279.4 1.0 multiply_reduce_fusion.13
  281.6 19.4 %all_gather.24 = bf16[1536,256]{0,1:T(8,128)(2,1)S(1)} all-gather(bf16[1536,16]{0,1:T(8,128)(2,1)S(1)} %bitcast_select_fusion.3), channel_id=1, replica_groups=mesh['segment'=4,'chan'=16,'dp'=8] {'chan'}, dimensions={1}, use_global_device_ids=true | all-gather | bytes 835584 | tf_op jit(solution)/shard_map/while/body/eval_jaxpr/all_gather | solution.py:83
  301.0 2.0 multiply_reduce_fusion.14
  303.6 1.0 fusion.353
  307.3 4.6 all-to-all-start
  318.8 1.0 all-to-all-done
  320.0 18.4 %all_gather.25 = bf16[1536,256]{0,1:T(8,128)(2,1)S(1)} all-gather(bf16[1536,16]{0,1:T(8,128)(2,1)S(1)} %add_convert_fusion.4), channel_id=1, replica_groups=mesh['segment'=4,'chan'=16,'dp'=8] {'chan'}, dimensions={1}, use_global_device_ids=true | all-gather | bytes 835584 | tf_op jit(solution)/shard_map/while/body/eval_jaxpr/all_gather | solution.py:83
  338.4 2.0 multiply_reduce_fusion.15
  343.6 4.6 all-to-all-start.1
  355.7 1.2 copy.167
  358.5 1.4 fusion.358
  360.0 4.3 collective-permute-start
  364.3 1.6 collective-permute-done
  366.0 2.3 copy.65
  368.4 23.7 %all-reduce.18 = (f32[1,2,96]{2,1,0:T(2,128)}, f32[1,2,96]{2,1,0:T(2,128)}) all-reduce(f32[1,2,96]{2,1,0:T(2,128)S(1)} %bitcast.586, f32[1,2,96]{2,1,0:T(2,128)S(1)} %bitcast.587), channel_id=1, replica_groups=mesh['segment'=4,'chan'=16,'dp'=8] {'dp'}, use_global_device_ids=true, to_apply=%region_24.25 | all-reduce | flops 384 | bytes 3072 | tf_op jit(solution)/shard_map/psum | solution.py:162
  392.1 67.2 %all-reduce.22.cloned.1.call-done = (f32[1,2,96,1536]{3,2,1,0:T(8,128)}, f32[1,2,96,432]{3,2,1,0:T(8,128)}) async-done(((f32[1,2,96,1536]{3,2,1,0:T(8,128)}, f32[1,2,96,432]{3,2,1,0:T(8,128)}), (f32[1,2,96,1536]{3,2,1,0:T(8,128)}, f32[1,2,96,432]{3,2,1,0:T(8,128)})) %all-reduce.22.cloned.1.call-update) | async-done | bytes 1511440 | tf_op jit(solution)/shard_map/psum | solution.py:162
  459.3 2.4 copy.207
  (667 shorter events, 101.0 us)
Async XLA Ops:
  7.2 452.1 %all-reduce.22.cloned.1.call-start = ((), (), s32[]{:S(2)}) async-start(), calls=%async_computation.2 | async-start | bytes 3145728 | tf_op jit(solution)/shard_map/psum | solution.py:162
  9.7 29.8 %copy-start.30 = (pred[256]{0:T(512)(128)(4,1)}, pred[256]{0:T(512)(128)(4,1)S(1)}, u32[]{:S(2)}) copy-start(pred[256]{0:T(512)(128)(4,1)S(1)} %compare_and_fusion.7) | copy-start | bytes 772 | tf_op jit(solution)/shard_map/while
  9.7 29.8 %copy-start.27 = (pred[256]{0:T(512)(128)(4,1)}, pred[256]{0:T(512)(128)(4,1)S(1)}, u32[]{:S(2)}) copy-start(pred[256]{0:T(512)(128)(4,1)S(1)} %compare_and_fusion.8) | copy-start | bytes 772 | tf_op jit(solution)/shard_map/while
  39.5 9.8 %copy-start.7 = (bf16[1,1,96,256]{3,2,1,0:T(8,128)(2,1)S(1)}, bf16[1,1,96,256]{3,2,1,0:T(8,128)(2,1)}, u32[]{:S(2)}) copy-start(bf16[1,1,96,256]{3,2,1,0:T(8,128)(2,1)} %get-tuple-element.857) | copy-start | bytes 147460 | tf_op jit(solution)/shard_map/while
  39.8 9.5 %copy-start.31 = (pred[256]{0:T(512)(128)(4,1)S(1)}, pred[256]{0:T(512)(128)(4,1)}, u32[]{:S(2)}) copy-start(pred[256]{0:T(512)(128)(4,1)} %copy-done.30) | copy-start | bytes 772 | tf_op jit(solution)/shard_map/while
  39.8 9.9 %copy-start.28 = (pred[256]{0:T(512)(128)(4,1)S(1)}, pred[256]{0:T(512)(128)(4,1)}, u32[]{:S(2)}) copy-start(pred[256]{0:T(512)(128)(4,1)} %copy-done.27) | copy-start | bytes 772 | tf_op jit(solution)/shard_map/while
  40.7 12.3 %all-to-all-start = ((bf16[96,16,16]{0,2,1:T(8,128)(2,1)}), bf16[96,16,16]{0,2,1:T(8,128)(2,1)S(1)}, u32[]{:S(2)}, u32[]{:S(2)}) async-start(bf16[96,16,16]{0,2,1:T(8,128)(2,1)} %convert_element_type.430), calls=%async_computation | async-start | bytes 131072 | tf_op jit(solution)/shard_map/while/body/eval_jaxpr/all_to_all | solution.py:89
  52.0 19.6 %copy-start.22 = (f32[96]{0:T(128)S(1)}, f32[96]{0:T(128)}, u32[]{:S(2)}) copy-start(f32[96]{0:T(128)} %mul.953) | copy-start | bytes 1156 | tf_op jit(solution)/shard_map/while
  75.0 6.5 %copy-start.6 = (bf16[1,1,96,256]{3,2,1,0:T(8,128)(2,1)S(1)}, bf16[1,1,96,256]{3,2,1,0:T(8,128)(2,1)}, u32[]{:S(2)}) copy-start(bf16[1,1,96,256]{3,2,1,0:T(8,128)(2,1)} %get-tuple-element.856) | copy-start | bytes 147460 | tf_op jit(solution)/shard_map/while
  76.8 14.7 %all-to-all-start.1 = ((bf16[96,16,16]{0,2,1:T(8,128)(2,1)}), bf16[96,16,16]{0,2,1:T(8,128)(2,1)S(1)}, u32[]{:S(2)}, u32[]{:S(2)}) async-start(bf16[96,16,16]{0,2,1:T(8,128)(2,1)} %convert_element_type.431), calls=%async_computation.1 | async-start | bytes 131072 | tf_op jit(solution)/shard_map/while/body/eval_jaxpr/all_to_all | solution.py:89
  93.2 4.5 collective-permute-start
  97.7 29.5 %copy-start.30 = (pred[256]{0:T(512)(128)(4,1)}, pred[256]{0:T(512)(128)(4,1)S(1)}, u32[]{:S(2)}) copy-start(pred[256]{0:T(512)(128)(4,1)S(1)} %compare_and_fusion.7) | copy-start | bytes 772 | tf_op jit(solution)/shard_map/while
  97.7 29.5 %copy-start.27 = (pred[256]{0:T(512)(128)(4,1)}, pred[256]{0:T(512)(128)(4,1)S(1)}, u32[]{:S(2)}) copy-start(pred[256]{0:T(512)(128)(4,1)S(1)} %compare_and_fusion.8) | copy-start | bytes 772 | tf_op jit(solution)/shard_map/while
  126.5 6.5 %copy-start.2 = (bf16[1,1,96,256]{3,2,1,0:T(8,128)(2,1)S(1)}, bf16[1,1,96,256]{3,2,1,0:T(8,128)(2,1)}, u32[]{:S(2)}) copy-start(bf16[1,1,96,256]{3,2,1,0:T(8,128)(2,1)} %get-tuple-element.854) | copy-start | bytes 147460 | tf_op jit(solution)/shard_map/while
  127.2 10.0 %copy-start.7 = (bf16[1,1,96,256]{3,2,1,0:T(8,128)(2,1)S(1)}, bf16[1,1,96,256]{3,2,1,0:T(8,128)(2,1)}, u32[]{:S(2)}) copy-start(bf16[1,1,96,256]{3,2,1,0:T(8,128)(2,1)} %get-tuple-element.857) | copy-start | bytes 147460 | tf_op jit(solution)/shard_map/while
  127.5 9.7 %copy-start.31 = (pred[256]{0:T(512)(128)(4,1)S(1)}, pred[256]{0:T(512)(128)(4,1)}, u32[]{:S(2)}) copy-start(pred[256]{0:T(512)(128)(4,1)} %copy-done.30) | copy-start | bytes 772 | tf_op jit(solution)/shard_map/while
  127.5 10.1 %copy-start.28 = (pred[256]{0:T(512)(128)(4,1)S(1)}, pred[256]{0:T(512)(128)(4,1)}, u32[]{:S(2)}) copy-start(pred[256]{0:T(512)(128)(4,1)} %copy-done.27) | copy-start | bytes 772 | tf_op jit(solution)/shard_map/while
  128.4 12.5 %all-to-all-start = ((bf16[96,16,16]{0,2,1:T(8,128)(2,1)}), bf16[96,16,16]{0,2,1:T(8,128)(2,1)S(1)}, u32[]{:S(2)}, u32[]{:S(2)}) async-start(bf16[96,16,16]{0,2,1:T(8,128)(2,1)} %convert_element_type.430), calls=%async_computation | async-start | bytes 131072 | tf_op jit(solution)/shard_map/while/body/eval_jaxpr/all_to_all | solution.py:89
  139.9 19.6 %copy-start.22 = (f32[96]{0:T(128)S(1)}, f32[96]{0:T(128)}, u32[]{:S(2)}) copy-start(f32[96]{0:T(128)} %mul.953) | copy-start | bytes 1156 | tf_op jit(solution)/shard_map/while
  164.7 14.7 %all-to-all-start.1 = ((bf16[96,16,16]{0,2,1:T(8,128)(2,1)}), bf16[96,16,16]{0,2,1:T(8,128)(2,1)S(1)}, u32[]{:S(2)}, u32[]{:S(2)}) async-start(bf16[96,16,16]{0,2,1:T(8,128)(2,1)} %convert_element_type.431), calls=%async_computation.1 | async-start | bytes 131072 | tf_op jit(solution)/shard_map/while/body/eval_jaxpr/all_to_all | solution.py:89
  178.7 6.6 %copy-start.10 = (f32[2,96]{1,0:T(2,128)S(1)}, f32[2,96]{1,0:T(2,128)}, u32[]{:S(2)}) copy-start(f32[2,96]{1,0:T(2,128)} %get-tuple-element.824) | copy-start | bytes 2308 | tf_op jit(solution)/shard_map/while
  178.7 6.6 %copy-start.13 = (f32[2,96]{1,0:T(2,128)S(1)}, f32[2,96]{1,0:T(2,128)}, u32[]{:S(2)}) copy-start(f32[2,96]{1,0:T(2,128)} %get-tuple-element.825) | copy-start | bytes 2308 | tf_op jit(solution)/shard_map/while
  178.7 6.6 %copy-start.23 = (f32[96]{0:T(128)S(1)}, f32[96]{0:T(128)}, u32[]{:S(2)}) copy-start(f32[96]{0:T(128)} %get-tuple-element.792) | copy-start | bytes 1156 | tf_op jit(solution)/shard_map/while
  178.7 6.6 %copy-start.24 = (f32[96]{0:T(128)S(1)}, f32[96]{0:T(128)}, u32[]{:S(2)}) copy-start(f32[96]{0:T(128)} %get-tuple-element.794) | copy-start | bytes 1156 | tf_op jit(solution)/shard_map/while
  178.7 6.6 %copy-start.25 = (f32[96]{0:T(128)S(1)}, f32[96]{0:T(128)}, u32[]{:S(2)}) copy-start(f32[96]{0:T(128)} %get-tuple-element.793) | copy-start | bytes 1156 | tf_op jit(solution)/shard_map/while
  178.8 6.6 %copy-start.26 = (f32[96]{0:T(128)S(1)}, f32[96]{0:T(128)}, u32[]{:S(2)}) copy-start(f32[96]{0:T(128)} %get-tuple-element.795) | copy-start | bytes 1156 | tf_op jit(solution)/shard_map/while
  179.4 7.6 %copy-start.4 = (f32[2,96,432]{1,2,0:T(8,128)}, f32[2,96,432]{1,2,0:T(8,128)S(1)}, u32[]{:S(2)}) copy-start(f32[2,96,432]{1,2,0:T(8,128)S(1)} %fusion.378) | copy-start | bytes 995332 | tf_op jit(solution)/shard_map/while
  181.1 6.0 %collective-permute-start = (bf16[1536,16]{0,1:T(8,128)(2,1)S(1)}, bf16[1536,16]{0,1:T(8,128)(2,1)S(1)}, u32[]{:S(2)}, u32[]{:S(2)}) collective-permute-start(bf16[1536,16]{0,1:T(8,128)(2,1)S(1)} %get-tuple-element.790), channel_id=1, source_target_pairs={{128,0},{256,128},{384,256},{129,1},{257,129},{385,257},{130,2},{2... | collective-permute-start | bytes 147464 | tf_op jit(solution)/shard_map/while/body/eval_jaxpr/ppermute | solution.py:16
  187.1 29.5 %copy-start.30 = (pred[256]{0:T(512)(128)(4,1)}, pred[256]{0:T(512)(128)(4,1)S(1)}, u32[]{:S(2)}) copy-start(pred[256]{0:T(512)(128)(4,1)S(1)} %compare_and_fusion.7) | copy-start | bytes 772 | tf_op jit(solution)/shard_map/while
  187.1 29.5 %copy-start.27 = (pred[256]{0:T(512)(128)(4,1)}, pred[256]{0:T(512)(128)(4,1)S(1)}, u32[]{:S(2)}) copy-start(pred[256]{0:T(512)(128)(4,1)S(1)} %compare_and_fusion.8) | copy-start | bytes 772 | tf_op jit(solution)/shard_map/while
  215.9 6.5 %copy-start.2 = (bf16[1,1,96,256]{3,2,1,0:T(8,128)(2,1)S(1)}, bf16[1,1,96,256]{3,2,1,0:T(8,128)(2,1)}, u32[]{:S(2)}) copy-start(bf16[1,1,96,256]{3,2,1,0:T(8,128)(2,1)} %get-tuple-element.854) | copy-start | bytes 147460 | tf_op jit(solution)/shard_map/while
  216.6 10.0 %copy-start.7 = (bf16[1,1,96,256]{3,2,1,0:T(8,128)(2,1)S(1)}, bf16[1,1,96,256]{3,2,1,0:T(8,128)(2,1)}, u32[]{:S(2)}) copy-start(bf16[1,1,96,256]{3,2,1,0:T(8,128)(2,1)} %get-tuple-element.857) | copy-start | bytes 147460 | tf_op jit(solution)/shard_map/while
  216.9 9.7 %copy-start.31 = (pred[256]{0:T(512)(128)(4,1)S(1)}, pred[256]{0:T(512)(128)(4,1)}, u32[]{:S(2)}) copy-start(pred[256]{0:T(512)(128)(4,1)} %copy-done.30) | copy-start | bytes 772 | tf_op jit(solution)/shard_map/while
  216.9 10.1 %copy-start.28 = (pred[256]{0:T(512)(128)(4,1)S(1)}, pred[256]{0:T(512)(128)(4,1)}, u32[]{:S(2)}) copy-start(pred[256]{0:T(512)(128)(4,1)} %copy-done.27) | copy-start | bytes 772 | tf_op jit(solution)/shard_map/while
  217.8 12.5 %all-to-all-start = ((bf16[96,16,16]{0,2,1:T(8,128)(2,1)}), bf16[96,16,16]{0,2,1:T(8,128)(2,1)S(1)}, u32[]{:S(2)}, u32[]{:S(2)}) async-start(bf16[96,16,16]{0,2,1:T(8,128)(2,1)} %convert_element_type.430), calls=%async_computation | async-start | bytes 131072 | tf_op jit(solution)/shard_map/while/body/eval_jaxpr/all_to_all | solution.py:89
  229.3 19.6 %copy-start.22 = (f32[96]{0:T(128)S(1)}, f32[96]{0:T(128)}, u32[]{:S(2)}) copy-start(f32[96]{0:T(128)} %mul.953) | copy-start | bytes 1156 | tf_op jit(solution)/shard_map/while
  252.3 6.5 %copy-start.6 = (bf16[1,1,96,256]{3,2,1,0:T(8,128)(2,1)S(1)}, bf16[1,1,96,256]{3,2,1,0:T(8,128)(2,1)}, u32[]{:S(2)}) copy-start(bf16[1,1,96,256]{3,2,1,0:T(8,128)(2,1)} %get-tuple-element.856) | copy-start | bytes 147460 | tf_op jit(solution)/shard_map/while
  254.2 14.7 %all-to-all-start.1 = ((bf16[96,16,16]{0,2,1:T(8,128)(2,1)}), bf16[96,16,16]{0,2,1:T(8,128)(2,1)S(1)}, u32[]{:S(2)}, u32[]{:S(2)}) async-start(bf16[96,16,16]{0,2,1:T(8,128)(2,1)} %convert_element_type.431), calls=%async_computation.1 | async-start | bytes 131072 | tf_op jit(solution)/shard_map/while/body/eval_jaxpr/all_to_all | solution.py:89
  268.1 6.6 %copy-start.10 = (f32[2,96]{1,0:T(2,128)S(1)}, f32[2,96]{1,0:T(2,128)}, u32[]{:S(2)}) copy-start(f32[2,96]{1,0:T(2,128)} %get-tuple-element.824) | copy-start | bytes 2308 | tf_op jit(solution)/shard_map/while
  268.2 6.6 %copy-start.13 = (f32[2,96]{1,0:T(2,128)S(1)}, f32[2,96]{1,0:T(2,128)}, u32[]{:S(2)}) copy-start(f32[2,96]{1,0:T(2,128)} %get-tuple-element.825) | copy-start | bytes 2308 | tf_op jit(solution)/shard_map/while
  268.2 6.6 %copy-start.23 = (f32[96]{0:T(128)S(1)}, f32[96]{0:T(128)}, u32[]{:S(2)}) copy-start(f32[96]{0:T(128)} %get-tuple-element.792) | copy-start | bytes 1156 | tf_op jit(solution)/shard_map/while
  268.2 6.6 %copy-start.24 = (f32[96]{0:T(128)S(1)}, f32[96]{0:T(128)}, u32[]{:S(2)}) copy-start(f32[96]{0:T(128)} %get-tuple-element.794) | copy-start | bytes 1156 | tf_op jit(solution)/shard_map/while
  268.2 6.6 %copy-start.25 = (f32[96]{0:T(128)S(1)}, f32[96]{0:T(128)}, u32[]{:S(2)}) copy-start(f32[96]{0:T(128)} %get-tuple-element.793) | copy-start | bytes 1156 | tf_op jit(solution)/shard_map/while
  268.2 6.6 %copy-start.26 = (f32[96]{0:T(128)S(1)}, f32[96]{0:T(128)}, u32[]{:S(2)}) copy-start(f32[96]{0:T(128)} %get-tuple-element.795) | copy-start | bytes 1156 | tf_op jit(solution)/shard_map/while
  268.9 7.6 %copy-start.4 = (f32[2,96,432]{1,2,0:T(8,128)}, f32[2,96,432]{1,2,0:T(8,128)S(1)}, u32[]{:S(2)}) copy-start(f32[2,96,432]{1,2,0:T(8,128)S(1)} %fusion.378) | copy-start | bytes 995332 | tf_op jit(solution)/shard_map/while
  270.5 6.0 %collective-permute-start = (bf16[1536,16]{0,1:T(8,128)(2,1)S(1)}, bf16[1536,16]{0,1:T(8,128)(2,1)S(1)}, u32[]{:S(2)}, u32[]{:S(2)}) collective-permute-start(bf16[1536,16]{0,1:T(8,128)(2,1)S(1)} %get-tuple-element.790), channel_id=1, source_target_pairs={{128,0},{256,128},{384,256},{129,1},{257,129},{385,257},{130,2},{2... | collective-permute-start | bytes 147464 | tf_op jit(solution)/shard_map/while/body/eval_jaxpr/ppermute | solution.py:16
  276.5 29.5 %copy-start.30 = (pred[256]{0:T(512)(128)(4,1)}, pred[256]{0:T(512)(128)(4,1)S(1)}, u32[]{:S(2)}) copy-start(pred[256]{0:T(512)(128)(4,1)S(1)} %compare_and_fusion.7) | copy-start | bytes 772 | tf_op jit(solution)/shard_map/while
  276.6 29.5 %copy-start.27 = (pred[256]{0:T(512)(128)(4,1)}, pred[256]{0:T(512)(128)(4,1)S(1)}, u32[]{:S(2)}) copy-start(pred[256]{0:T(512)(128)(4,1)S(1)} %compare_and_fusion.8) | copy-start | bytes 772 | tf_op jit(solution)/shard_map/while
  305.4 6.5 %copy-start.2 = (bf16[1,1,96,256]{3,2,1,0:T(8,128)(2,1)S(1)}, bf16[1,1,96,256]{3,2,1,0:T(8,128)(2,1)}, u32[]{:S(2)}) copy-start(bf16[1,1,96,256]{3,2,1,0:T(8,128)(2,1)} %get-tuple-element.854) | copy-start | bytes 147460 | tf_op jit(solution)/shard_map/while
  306.1 10.0 %copy-start.7 = (bf16[1,1,96,256]{3,2,1,0:T(8,128)(2,1)S(1)}, bf16[1,1,96,256]{3,2,1,0:T(8,128)(2,1)}, u32[]{:S(2)}) copy-start(bf16[1,1,96,256]{3,2,1,0:T(8,128)(2,1)} %get-tuple-element.857) | copy-start | bytes 147460 | tf_op jit(solution)/shard_map/while
  306.4 9.7 %copy-start.31 = (pred[256]{0:T(512)(128)(4,1)S(1)}, pred[256]{0:T(512)(128)(4,1)}, u32[]{:S(2)}) copy-start(pred[256]{0:T(512)(128)(4,1)} %copy-done.30) | copy-start | bytes 772 | tf_op jit(solution)/shard_map/while
  306.4 10.1 %copy-start.28 = (pred[256]{0:T(512)(128)(4,1)S(1)}, pred[256]{0:T(512)(128)(4,1)}, u32[]{:S(2)}) copy-start(pred[256]{0:T(512)(128)(4,1)} %copy-done.27) | copy-start | bytes 772 | tf_op jit(solution)/shard_map/while
  307.3 12.5 %all-to-all-start = ((bf16[96,16,16]{0,2,1:T(8,128)(2,1)}), bf16[96,16,16]{0,2,1:T(8,128)(2,1)S(1)}, u32[]{:S(2)}, u32[]{:S(2)}) async-start(bf16[96,16,16]{0,2,1:T(8,128)(2,1)} %convert_element_type.430), calls=%async_computation | async-start | bytes 131072 | tf_op jit(solution)/shard_map/while/body/eval_jaxpr/all_to_all | solution.py:89
  318.8 19.6 %copy-start.22 = (f32[96]{0:T(128)S(1)}, f32[96]{0:T(128)}, u32[]{:S(2)}) copy-start(f32[96]{0:T(128)} %mul.953) | copy-start | bytes 1156 | tf_op jit(solution)/shard_map/while
  341.7 6.5 %copy-start.6 = (bf16[1,1,96,256]{3,2,1,0:T(8,128)(2,1)S(1)}, bf16[1,1,96,256]{3,2,1,0:T(8,128)(2,1)}, u32[]{:S(2)}) copy-start(bf16[1,1,96,256]{3,2,1,0:T(8,128)(2,1)} %get-tuple-element.856) | copy-start | bytes 147460 | tf_op jit(solution)/shard_map/while
  343.6 14.7 %all-to-all-start.1 = ((bf16[96,16,16]{0,2,1:T(8,128)(2,1)}), bf16[96,16,16]{0,2,1:T(8,128)(2,1)S(1)}, u32[]{:S(2)}, u32[]{:S(2)}) async-start(bf16[96,16,16]{0,2,1:T(8,128)(2,1)} %convert_element_type.431), calls=%async_computation.1 | async-start | bytes 131072 | tf_op jit(solution)/shard_map/while/body/eval_jaxpr/all_to_all | solution.py:89
  357.6 6.6 %copy-start.10 = (f32[2,96]{1,0:T(2,128)S(1)}, f32[2,96]{1,0:T(2,128)}, u32[]{:S(2)}) copy-start(f32[2,96]{1,0:T(2,128)} %get-tuple-element.824) | copy-start | bytes 2308 | tf_op jit(solution)/shard_map/while
  357.6 6.6 %copy-start.13 = (f32[2,96]{1,0:T(2,128)S(1)}, f32[2,96]{1,0:T(2,128)}, u32[]{:S(2)}) copy-start(f32[2,96]{1,0:T(2,128)} %get-tuple-element.825) | copy-start | bytes 2308 | tf_op jit(solution)/shard_map/while
  357.6 6.6 %copy-start.23 = (f32[96]{0:T(128)S(1)}, f32[96]{0:T(128)}, u32[]{:S(2)}) copy-start(f32[96]{0:T(128)} %get-tuple-element.792) | copy-start | bytes 1156 | tf_op jit(solution)/shard_map/while
  357.6 6.6 %copy-start.24 = (f32[96]{0:T(128)S(1)}, f32[96]{0:T(128)}, u32[]{:S(2)}) copy-start(f32[96]{0:T(128)} %get-tuple-element.794) | copy-start | bytes 1156 | tf_op jit(solution)/shard_map/while
  357.6 6.6 %copy-start.25 = (f32[96]{0:T(128)S(1)}, f32[96]{0:T(128)}, u32[]{:S(2)}) copy-start(f32[96]{0:T(128)} %get-tuple-element.793) | copy-start | bytes 1156 | tf_op jit(solution)/shard_map/while
  357.6 6.6 %copy-start.26 = (f32[96]{0:T(128)S(1)}, f32[96]{0:T(128)}, u32[]{:S(2)}) copy-start(f32[96]{0:T(128)} %get-tuple-element.795) | copy-start | bytes 1156 | tf_op jit(solution)/shard_map/while
  358.3 7.6 %copy-start.4 = (f32[2,96,432]{1,2,0:T(8,128)}, f32[2,96,432]{1,2,0:T(8,128)S(1)}, u32[]{:S(2)}) copy-start(f32[2,96,432]{1,2,0:T(8,128)S(1)} %fusion.378) | copy-start | bytes 995332 | tf_op jit(solution)/shard_map/while
  360.0 6.0 %collective-permute-start = (bf16[1536,16]{0,1:T(8,128)(2,1)S(1)}, bf16[1536,16]{0,1:T(8,128)(2,1)S(1)}, u32[]{:S(2)}, u32[]{:S(2)}) collective-permute-start(bf16[1536,16]{0,1:T(8,128)(2,1)S(1)} %get-tuple-element.790), channel_id=1, source_target_pairs={{128,0},{256,128},{384,256},{129,1},{257,129},{385,257},{130,2},{2... | collective-permute-start | bytes 147464 | tf_op jit(solution)/shard_map/while/body/eval_jaxpr/ppermute | solution.py:16
  (69 other events, 152.1 us)
Sparse Core Ops, SparseCore 0:
  368.5 90.7 all-reduce.21
where the time goes:
time: 472 us; the launch traced here: 469 us
  blocking collectives  175 us (37%)
  waiting for transfers between devices  77.7 us (16%)
  matrix products  66 us (14%)
  local copies, waits for them, and re-layouts  56 us (12%)
  starting transfers between devices  52.4 us (11%)
  other arithmetic  25.2 us (5%)
  between operations  14.1 us (3%)
    all_gather x8, blocking collectives, block_sharded(): grad_piece = lax.all_gather(grad_slab, 'chan', axis=1, tiled=True)  152 us
    psum x1, waiting for transfers between devices, per_device(): lax.psum((final[2], final[3], final[4], final[5]), 'dp')  67.2 us
    dot_general x72, matrix products, conv_backward(): jnp.einsum('gop,gjp->goj', grad_pre, source, preferred_element_type=jnp.f...  36.9 us
    all_to_all x8, starting transfers between devices, block_sharded(): lax.all_to_all(branch, 'chan', split_axis=1, concat_axis=0, tiled=True)  36.9 us
    psum x1, blocking collectives, per_device(): lax.psum((final[2], final[3], final[4], final[5]), 'dp')  23.7 us
    dot_general x8, matrix products, block_sharded(): fresh = jnp.dot(w_proj, grad_piece, preferred_element_type=jnp.float32)  15.9 us
    ppermute x4, starting transfers between devices, passed_along(): return lax.ppermute(block, axis, route)  15.5 us
    dot_general x72, matrix products, conv_backward(): jnp.einsum('goj,gop->gjp', taps_w[:, :, tap_at, :], grad_pre, preferred_e...  10.6 us
  transfers between devices with their start and end apart: 13, of which 9 were waited for; matrix products, arithmetic and copies ran while one was open for 13% of the time, Pallas kernels for 0%

commit v1 on v0

v1 whole, which is shorter than its diff:
```python
import functools

import jax
import jax.numpy as jnp
from jax import lax
from jax.experimental import pallas as pl
from jax.experimental.pallas import tpu as pltpu
from jax.sharding import PartitionSpec as P

GS = 48
WW = 64
NORM_EPS = 1e-05
TAIL = 512
F32 = jnp.float32
BF16 = jnp.bfloat16
VMEM = pl.BlockSpec(memory_space=pltpu.VMEM)
SMEM = pl.BlockSpec(memory_space=pltpu.SMEM)
ANY = pl.BlockSpec(memory_space=pl.ANY)
NT = (((1,), (1,)), ((), ()))
TN = (((0,), (0,)), ((), ()))
PARAMS = pltpu.CompilerParams(vmem_limit_bytes=48 * 1024 * 1024)


def total(block):
    return jnp.sum(jnp.sum(block, axis=1, keepdims=True), axis=0, keepdims=True)


def forward_kernel(h_ref, gain_ref, bias_ref, xhat_ref, slope_ref, rate_ref, act_ref):
    chans, positions = h_ref.shape
    scale = 1.0 / (GS * positions)
    for at in range(0, chans, GS):
        rows = slice(at, at + GS)
        pre = h_ref[rows, :].astype(F32)
        pre = pre - total(pre) * scale
        inv_std = lax.rsqrt(total(pre * pre) * scale + NORM_EPS)
        xhat = pre * inv_std
        gain = gain_ref[rows, :]
        n = xhat * gain + bias_ref[rows, :]
        sig = jax.nn.sigmoid(n)
        slope = sig * (1.0 + n * (1.0 - sig))
        xhat_ref[rows, :] = xhat
        slope_ref[rows, :] = slope
        rate_ref[rows, :] = slope * (gain * inv_std)
        act_ref[rows, :] = (n * sig).astype(BF16)


def forward(h, gain, bias):
    full = jax.ShapeDtypeStruct(h.shape, F32)
    return pl.pallas_call(
        forward_kernel,
        out_shape=(full, full, full, jax.ShapeDtypeStruct(h.shape, BF16)),
        in_specs=[VMEM] * 3,
        out_specs=[VMEM] * 4,
        compiler_params=PARAMS,
        name="norm_forward",
    )(h, gain, bias)


def shifted(value, step_row, step_col, row, col):
    length = value.shape[1]
    rows = length // WW
    by = step_row * WW + step_col
    if by == 0:
        return value
    moved = pltpu.roll(value, (-by) % length, axis=1)
    inside = None
    if step_row:
        inside = row < rows - 1 if step_row > 0 else row > 0
    if step_col:
        here = col < WW - 1 if step_col > 0 else col > 0
        inside = here if inside is None else inside & here
    return jnp.where(inside, moved, 0.0)


def grid_of(shape):
    lane = lax.broadcasted_iota(jnp.int32, shape, 1)
    return lane // WW, lane % WW


def block_kernel(
    first, flags_ref, g_ref, w_ref, wc_ref, xhat_ref, rate_ref, *refs
):
    if first:
        out_ref, keep_ref, sg_ref, sgh_ref, sga_ref, sem = refs
    else:
        _, _, _, _, out_ref, keep_ref, sg_ref, sgh_ref, sga_ref, sem = refs
    chans, positions = xhat_ref.shape
    scale = 1.0 / (GS * positions)
    valid = flags_ref[0] > 0
    keep = pltpu.make_async_copy(g_ref, sg_ref, sem)
    if first:
        keep.start()
    else:

        @pl.when(valid)
        def _():
            keep.start()

    own = pl.multiple_of(flags_ref[1] * chans, chans)
    ga = jnp.dot(w_ref[...], g_ref[...], preferred_element_type=F32)
    row, col = grid_of((GS, positions))
    for at in range(0, chans, GS):
        rows = slice(at, at + GS)
        xhat = xhat_ref[rows, :]
        rw = ga[rows, :] * rate_ref[rows, :]
        gh = rw - total(rw) * scale - xhat * (total(rw * xhat) * scale)
        gh = gh.astype(BF16)
        spread = lax.dot_general(wc_ref[rows, :], gh, TN, preferred_element_type=F32)
        branch = None
        for step_col in (-1, 0, 1):
            part = None
            for step_row in (-1, 0, 1):
                tap = 3 * (step_row + 1) + step_col + 1
                term = shifted(spread[tap * GS : (tap + 1) * GS, :], -step_row, 0, row, col)
                part = term if part is None else part + term
            part = shifted(part, 0, -step_col, row, col)
            branch = part if branch is None else branch + part
        mine = g_ref[pl.ds(own + at, GS), :].astype(F32)
        result = (mine + branch.astype(BF16).astype(F32)).astype(BF16)
        out_ref[rows, :] = result
        if first:
            sgh_ref[rows, :] = gh
            sga_ref[rows, :] = ga[rows, :]
            keep_ref[rows, :] = result
        else:

            @pl.when(valid)
            def _():
                sgh_ref[rows, :] = gh
                sga_ref[rows, :] = ga[rows, :]
                keep_ref[rows, :] = result

    if first:
        keep.wait()
    else:

        @pl.when(valid)
        def _():
            keep.wait()


def block(flags, g, w, wc, xhat, rate, saved):
    chans, positions = xhat.shape
    first = saved is None
    shapes = (
        jax.ShapeDtypeStruct((chans, positions), BF16),
        jax.ShapeDtypeStruct((chans, positions), BF16),
        jax.ShapeDtypeStruct(g.shape, BF16),
        jax.ShapeDtypeStruct((chans, positions), BF16),
        jax.ShapeDtypeStruct((chans, positions), F32),
    )
    saved = () if first else saved
    result = pl.pallas_call(
        functools.partial(block_kernel, first),
        out_shape=shapes,
        in_specs=[SMEM] + [VMEM] * 5 + ([] if first else [VMEM, ANY, VMEM, VMEM]),
        out_specs=[VMEM, VMEM, ANY, VMEM, VMEM],
        scratch_shapes=[pltpu.SemaphoreType.DMA],
        input_output_aliases={} if first else {6: 1, 7: 2, 8: 3, 9: 4},
        compiler_params=PARAMS,
        name="block_backward",
    )(flags, g, w, wc, xhat, rate, *saved)
    return result[0], result[1:]


def weights_kernel(*refs):
    out_ref, stack = refs[-2:]
    chans, positions = refs[0].shape
    width = out_ref.shape[1] - TAIL
    row, col = grid_of((GS, positions))
    lane = lax.broadcasted_iota(jnp.int32, (GS, TAIL), 1)
    stack[9 * GS :, :] = jnp.zeros((TAIL - 9 * GS, positions), BF16)
    for b in range(2):
        act_ref, g_ref, gh_ref, ga_ref, x_ref, xhat_ref, slope_ref = refs[7 * b : 7 * b + 7]
        at = b * chans
        out_ref[at : at + chans, :width] = lax.dot_general(
            act_ref[...], g_ref[...], NT, preferred_element_type=F32
        ).astype(BF16)
        for q in range(0, chans, GS):
            rows = slice(q, q + GS)
            x = x_ref[rows, :].astype(F32)
            for step_row in (-1, 0, 1):
                for step_col in (-1, 0, 1):
                    tap = 3 * (step_row + 1) + step_col + 1
                    stack[tap * GS : (tap + 1) * GS, :] = shifted(
                        x, step_row, step_col, row, col
                    ).astype(BF16)
            taps = lax.dot_general(gh_ref[rows, :], stack[...], NT, preferred_element_type=F32)
            gn = ga_ref[rows, :] * slope_ref[rows, :]
            by_gain = jnp.sum(gn * xhat_ref[rows, :], axis=1, keepdims=True)
            by_bias = jnp.sum(gn, axis=1, keepdims=True)
            taps = jnp.where(lane == 9 * GS, by_gain, taps)
            taps = jnp.where(lane == 9 * GS + 1, by_bias, taps)
            out_ref[at + q : at + q + GS, width:] = taps.astype(BF16)


def weight_grads(first, second, width):
    chans, positions = first[0].shape
    return pl.pallas_call(
        weights_kernel,
        out_shape=jax.ShapeDtypeStruct((2 * chans, width + TAIL), BF16),
        in_specs=[VMEM] * 14,
        out_specs=VMEM,
        scratch_shapes=[pltpu.VMEM((TAIL, positions), BF16)],
        compiler_params=PARAMS,
        name="weight_grads",
    )(*first, *second)


def reduce_kernel(in_ref, out_ref):
    count = in_ref.shape[0]
    acc = in_ref[0].astype(F32)
    for m in range(1, count):
        acc = acc + in_ref[m].astype(F32)
    done = acc.astype(BF16)
    for m in range(count):
        out_ref[m] = done


def spread_sum(parts):
    return pl.pallas_call(
        reduce_kernel,
        out_shape=jax.ShapeDtypeStruct(parts.shape, BF16),
        in_specs=[VMEM],
        out_specs=VMEM,
        compiler_params=PARAMS,
        name="sum_microbatches",
    )(parts)


def widen_kernel(in_ref, proj_ref, conv_ref, tail_ref):
    chans, width = proj_ref.shape[1:]
    for b in range(2):
        rows = slice(b * chans, (b + 1) * chans)
        proj_ref[b] = in_ref[rows, :width].astype(F32)
        conv_ref[b] = in_ref[rows, width : width + 9 * GS].astype(F32)
        tail_ref[b] = in_ref[rows, width + TAIL - 128 :].astype(F32)


def widen(sums, chans, width):
    return pl.pallas_call(
        widen_kernel,
        out_shape=(
            jax.ShapeDtypeStruct((2, chans, width), F32),
            jax.ShapeDtypeStruct((2, chans, 9 * GS), F32),
            jax.ShapeDtypeStruct((2, chans, 128), F32),
        ),
        in_specs=[VMEM],
        out_specs=[VMEM] * 3,
        compiler_params=PARAMS,
        name="widen",
    )(sums)


def per_device(
    grad_top,
    inputs_one,
    conv_one,
    inputs_two,
    conv_two,
    proj_weight,
    conv_weight,
    norm_gain,
    norm_bias,
):
    segments = lax.axis_size("segment")
    segment_at = lax.axis_index("segment")
    chan_at = lax.axis_index("chan")
    members = lax.axis_size("dp")
    chans, positions = conv_one.shape[2:]
    width = proj_weight.shape[3]

    w = (proj_weight[0, 0], proj_weight[0, 1])
    wc = (conv_weight[0, 0], conv_weight[0, 1])
    gain = norm_gain[0][:, :, None]
    bias = norm_bias[0][:, :, None]
    state = (
        forward(conv_one[0, 0], gain[0], bias[0]),
        forward(conv_two[0, 0], gain[1], bias[1]),
    )
    saved = [None, None]
    out = None
    for tick in range(segments):
        valid = (segment_at == segments - 1 - tick).astype(jnp.int32)
        flags = jnp.stack([valid, chan_at.astype(jnp.int32)])
        if tick == 0:
            g = lax.all_gather(grad_top[0], "chan", axis=1, tiled=True)
        else:
            lower = segments - 1 - tick
            pair = [[lower, lower + 1]]
            rest = [s for s in range(segments) if s not in pair[0]]
            groups = sorted(pair + [rest[i : i + 2] for i in range(0, len(rest), 2)])
            both = lax.all_gather(
                out, "segment", axis=0, tiled=True, axis_index_groups=groups
            )
            g = lax.all_gather(both[chans:], "chan", axis=0, tiled=True)
        for b in (1, 0):
            out, saved[b] = block(
                flags, g, w[b], wc[b], state[b][0], state[b][2], saved[b]
            )
            if b == 1:
                g = lax.all_gather(out, "chan", axis=0, tiled=True)

    latent = lax.all_to_all(saved[0][0], "chan", split_axis=1, concat_axis=0, tiled=True)
    saved_in = (inputs_one[0, 0], inputs_two[0, 0])
    grads = weight_grads(
        *(
            (state[b][3],) + tuple(saved[b][1:]) + (saved_in[b], state[b][0], state[b][1])
            for b in (0, 1)
        ),
        width,
    )
    parts = grads.reshape(members, 2 * chans // members, width + TAIL)
    parts = lax.all_to_all(parts, "dp", split_axis=0, concat_axis=0, tiled=True)
    parts = spread_sum(parts)
    parts = lax.all_to_all(parts, "dp", split_axis=0, concat_axis=0, tiled=True)
    proj, conv, tail = widen(parts.reshape(2 * chans, width + TAIL), chans, width)
    at = 9 * GS - (TAIL - 128)
    return (
        latent[None, None],
        proj[None],
        conv[None],
        tail[None, :, :, at],
        tail[None, :, :, at + 1],
    )


def solution(mesh):
    return jax.shard_map(
        per_device,
        mesh=mesh,
        in_specs=(
            P("dp", None, "chan"),
            P("segment", "dp", "chan", None),
            P("segment", "dp", "chan", None),
            P("segment", "dp", "chan", None),
            P("segment", "dp", "chan", None),
            P("segment", None, "chan", None),
            P("segment", None, "chan", None),
            P("segment", None, "chan"),
            P("segment", None, "chan"),
        ),
        out_specs=(
            P("segment", "dp", None, "chan"),
            P("segment", None, "chan", None),
            P("segment", None, "chan", None),
            P("segment", None, "chan"),
            P("segment", None, "chan"),
        ),
        check_vma=False,
    )
```

time: 472 us -> 256 us (0.54)
  matrix products: 66 us -> 0 us
  local copies, waits for them, and re-layouts: 56 us -> 6.58 us
  starting transfers between devices: 52.4 us -> 18.3 us
  other arithmetic: 25.2 us -> 0.3 us
  waiting for transfers between devices: 77.7 us -> 52.9 us
  Pallas kernels: 0 us -> 19.3 us
  blocking collectives: 175 us -> 157 us
  between operations: 14.1 us -> 0.82 us
    psum x1 -> x0, waiting for transfers between devices: 67.2 us -> none  [per_device(): lax.psum((final[2], final[3], final[4], final[5]), 'dp')]
    dot_general x160 -> x0, matrix products: 66 us -> none  [the longest x72 36.9 us: conv_backward(): jnp.einsum('gop,gjp->goj', grad_pre, source, preferred_element_type=jnp.f...]
    all_to_all x8 -> x3, waiting for transfers between devices: 4.02 us -> 52.9 us  [the longest x2 46 us: per_device(): parts = lax.all_to_all(parts, 'dp', split_axis=0, concat_axis=0, tiled=True)]
    psum x1 -> x0, blocking collectives: 23.7 us -> none  [per_device(): lax.psum((final[2], final[3], final[4], final[5]), 'dp')]
    pallas_call x0 -> x13, Pallas kernels: none -> 19.3 us  [the longest x8 14.7 us: block(): pl.pallas_call(functools.partial(block_kernel, first), out_shape=shapes,...]
    all_to_all x8 -> x3, starting transfers between devices: 36.9 us -> 18.3 us  [the longest x2 13.3 us: per_device(): parts = lax.all_to_all(parts, 'dp', split_axis=0, concat_axis=0, tiled=True)]
    ppermute x4 -> x0, starting transfers between devices: 15.5 us -> none  [passed_along(): return lax.ppermute(block, axis, route)]
    slice x20 -> x4, local copies, waits for them, and re-layouts: 13.7 us -> 0.82 us  [the longest x1 0.8 us: per_device(): tail[None, :, :, at + 1]]
  transfers between devices with their start and end apart: 13 -> 3, of which waited for: 9 -> 3; matrix products, arithmetic and copies ran while one was open for 13% -> 1% of each run, Pallas kernels for 0% -> 0%
where the time goes in v1:
time: 256 us; the launch traced here: 255 us
  blocking collectives  157 us (61%)
  waiting for transfers between devices  52.9 us (21%)
  Pallas kernels  19.3 us (8%)
  starting transfers between devices  18.3 us (7%)
  local copies, waits for them, and re-layouts  6.58 us (3%)
    all_gather x4, blocking collectives, per_device(): g = lax.all_gather(out, 'chan', axis=0, tiled=True)  69.4 us
    all_gather x3, blocking collectives, per_device(): g = lax.all_gather(both[chans:], 'chan', axis=0, tiled=True)  51.4 us
    all_to_all x2, waiting for transfers between devices, per_device(): parts = lax.all_to_all(parts, 'dp', split_axis=0, concat_axis=0, tiled=True)  46 us
    all_gather x1, blocking collectives, per_device(): g = lax.all_gather(grad_top[0], 'chan', axis=1, tiled=True)  19.7 us
    all_gather x3, blocking collectives, per_device(): lax.all_gather(out, 'segment', axis=0, tiled=True, axis_index_groups=groups)  16 us
    pallas_call x8, Pallas kernels, block(): pl.pallas_call(functools.partial(block_kernel, first), out_shape=shapes,...  14.7 us
    all_to_all x2, starting transfers between devices, per_device(): parts = lax.all_to_all(parts, 'dp', split_axis=0, concat_axis=0, tiled=True)  13.3 us
    all_to_all x1, waiting for transfers between devices, per_device(): lax.all_to_all(saved[0][0], 'chan', split_axis=1, concat_axis=0, tiled=True)  6.88 us
  transfers between devices with their start and end apart: 3, of which 3 were waited for; matrix products, arithmetic and copies ran while one was open for 1% of the time, Pallas kernels for 0%

profile of v1, /device:TPU:6, one launch (start us, length us, event | category | flops | bytes accessed | tf_op | source)
XLA Modules:
  0.0 254.8 jit_solution(16539120182392329626)
XLA Ops:
  0.6 0.0 copy-start.4
  0.7 0.1 pad_add_fusion.flags_ref
  0.7 0.1 pad_add_fusion.1.flags_ref
  0.8 0.1 pad_add_fusion.2.flags_ref
  0.9 0.1 pad_add_fusion.3.flags_ref
  1.0 0.8 slice_bitcast_fusion.5
  1.7 0.8 slice_bitcast_fusion.4
  2.5 0.1 copy.61.bias_ref
  2.6 0.1 copy.60.gain_ref
  2.7 0.1 copy.59.bias_ref
  2.8 0.1 copy.58.gain_ref
  2.9 1.0 slice_bitcast_fusion.2
  3.8 1.1 slice_bitcast_fusion
  4.9 0.0 copy-done.4
  5.0 0.0 copy-start
  5.0 19.7 %all-gather = bf16[1,1536,256]{1,2,0:T(8,128)(2,1)S(1)} all-gather(bf16[1,1536,16]{1,2,0:T(8,128)(2,1)S(1)} %copy-done.4), channel_id=2, replica_groups=mesh['segment'=4,'chan'=16,'dp'=8] {'chan'}, dimensions={2}, use_global_device_ids=true | all-gather | bytes 835584 | tf_op jit(solution)/shard_map/all_gather | solution.py:287
  24.7 0.3 copy.57
  25.0 0.0 copy-done
  25.0 0.0 copy-start.1
  25.0 0.3 norm_forward.2
  25.3 1.5 block_backward.8
  26.8 17.1 %all_gather.34.g_ref = bf16[1536,256]{1,0:T(8,128)(2,1)S(1)} all-gather(bf16[96,256]{1,0:T(8,128)(2,1)S(1)} %get-tuple-element.56), channel_id=1, replica_groups=mesh['segment'=4,'chan'=16,'dp'=8] {'chan'}, dimensions={0}, use_global_device_ids=true | all-gather | bytes 835584 | tf_op jit(solution)/shard_map/all_gather | solution.py:302
  43.9 0.0 copy-done.1
  43.9 0.3 norm_forward.3
  44.2 1.5 block_backward.9
  45.8 4.8 %all_gather.35 = bf16[192,256]{1,0:T(8,128)(2,1)S(1)} all-gather(bf16[96,256]{1,0:T(8,128)(2,1)S(1)} %get-tuple-element.59), channel_id=1, replica_groups={{0,128},{256,384},{1,129},{257,385},{2,130},{258,386},{3,131},{259,387}..., dimensions={0}, use_global_device_ids=true | all-gather | bytes 147456 | tf_op jit(solution)/shard_map/all_gather | solution.py:293
  50.5 17.5 %all_gather.36.g_ref = bf16[1536,256]{1,0:T(8,128)(2,1)S(1)} all-gather(bf16[96,256]{1,0:T(8,128)(2,1)S(1)} %slice.56), channel_id=1, replica_groups=mesh['segment'=4,'chan'=16,'dp'=8] {'chan'}, dimensions={0}, use_global_device_ids=true | all-gather | bytes 835584 | tf_op jit(solution)/shard_map/all_gather | solution.py:296
  68.0 1.8 block_backward.10
  69.9 17.1 %all_gather.37.g_ref = bf16[1536,256]{1,0:T(8,128)(2,1)S(1)} all-gather(bf16[96,256]{1,0:T(8,128)(2,1)S(1)} %get-tuple-element.64), channel_id=1, replica_groups=mesh['segment'=4,'chan'=16,'dp'=8] {'chan'}, dimensions={0}, use_global_device_ids=true | all-gather | bytes 835584 | tf_op jit(solution)/shard_map/all_gather | solution.py:302
  87.0 1.8 block_backward.11
  88.8 6.5 %all_gather.38 = bf16[192,256]{1,0:T(8,128)(2,1)S(1)} all-gather(bf16[96,256]{1,0:T(8,128)(2,1)S(1)} %get-tuple-element.69), channel_id=1, replica_groups={{0,384},{128,256},{1,385},{129,257},{2,386},{130,258},{3,387},{131,259}..., dimensions={0}, use_global_device_ids=true | all-gather | bytes 147456 | tf_op jit(solution)/shard_map/all_gather | solution.py:293
  95.3 16.9 %all_gather.39.g_ref = bf16[1536,256]{1,0:T(8,128)(2,1)S(1)} all-gather(bf16[96,256]{1,0:T(8,128)(2,1)S(1)} %slice.57), channel_id=1, replica_groups=mesh['segment'=4,'chan'=16,'dp'=8] {'chan'}, dimensions={0}, use_global_device_ids=true | all-gather | bytes 835584 | tf_op jit(solution)/shard_map/all_gather | solution.py:296
  112.3 1.8 block_backward.12
  114.1 17.6 %all_gather.40.g_ref = bf16[1536,256]{1,0:T(8,128)(2,1)S(1)} all-gather(bf16[96,256]{1,0:T(8,128)(2,1)S(1)} %get-tuple-element.74), channel_id=1, replica_groups=mesh['segment'=4,'chan'=16,'dp'=8] {'chan'}, dimensions={0}, use_global_device_ids=true | all-gather | bytes 835584 | tf_op jit(solution)/shard_map/all_gather | solution.py:302
  131.7 1.8 block_backward.13
  133.6 4.8 %all_gather.41 = bf16[192,256]{1,0:T(8,128)(2,1)S(1)} all-gather(bf16[96,256]{1,0:T(8,128)(2,1)S(1)} %get-tuple-element.79), channel_id=1, replica_groups={{0,128},{256,384},{1,129},{257,385},{2,130},{258,386},{3,131},{259,387}..., dimensions={0}, use_global_device_ids=true | all-gather | bytes 147456 | tf_op jit(solution)/shard_map/all_gather | solution.py:293
  138.3 16.9 %all_gather.42.g_ref = bf16[1536,256]{1,0:T(8,128)(2,1)S(1)} all-gather(bf16[96,256]{1,0:T(8,128)(2,1)S(1)} %slice.58), channel_id=1, replica_groups=mesh['segment'=4,'chan'=16,'dp'=8] {'chan'}, dimensions={0}, use_global_device_ids=true | all-gather | bytes 835584 | tf_op jit(solution)/shard_map/all_gather | solution.py:296
  155.3 1.8 block_backward.14
  157.1 17.6 %all_gather.43.g_ref = bf16[1536,256]{1,0:T(8,128)(2,1)S(1)} all-gather(bf16[96,256]{1,0:T(8,128)(2,1)S(1)} %get-tuple-element.84), channel_id=1, replica_groups=mesh['segment'=4,'chan'=16,'dp'=8] {'chan'}, dimensions={0}, use_global_device_ids=true | all-gather | bytes 835584 | tf_op jit(solution)/shard_map/all_gather | solution.py:302
  174.8 0.0 copy-start.2
  174.8 0.0 copy-start.3
  174.8 2.5 block_backward.15
  177.2 0.0 copy-done.2
  177.2 0.0 copy-done.3
  177.3 1.8 weight_grads.1
  179.0 9.8 %all-to-all-start.1 = ((bf16[8,24,2048]{2,1,0:T(8,128)(2,1)}), bf16[8,24,2048]{2,1,0:T(8,128)(2,1)S(1)}, u32[]{:S(2)}, u32[]{:S(2)}) async-start(bf16[8,24,2048]{2,1,0:T(8,128)(2,1)} %bitcast.20), calls=%async_computation.1 | async-start | bytes 1572864 | tf_op jit(solution)/shard_map/all_to_all | solution.py:314
  188.8 0.7 copy.62
  189.6 22.9 %all-to-all-done.1.in_ref = bf16[8,24,2048]{2,1,0:T(8,128)(2,1)S(1)} async-done(((bf16[8,24,2048]{2,1,0:T(8,128)(2,1)}), bf16[8,24,2048]{2,1,0:T(8,128)(2,1)S(1)}, u32[]{:S(2)}, u32[]{:S(2)}) %all-to-all-start.1) | async-done | bytes 786464 | tf_op jit(solution)/shard_map/all_to_all | solution.py:314
  212.5 5.0 %all-to-all-start = ((bf16[96,16,16]{0,2,1:T(8,128)(2,1)}), bf16[96,16,16]{0,2,1:T(8,128)(2,1)S(1)}, u32[]{:S(2)}, u32[]{:S(2)}) async-start(bf16[96,16,16]{0,2,1:T(8,128)(2,1)} %bitcast.16), calls=%async_computation | async-start | bytes 131072 | tf_op jit(solution)/shard_map/all_to_all | solution.py:304
  217.5 1.0 sum_microbatches.1
  218.5 6.9 %all-to-all-done = bf16[96,16,16]{0,2,1:T(8,128)(2,1)S(1)} async-done(((bf16[96,16,16]{0,2,1:T(8,128)(2,1)}), bf16[96,16,16]{0,2,1:T(8,128)(2,1)S(1)}, u32[]{:S(2)}, u32[]{:S(2)}) %all-to-all-start) | async-done | bytes 49184 | tf_op jit(solution)/shard_map/all_to_all | solution.py:304
  225.3 3.5 %all-to-all-start.2 = ((bf16[8,24,2048]{2,1,0:T(8,128)(2,1)}), bf16[8,24,2048]{2,1,0:T(8,128)(2,1)S(1)}, u32[]{:S(2)}, u32[]{:S(2)}) async-start(bf16[8,24,2048]{2,1,0:T(8,128)(2,1)} %sum_microbatches.1), calls=%async_computation.2 | async-start | bytes 1572864 | tf_op jit(solution)/shard_map/all_to_all | solution.py:316
  228.9 0.7 broadcast_in_dim.9
  229.7 23.1 %all-to-all-done.2 = bf16[8,24,2048]{2,1,0:T(8,128)(2,1)S(1)} async-done(((bf16[8,24,2048]{2,1,0:T(8,128)(2,1)}), bf16[8,24,2048]{2,1,0:T(8,128)(2,1)S(1)}, u32[]{:S(2)}, u32[]{:S(2)}) %all-to-all-start.2) | async-done | bytes 786464 | tf_op jit(solution)/shard_map/all_to_all | solution.py:316
  252.8 1.2 widen.1
  254.0 0.8 slice_reduce_fusion
  (4 shorter events, 0.0 us)
Async XLA Ops:
  0.6 4.3 %copy-start.4 = (bf16[1,1536,16]{1,2,0:T(8,128)(2,1)S(1)}, bf16[1,1536,16]{1,2,0:T(8,128)(2,1)}, u32[]{:S(2)}) copy-start(bf16[1,1536,16]{1,2,0:T(8,128)(2,1)} %param.9) | copy-start | bytes 147460
  5.0 20.0 %copy-start = (bf16[1,1,96,256]{3,2,1,0:T(8,128)(2,1)S(1)}, bf16[1,1,96,256]{3,2,1,0:T(8,128)(2,1)}, u32[]{:S(2)}) copy-start(bf16[1,1,96,256]{3,2,1,0:T(8,128)(2,1)} %param.13) | copy-start | bytes 147460
  25.0 18.9 %copy-start.1 = (bf16[1,1,96,256]{3,2,1,0:T(8,128)(2,1)S(1)}, bf16[1,1,96,256]{3,2,1,0:T(8,128)(2,1)}, u32[]{:S(2)}) copy-start(bf16[1,1,96,256]{3,2,1,0:T(8,128)(2,1)} %param.11) | copy-start | bytes 147460
  174.8 2.5 copy-start.2
  174.8 2.5 copy-start.3
  179.0 33.5 %all-to-all-start.1 = ((bf16[8,24,2048]{2,1,0:T(8,128)(2,1)}), bf16[8,24,2048]{2,1,0:T(8,128)(2,1)S(1)}, u32[]{:S(2)}, u32[]{:S(2)}) async-start(bf16[8,24,2048]{2,1,0:T(8,128)(2,1)} %bitcast.20), calls=%async_computation.1 | async-start | bytes 1572864 | tf_op jit(solution)/shard_map/all_to_all | solution.py:314
  212.5 12.8 %all-to-all-start = ((bf16[96,16,16]{0,2,1:T(8,128)(2,1)}), bf16[96,16,16]{0,2,1:T(8,128)(2,1)S(1)}, u32[]{:S(2)}, u32[]{:S(2)}) async-start(bf16[96,16,16]{0,2,1:T(8,128)(2,1)} %bitcast.16), calls=%async_computation | async-start | bytes 131072 | tf_op jit(solution)/shard_map/all_to_all | solution.py:304
  225.3 27.4 %all-to-all-start.2 = ((bf16[8,24,2048]{2,1,0:T(8,128)(2,1)}), bf16[8,24,2048]{2,1,0:T(8,128)(2,1)S(1)}, u32[]{:S(2)}, u32[]{:S(2)}) async-start(bf16[8,24,2048]{2,1,0:T(8,128)(2,1)} %sum_microbatches.1), calls=%async_computation.2 | async-start | bytes 1572864 | tf_op jit(solution)/shard_map/all_to_all | solution.py:316

commit v2 on v1

v2 whole, which is shorter than its diff:
```python
import functools

import jax
import jax.numpy as jnp
from jax import lax
from jax.experimental import pallas as pl
from jax.experimental.pallas import tpu as pltpu
from jax.sharding import PartitionSpec as P

GS = 48
WW = 64
NORM_EPS = 1e-05
TAIL = 512
F32 = jnp.float32
BF16 = jnp.bfloat16
VMEM = pl.BlockSpec(memory_space=pltpu.VMEM)
SMEM = pl.BlockSpec(memory_space=pltpu.SMEM)
ANY = pl.BlockSpec(memory_space=pl.ANY)
NT = (((1,), (1,)), ((), ()))
TN = (((0,), (0,)), ((), ()))
PARAMS = pltpu.CompilerParams(vmem_limit_bytes=32 * 1024 * 1024)


def shape_of(shape, dtype):
    return jax.ShapeDtypeStruct(shape, dtype)


def total(block):
    return jnp.sum(jnp.sum(block, axis=1, keepdims=True), axis=0, keepdims=True)


def norm_group(h, gain, bias):
    scale = 1.0 / (h.shape[0] * h.shape[1])
    pre = h.astype(F32)
    pre = pre - total(pre) * scale
    inv_std = lax.rsqrt(total(pre * pre) * scale + NORM_EPS)
    xhat = pre * inv_std
    n = xhat * gain + bias
    sig = jax.nn.sigmoid(n)
    slope = sig * (1.0 + n * (1.0 - sig))
    return xhat, n, sig, slope, inv_std


def column(line):
    count = line.shape[1]
    down = lax.broadcasted_iota(jnp.int32, (count, count), 0)
    across = lax.broadcasted_iota(jnp.int32, (count, count), 1)
    return jnp.sum(jnp.where(down == across, line, 0.0), axis=1, keepdims=True)


def prepare_kernel(
    w_ref, wc_ref, h1_ref, h2_ref, gain_ref, bias_ref,
    pack_ref, xhat_ref, slope_ref, rate_ref, act_ref,
):
    chans, width = w_ref.shape[2:]
    taps = wc_ref.shape[3]
    lane = lax.broadcasted_iota(jnp.int32, (chans, TAIL - 384), 1)
    for b, h_ref in enumerate((h1_ref, h2_ref)):
        pack_ref[b, :, :width] = w_ref[0, b]
        pack_ref[b, :, width : width + 384] = wc_ref[0, b, :, :384]
        last = wc_ref[0, b, :, 384:].astype(F32)
        last = jnp.concatenate(
            [last, jnp.zeros((chans, TAIL - taps), F32)], axis=1
        )
        gain = column(gain_ref[0, b : b + 1, :])
        bias = column(bias_ref[0, b : b + 1, :])
        at = taps - 384
        for whole in (gain, bias):
            rest = whole
            for _ in range(3):
                piece = rest.astype(BF16).astype(F32)
                rest = rest - piece
                last = jnp.where(lane == at, piece, last)
                at += 1
        pack_ref[b, :, width + 384 : width + TAIL] = last.astype(BF16)
        pack_ref[b, :, width + TAIL :] = h_ref[0, 0]
        for q in range(0, chans, GS):
            rows = slice(q, q + GS)
            xhat, n, sig, slope, inv_std = norm_group(
                h_ref[0, 0, rows, :], gain[rows], bias[rows]
            )
            xhat_ref[b, rows, :] = xhat
            slope_ref[b, rows, :] = slope
            rate_ref[b, rows, :] = slope * (gain[rows] * inv_std)
            act_ref[b, rows, :] = (n * sig).astype(BF16)


def prepare(proj_weight, conv_weight, conv_one, conv_two, gain, bias):
    chans, width = proj_weight.shape[2:]
    positions = conv_one.shape[3]
    full = shape_of((2, chans, positions), F32)
    return pl.pallas_call(
        prepare_kernel,
        out_shape=(
            shape_of((2, chans, width + TAIL + positions), BF16),
            full,
            full,
            full,
            shape_of((2, chans, positions), BF16),
        ),
        in_specs=[VMEM] * 6,
        out_specs=[VMEM] * 5,
        compiler_params=PARAMS,
        name="prepare",
    )(proj_weight, conv_weight, conv_one, conv_two, gain, bias)


def wide_norm_kernel(taps, tail_ref, h_ref, xhat_ref, rate_ref):
    count, _, chans, _ = tail_ref.shape
    at = taps - 384
    for b in range(2):
        for y in range(count):
            side = tail_ref[y, b, :, 384:].astype(F32)
            gain = side[:, at : at + 1] + side[:, at + 1 : at + 2] + side[:, at + 2 : at + 3]
            bias = side[:, at + 3 : at + 4] + side[:, at + 4 : at + 5] + side[:, at + 5 : at + 6]
            for q in range(0, chans, GS):
                rows = slice(q, q + GS)
                xhat, _, _, slope, inv_std = norm_group(
                    h_ref[y, b, rows, :], gain[rows], bias[rows]
                )
                to = slice(y * chans + q, y * chans + q + GS)
                xhat_ref[b, to, :] = xhat
                rate_ref[b, to, :] = slope * (gain[rows] * inv_std)


def wide_norm(packs, width, positions):
    count, _, chans, _ = packs.shape
    full = shape_of((2, count * chans, positions), F32)
    return pl.pallas_call(
        functools.partial(wide_norm_kernel, 9 * GS),
        out_shape=(full, full),
        grid=(1,),
        in_specs=[
            pl.BlockSpec((count, 2, chans, TAIL), lambda i: (0, 0, 0, width // TAIL)),
            pl.BlockSpec(
                (count, 2, chans, positions),
                lambda i: (0, 0, 0, (width + TAIL) // positions),
            ),
        ],
        out_specs=[VMEM] * 2,
        compiler_params=PARAMS,
        name="wide_norm",
    )(packs, packs)


def shifted(value, step_row, step_col, row, col):
    length = value.shape[1]
    rows = length // WW
    by = step_row * WW + step_col
    if by == 0:
        return value
    moved = pltpu.roll(value, (-by) % length, axis=1)
    inside = None
    if step_row:
        inside = row < rows - 1 if step_row > 0 else row > 0
    if step_col:
        here = col < WW - 1 if step_col > 0 else col > 0
        inside = here if inside is None else inside & here
    return jnp.where(inside, moved, 0.0)


def grid_of(shape):
    lane = lax.broadcasted_iota(jnp.int32, shape, 1)
    return lane // WW, lane % WW


def own_positions(g, chan_at, count):
    down = lax.broadcasted_iota(jnp.int32, (count, g.shape[1]), 0)
    across = lax.broadcasted_iota(jnp.int32, (count, g.shape[1]), 1)
    pick = jnp.where(across == down + chan_at * count, 1.0, 0.0).astype(BF16)
    return lax.dot_general(pick, g, NT, preferred_element_type=F32).astype(BF16)


def block(b, wide, flags, g, ordered, params, state, saved, latent, make_latent):
    xhat, rate = state
    chans, positions = xhat.shape[1:]
    own_rows = params[0].shape[-2]
    whole = g.shape[0]
    slab = positions // (whole // own_rows)
    first = saved is None
    has_latent = latent is not None or make_latent
    scale = 1.0 / (GS * positions)
    per = whole // 2 // own_rows

    def kernel(*refs):
        refs = list(refs)
        take = lambda k: [refs.pop(0) for _ in range(k)]
        flags_ref, g_ref = take(2)
        weights = take(len(params))
        xhat_ref, rate_ref = take(2)
        if not first:
            take(3)
        if latent is not None:
            take(1)
        out_ref, sg_ref, sgh_ref, sga_ref = take(4)
        lat_ref = take(1)[0] if has_latent else None
        ga_buf, gh_buf, g_buf, sem = take(4)
        valid = flags_ref[0] > 0
        late = flags_ref[1] > 0
        chan_at = flags_ref[2]
        core = chan_at & 1
        if ordered:
            src = g_ref
        else:
            for c in range(2):
                for y in range(per):
                    to = (2 * y + c) * own_rows
                    at = (c * per + y) * own_rows
                    g_buf[to : to + own_rows, :] = g_ref[at : at + own_rows, :]
            src = g_buf
        keep = pltpu.make_async_copy(src, sg_ref, sem)

        @pl.when(valid)
        def _():
            keep.start()

        if wide:
            (pack_ref,) = weights
            width = whole
            for y in range(per):
                ga_buf[y * own_rows : (y + 1) * own_rows, :] = jnp.dot(
                    pack_ref[y, b, :, :width], src[...], preferred_element_type=F32
                )
        else:
            w_ref, wc_ref = weights
            ga_buf[...] = jnp.dot(w_ref[0, b], src[...], preferred_element_type=F32)
        row, col = grid_of((GS, positions))
        for at in range(0, chans, GS):
            y, q = divmod(at, own_rows)
            rows = slice(at, at + GS)
            if wide:
                taps_w = pack_ref[y, b, q : q + GS, width : width + 9 * GS]
                mine_at = (2 * y + core) * own_rows + q
            else:
                taps_w = wc_ref[0, b, q : q + GS, :]
                mine_at = chan_at * own_rows + q
            xhat_q = xhat_ref[b, rows, :]
            rw = ga_buf[rows, :] * rate_ref[b, rows, :]
            gh = rw - total(rw) * scale - xhat_q * (total(rw * xhat_q) * scale)
            gh = gh.astype(BF16)
            gh_buf[rows, :] = gh
            spread = lax.dot_general(taps_w, gh, TN, preferred_element_type=F32)
            branch = None
            for step_col in (-1, 0, 1):
                part = None
                for step_row in (-1, 0, 1):
                    tap = 3 * (step_row + 1) + step_col + 1
                    term = shifted(spread[tap * GS : (tap + 1) * GS, :], -step_row, 0, row, col)
                    part = term if part is None else part + term
                part = shifted(part, 0, -step_col, row, col)
                branch = part if branch is None else branch + part
            mine = src[pl.ds(pl.multiple_of(mine_at, GS), GS), :].astype(F32)
            out_ref[rows, :] = (mine + branch.astype(BF16).astype(F32)).astype(BF16)

        @pl.when(valid)
        def _():
            mine = (chan_at >> 1) * own_rows if wide else 0
            mine = pl.multiple_of(mine, own_rows) if wide else 0
            sgh_ref[...] = gh_buf[pl.ds(mine, own_rows), :]
            sga_ref[...] = ga_buf[pl.ds(mine, own_rows), :]
            keep.wait()

        if has_latent:

            @pl.when(late)
            def _():
                lat_ref[...] = own_positions(src[...], chan_at, slab)

    shapes = [
        shape_of((chans, positions), BF16),
        shape_of((whole, positions), BF16),
        shape_of((own_rows, positions), BF16),
        shape_of((own_rows, positions), F32),
    ]
    out_specs = [VMEM, ANY, VMEM, VMEM]
    operands = [flags, g, *params, xhat, rate]
    in_specs = [SMEM] + [VMEM] * (len(operands) - 1)
    aliases = {}
    if not first:
        for i, kept in enumerate(saved):
            aliases[len(operands)] = 1 + i
            operands.append(kept)
            in_specs.append(out_specs[1 + i])
    if has_latent:
        shapes.append(shape_of((slab, whole), BF16))
        out_specs.append(VMEM)
        if latent is not None:
            aliases[len(operands)] = 4
            operands.append(latent)
            in_specs.append(VMEM)
    result = pl.pallas_call(
        kernel,
        out_shape=shapes,
        in_specs=in_specs,
        out_specs=out_specs,
        scratch_shapes=[
            pltpu.VMEM((chans, positions), F32),
            pltpu.VMEM((chans, positions), BF16),
            pltpu.VMEM((8, 128) if ordered else (whole, positions), BF16),
            pltpu.SemaphoreType.DMA,
        ],
        input_output_aliases=aliases,
        compiler_params=PARAMS,
        name="wide_block" if wide else "own_block",
    )(*operands)
    return result[0], tuple(result[1:4]), result[4] if has_latent else latent


def weights_kernel(*refs):
    flags_ref, last_ref, lat_in_ref = refs[:3]
    act_ref, xhat_ref, slope_ref = refs[3:6]
    x_refs = refs[6:8]
    saved_refs = (refs[8:11], refs[11:14])
    out_ref, lat_ref, stack, g_buf = refs[14:]
    chans, positions = x_refs[0].shape[2:]
    width = out_ref.shape[1] - TAIL
    row, col = grid_of((GS, positions))
    lane = lax.broadcasted_iota(jnp.int32, (GS, TAIL), 1)
    stack[9 * GS :, :] = jnp.zeros((TAIL - 9 * GS, positions), BF16)
    for b in range(2):
        g_ref, gh_ref, ga_ref = saved_refs[b]
        x_ref = x_refs[b]
        at = b * chans
        out_ref[at : at + chans, :width] = lax.dot_general(
            act_ref[b], g_ref[...], NT, preferred_element_type=F32
        ).astype(BF16)
        for q in range(0, chans, GS):
            rows = slice(q, q + GS)
            x = x_ref[0, 0, rows, :].astype(F32)
            for step_row in (-1, 0, 1):
                for step_col in (-1, 0, 1):
                    tap = 3 * (step_row + 1) + step_col + 1
                    stack[tap * GS : (tap + 1) * GS, :] = shifted(
                        x, step_row, step_col, row, col
                    ).astype(BF16)
            taps = lax.dot_general(gh_ref[rows, :], stack[...], NT, preferred_element_type=F32)
            gn = ga_ref[rows, :] * slope_ref[b, rows, :]
            by_gain = jnp.sum(gn * xhat_ref[b, rows, :], axis=1, keepdims=True)
            by_bias = jnp.sum(gn, axis=1, keepdims=True)
            taps = jnp.where(lane == 9 * GS, by_gain, taps)
            taps = jnp.where(lane == 9 * GS + 1, by_bias, taps)
            out_ref[at + q : at + q + GS, width:] = taps.astype(BF16)
    lat_ref[...] = lat_in_ref[...]

    @pl.when(flags_ref[0] > 0)
    def _():
        per = last_ref.shape[0] // 2 // chans
        for c in range(2):
            for y in range(per):
                to = (2 * y + c) * chans
                src = (c * per + y) * chans
                g_buf[to : to + chans, :] = last_ref[src : src + chans, :]
        lat_ref[...] = own_positions(g_buf[...], flags_ref[2], lat_ref.shape[0])


def weight_grads(flags, last, latent, act, xhat, slope, inputs, saved):
    chans, positions = act.shape[1:]
    width = last.shape[0]
    return pl.pallas_call(
        weights_kernel,
        out_shape=(
            shape_of((2 * chans, width + TAIL), BF16),
            shape_of(latent.shape, BF16),
        ),
        in_specs=[SMEM] + [VMEM] * 13,
        out_specs=[VMEM] * 2,
        scratch_shapes=[
            pltpu.VMEM((TAIL, positions), BF16),
            pltpu.VMEM((width, positions), BF16),
        ],
        compiler_params=PARAMS,
        name="weight_grads",
    )(flags, last, latent, act, xhat, slope, *inputs, *saved[0], *saved[1])


def reduce_kernel(in_ref, out_ref):
    count = in_ref.shape[0]
    acc = in_ref[0].astype(F32)
    for m in range(1, count):
        acc = acc + in_ref[m].astype(F32)
    done = acc.astype(BF16)
    for m in range(count):
        out_ref[m] = done


def spread_sum(parts):
    return pl.pallas_call(
        reduce_kernel,
        out_shape=shape_of(parts.shape, BF16),
        in_specs=[VMEM],
        out_specs=VMEM,
        compiler_params=PARAMS,
        name="sum_microbatches",
    )(parts)


def widen_kernel(in_ref, proj_ref, conv_ref, gain_ref, bias_ref):
    chans, width = proj_ref.shape[2:]
    down = lax.broadcasted_iota(jnp.int32, (chans, chans), 0)
    across = lax.broadcasted_iota(jnp.int32, (chans, chans), 1)
    at = 9 * GS - (TAIL - 128)
    for b in range(2):
        rows = slice(b * chans, (b + 1) * chans)
        proj_ref[0, b] = in_ref[rows, :width].astype(F32)
        conv_ref[0, b] = in_ref[rows, width : width + 9 * GS].astype(F32)
        tail = in_ref[rows, width + TAIL - 128 :].astype(F32)
        for i, ref in enumerate((gain_ref, bias_ref)):
            lined = jnp.where(down == across, tail[:, at + i : at + i + 1], 0.0)
            ref[0, b : b + 1, :] = jnp.sum(lined, axis=0, keepdims=True)


def widen(sums, chans, width):
    return pl.pallas_call(
        widen_kernel,
        out_shape=(
            shape_of((1, 2, chans, width), F32),
            shape_of((1, 2, chans, 9 * GS), F32),
            shape_of((1, 2, chans), F32),
            shape_of((1, 2, chans), F32),
        ),
        in_specs=[VMEM],
        out_specs=[VMEM] * 4,
        compiler_params=PARAMS,
        name="widen",
    )(sums)


def gather(block_, axis, groups=None):
    return lax.all_gather(block_, axis, axis=0, tiled=True, axis_index_groups=groups)


def per_device(
    grad_top,
    inputs_one,
    conv_one,
    inputs_two,
    conv_two,
    proj_weight,
    conv_weight,
    norm_gain,
    norm_bias,
):
    segments = lax.axis_size("segment")
    segment_at = lax.axis_index("segment")
    chan_at = lax.axis_index("chan")
    members = lax.axis_size("dp")
    shards = lax.axis_size("chan")
    chans, positions = conv_one.shape[2:]
    width = proj_weight.shape[3]
    cores = [[2 * y, 2 * y + 1] for y in range(shards // 2)]
    columns = [[2 * y + c for y in range(shards // 2)] for c in range(2)]

    pack, xhat, slope, rate, act = prepare(
        proj_weight, conv_weight, conv_one, conv_two, norm_gain, norm_bias
    )
    packs = gather(pack, "chan", columns).reshape((shards // 2,) + pack.shape)
    own = (proj_weight, conv_weight)
    wide_state = None
    saved = [None, None]
    latent = None
    out = None
    for tick in range(segments):
        flags = jnp.stack(
            [
                (segment_at == segments - 1 - tick).astype(jnp.int32),
                (segment_at == segments - tick).astype(jnp.int32),
                chan_at.astype(jnp.int32),
            ]
        )
        if tick == 0:
            g = lax.all_gather(grad_top[0], "chan", axis=1, tiled=True)
        else:
            lower = segments - 1 - tick
            rest = [s for s in range(segments) if s not in (lower, lower + 1)]
            groups = sorted(
                [[lower, lower + 1]] + [rest[i : i + 2] for i in range(0, len(rest), 2)]
            )
            half = out.shape[0]
            moved = gather(out, "segment", groups)[half:]
            g = gather(moved, "chan", None if half == chans else cores)
        for b in (1, 0):
            ordered = tick == 0 or out.shape[0] == chans
            wide = tick > 1 or (tick == 1 and b == 0)
            if wide and wide_state is None:
                packs, g = lax.optimization_barrier((packs, g))
                wide_state = wide_norm(packs, width, positions)
            out, saved[b], kept = block(
                b,
                wide,
                flags,
                g,
                ordered,
                (packs,) if wide else own,
                wide_state if wide else (xhat, rate),
                saved[b],
                latent if b == 1 else None,
                b == 1 and tick == 1,
            )
            latent = kept if b == 1 else latent
            if b == 1 or tick == segments - 1:
                g = gather(out, "chan", None if out.shape[0] == chans else cores)

    grads, latent = weight_grads(
        flags, g, latent, act, xhat, slope, (inputs_one, inputs_two), saved
    )
    parts = grads.reshape(members, 2 * chans // members, width + TAIL)
    parts = lax.all_to_all(parts, "dp", split_axis=0, concat_axis=0, tiled=True)
    parts = spread_sum(parts)
    parts = lax.all_to_all(parts, "dp", split_axis=0, concat_axis=0, tiled=True)
    proj, conv, by_gain, by_bias = widen(parts.reshape(2 * chans, width + TAIL), chans, width)
    return latent.T[None, None], proj, conv, by_gain, by_bias


def solution(mesh):
    return jax.shard_map(
        per_device,
        mesh=mesh,
        in_specs=(
            P("dp", None, "chan"),
            P("segment", "dp", "chan", None),
            P("segment", "dp", "chan", None),
            P("segment", "dp", "chan", None),
            P("segment", "dp", "chan", None),
            P("segment", None, "chan", None),
            P("segment", None, "chan", None),
            P("segment", None, "chan"),
            P("segment", None, "chan"),
        ),
        out_specs=(
            P("segment", "dp", None, "chan"),
            P("segment", None, "chan", None),
            P("segment", None, "chan", None),
            P("segment", None, "chan"),
            P("segment", None, "chan"),
        ),
        check_vma=False,
    )
```

time: 256 us -> 261 us (1.020)
  waiting for transfers between devices: 52.9 us -> 6.49 us
  Pallas kernels: 19.3 us -> 50.2 us
  blocking collectives: 157 us -> 181 us
  starting transfers between devices: 18.3 us -> 0.04 us
  between operations: 0.82 us -> 14.2 us
    all_to_all x0 -> x2, blocking collectives: none -> 55.3 us  [per_device(): parts = lax.all_to_all(parts, 'dp', split_axis=0, concat_axis=0, tiled=True)]
    all_to_all x3 -> x0, waiting for transfers between devices: 52.9 us -> none  [the longest x2 46 us: per_device(): parts = lax.all_to_all(parts, 'dp', split_axis=0, concat_axis=0, tiled=True)]
    pallas_call x13, Pallas kernels: 19.3 us -> 50.2 us  [the longest x8 41.2 us: block(): pl.pallas_call(kernel, out_shape=shapes, in_specs=in_specs, out_specs=out...]
    all_gather x10 -> x11, blocking collectives: 137 us -> 106 us  [gather(): lax.all_gather(block_, axis, axis=0, tiled=True, axis_index_groups=groups)]
    all_to_all x3 -> x0, starting transfers between devices: 18.3 us -> none  [the longest x2 13.3 us: per_device(): parts = lax.all_to_all(parts, 'dp', split_axis=0, concat_axis=0, tiled=True)]
    unnamed x10 -> x26, local copies, waits for them, and re-layouts: 0.02 us -> 7.97 us
    all_gather x0 -> x1, waiting for transfers between devices: none -> 6.47 us  [gather(): lax.all_gather(block_, axis, axis=0, tiled=True, axis_index_groups=groups)]
    squeeze x8 -> x0, local copies, waits for them, and re-layouts: 3.97 us -> none  [the longest x1 1.09 us: per_device(): w = (proj_weight[0, 0], proj_weight[0, 1])]
  transfers between devices with their start and end apart: 3 -> 1, of which waited for: 3 -> 1; matrix products, arithmetic and copies ran while one was open for 1% -> 0% of each run, Pallas kernels for 0% -> 2%
where the time goes in v2:
time: 261 us
  blocking collectives  181 us (69%)
  Pallas kernels  50.2 us (19%)
  between operations  14.2 us (5%)
  local copies, waits for them, and re-layouts  8.29 us (3%)
  waiting for transfers between devices  6.49 us (2%)
    all_gather x11, blocking collectives, gather(): lax.all_gather(block_, axis, axis=0, tiled=True, axis_index_groups=groups)  106 us
    all_to_all x2, blocking collectives, per_device(): parts = lax.all_to_all(parts, 'dp', split_axis=0, concat_axis=0, tiled=True)  55.3 us
    pallas_call x8, Pallas kernels, block(): pl.pallas_call(kernel, out_shape=shapes, in_specs=in_specs, out_specs=out...  41.2 us
    all_gather x1, blocking collectives, per_device(): g = lax.all_gather(grad_top[0], 'chan', axis=1, tiled=True)  19.9 us
    unnamed x26, local copies, waits for them, and re-layouts  7.97 us
    all_gather x1, waiting for transfers between devices, gather(): lax.all_gather(block_, axis, axis=0, tiled=True, axis_index_groups=groups)  6.47 us
  transfers between devices with their start and end apart: 1, of which 1 were waited for; matrix products, arithmetic and copies ran while one was open for 0% of the time, Pallas kernels for 2%

profile of v2, /device:TPU:6, one launch (start us, length us, event | category | flops | bytes accessed | tf_op | source)
XLA Modules:
  0.0 260.8 jit_solution(1633515494321890389)
XLA Ops:
  7.2 0.0 all-gather.3.cloned.1.call-start
  7.2 0.0 copy-start.2
  7.2 1.1 copy-done.2
  8.3 0.0 copy-start.4
  8.3 0.9 copy-done.4
  9.2 0.0 copy-start.6
  9.2 0.8 copy-done.6
  10.0 0.0 copy-start.7
  10.0 0.8 copy-done.7
  10.8 0.0 copy-start.10
  10.8 0.7 copy-done.10
  11.5 0.0 copy-start.11
  11.5 0.7 copy-done.11
  12.2 0.0 copy-start.12
  12.2 1.3 prepare.1
  13.4 0.0 copy-start.3
  13.4 0.0 copy-start.5
  13.4 0.0 all-gather.3.cloned.1.call-update
  13.5 0.0 copy-done.12
  13.5 19.9 %all-gather = bf16[1,1536,256]{1,2,0:T(8,128)(2,1)S(1)} all-gather(bf16[1,1536,16]{1,2,0:T(8,128)(2,1)S(1)} %copy-done.12), channel_id=2, replica_groups=mesh['segment'=4,'chan'=16,'dp'=8] {'chan'}, dimensions={2}, use_global_device_ids=true | all-gather | bytes 835584 | tf_op jit(solution)/shard_map/all_gather | solution.py:471
  33.4 0.3 copy.35
  33.6 0.1 add_add_fusion.3.refs_0_
  33.7 0.0 copy-done.3
  33.7 0.0 copy-done.5
  33.7 1.5 own_block.3
  35.3 21.7 %all_gather.41.refs_1_ = bf16[1536,256]{1,0:T(8,128)(2,1)S(1)} all-gather(bf16[96,256]{1,0:T(8,128)(2,1)S(1)} %get-tuple-element.58), channel_id=1, replica_groups=mesh['segment'=4,'chan'=16,'dp'=8] {'chan'}, dimensions={0}, use_global_device_ids=true | all-gather | bytes 835584 | tf_op jit(solution)/shard_map/all_gather | solution.py:429
  56.9 1.5 own_block.4
  58.5 4.8 %all_gather.42 = bf16[192,256]{1,0:T(8,128)(2,1)S(1)} all-gather(bf16[96,256]{1,0:T(8,128)(2,1)S(1)} %get-tuple-element.59), channel_id=1, replica_groups={{0,128},{256,384},{1,129},{257,385},{2,130},{258,386},{3,131},{259,387}..., dimensions={0}, use_global_device_ids=true | all-gather | bytes 147456 | tf_op jit(solution)/shard_map/all_gather | solution.py:429
  63.2 0.1 add_add_fusion.2.refs_0_
  63.3 21.6 %all_gather.43.refs_1_ = bf16[1536,256]{1,0:T(8,128)(2,1)S(1)} all-gather(bf16[96,256]{1,0:T(8,128)(2,1)S(1)} %slice.12), channel_id=1, replica_groups=mesh['segment'=4,'chan'=16,'dp'=8] {'chan'}, dimensions={0}, use_global_device_ids=true | all-gather | bytes 835584 | tf_op jit(solution)/shard_map/all_gather | solution.py:429
  84.9 1.8 own_block.5
  86.7 0.1 add_add_fusion.1.refs_0_
  86.8 0.1 add_add_fusion.refs_0_
  86.9 21.7 %all_gather.44.refs_1_ = bf16[1536,256]{1,0:T(8,128)(2,1)S(1)} all-gather(bf16[96,256]{1,0:T(8,128)(2,1)S(1)} %get-tuple-element.63), channel_id=1, replica_groups=mesh['segment'=4,'chan'=16,'dp'=8] {'chan'}, dimensions={0}, use_global_device_ids=true | all-gather | bytes 835584 | tf_op jit(solution)/shard_map/all_gather | solution.py:429
  108.5 6.5 %all-gather.3.cloned.1.call-done = bf16[16,96,2304]{2,1,0:T(8,128)(2,1)} async-done(((bf16[2,96,2304]{2,1,0:T(8,128)(2,1)}), bf16[16,96,2304]{2,1,0:T(8,128)(2,1)}) %all-gather.3.cloned.1.call-update) | async-done | bytes 7077904 | tf_op jit(solution)/shard_map/all_gather | solution.py:429
  115.0 0.0 copy-start
  115.0 3.0 %copy-done = bf16[16,96,2304]{2,1,0:T(8,128)(2,1)S(1)} copy-done((bf16[16,96,2304]{2,1,0:T(8,128)(2,1)S(1)}, bf16[16,96,2304]{2,1,0:T(8,128)(2,1)}, u32[]{:S(2)}) %copy-start) | copy-done | bytes 7077912
  118.0 0.0 copy-start.1
  118.0 4.4 %wide_norm.1 = (f32[2,768,256]{2,1,0:T(8,128)S(1)}, f32[2,768,256]{2,1,0:T(8,128)S(1)}) custom-call(bf16[8,2,96,2304]{3,2,1,0:T(8,128)(2,1)S(1)} %bitcast.13, bf16[8,2,96,2304]{3,2,1,0:T(8,128)(2,1)S(1)} %bitcast.14), custom_call_target="tpu_custom_call" | custom-call | tf_op jit(solution)/shard_map/wide_norm/pallas_call | solution.py:129
  122.4 0.0 copy-done.1
  122.5 7.2 %wide_block.5 = (bf16[768,256]{1,0:T(8,128)(2,1)S(1)}, bf16[1536,256]{1,0:T(8,128)(2,1)S(1)}, bf16[96,256]{1,0:T(8,128)(2,1)S(1)}, f32[96,256]{1,0:T(8,128)S(1)}) custom-call(s32[3]{0:T(128)S(1)} %add_add_fusion.2.refs_0_, bf16[1536,256]{1,0:T(8,128)(2,1)S(1)} %all_gather.44.refs_1_, ...), custom_call_target="tpu_custom_call", output_to_operand_aliasing={{1}: (5, {}), {2}: (6, {}), {3}: (7, {})} | custom-call | tf_op jit(solution)/shard_map/wide_block/pallas_call | solution.py:291
  129.6 12.7 %all_gather.45 = bf16[1536,256]{1,0:T(8,128)(2,1)S(1)} all-gather(bf16[768,256]{1,0:T(8,128)(2,1)S(1)} %get-tuple-element.71), channel_id=1, replica_groups={{0,384},{128,256},{1,385},{129,257},{2,386},{130,258},{3,387},{131,259}..., dimensions={0}, use_global_device_ids=true | all-gather | bytes 1179648 | tf_op jit(solution)/shard_map/all_gather | solution.py:429
  142.4 2.4 all_gather.46.refs_1_
  144.8 7.4 %wide_block.6 = (bf16[768,256]{1,0:T(8,128)(2,1)S(1)}, bf16[1536,256]{1,0:T(8,128)(2,1)S(1)}, bf16[96,256]{1,0:T(8,128)(2,1)S(1)}, f32[96,256]{1,0:T(8,128)S(1)}, bf16[16,1536]{1,0:T(8,128)(2,1)S(1)}) custom-call(s32[3]{0:T(128)S(1)} %add_add_fusion.1.refs_0_, ...), custom_call_target="tpu_custom_call", output_to_operand_aliasing={{1}: (5, {}), {2}: (6, {}), {3}: (7, {}), {4}: (8, {})} | custom-call | tf_op jit(solution)/shard_map/wide_block/pallas_call | solution.py:291
  152.1 2.4 all_gather.47.refs_1_
  154.5 7.2 %wide_block.7 = (bf16[768,256]{1,0:T(8,128)(2,1)S(1)}, bf16[1536,256]{1,0:T(8,128)(2,1)S(1)}, bf16[96,256]{1,0:T(8,128)(2,1)S(1)}, f32[96,256]{1,0:T(8,128)S(1)}) custom-call(s32[3]{0:T(128)S(1)} %add_add_fusion.1.refs_0_, bf16[1536,256]{1,0:T(8,128)(2,1)S(1)} %all_gather.47.refs_1_, ...), custom_call_target="tpu_custom_call", output_to_operand_aliasing={{1}: (5, {}), {2}: (6, {}), {3}: (7, {})} | custom-call | tf_op jit(solution)/shard_map/wide_block/pallas_call | solution.py:291
  161.7 11.8 %all_gather.48 = bf16[1536,256]{1,0:T(8,128)(2,1)S(1)} all-gather(bf16[768,256]{1,0:T(8,128)(2,1)S(1)} %get-tuple-element.80), channel_id=1, replica_groups={{0,128},{256,384},{1,129},{257,385},{2,130},{258,386},{3,131},{259,387}..., dimensions={0}, use_global_device_ids=true | all-gather | bytes 1179648 | tf_op jit(solution)/shard_map/all_gather | solution.py:429
  173.6 2.4 all_gather.49.refs_1_
  175.9 7.4 %wide_block.8 = (bf16[768,256]{1,0:T(8,128)(2,1)S(1)}, bf16[1536,256]{1,0:T(8,128)(2,1)S(1)}, bf16[96,256]{1,0:T(8,128)(2,1)S(1)}, f32[96,256]{1,0:T(8,128)S(1)}, bf16[16,1536]{1,0:T(8,128)(2,1)S(1)}) custom-call(s32[3]{0:T(128)S(1)} %add_add_fusion.refs_0_, ...), custom_call_target="tpu_custom_call", output_to_operand_aliasing={{1}: (5, {}), {2}: (6, {}), {3}: (7, {}), {4}: (8, {})} | custom-call | tf_op jit(solution)/shard_map/wide_block/pallas_call | solution.py:291
  183.4 2.4 all_gather.50.refs_1_
  185.7 0.0 copy-start.8
  185.7 0.0 copy-start.9
  185.7 7.2 %wide_block.9 = (bf16[768,256]{1,0:T(8,128)(2,1)S(1)}, bf16[1536,256]{1,0:T(8,128)(2,1)S(1)}, bf16[96,256]{1,0:T(8,128)(2,1)S(1)}, f32[96,256]{1,0:T(8,128)S(1)}) custom-call(s32[3]{0:T(128)S(1)} %add_add_fusion.refs_0_, bf16[1536,256]{1,0:T(8,128)(2,1)S(1)} %all_gather.50.refs_1_, ...), custom_call_target="tpu_custom_call", output_to_operand_aliasing={{1}: (5, {}), {2}: (6, {}), {3}: (7, {})} | custom-call | tf_op jit(solution)/shard_map/wide_block/pallas_call | solution.py:291
  192.9 2.4 all_gather.51.refs_1_
  195.3 0.0 copy-done.8
  195.3 0.0 copy-done.9
  195.3 2.1 weight_grads.1
  197.4 30.5 %all_to_all.10.in_ref = bf16[8,24,2048]{2,1,0:T(8,128)(2,1)S(1)} all-to-all(bf16[8,24,2048]{2,1,0:T(8,128)(2,1)S(1)} %bitcast.22), channel_id=1, replica_groups=mesh['segment'=4,'chan'=16,'dp'=8] {'dp'}, dimensions={0} | all-to-all | bytes 1572864 | tf_op jit(solution)/shard_map/all_to_all | solution.py:507
  227.9 0.1 sum_microbatches.1
  228.0 24.7 %all_to_all.11 = bf16[8,24,2048]{2,1,0:T(8,128)(2,1)S(1)} all-to-all(bf16[8,24,2048]{2,1,0:T(8,128)(2,1)S(1)} %sum_microbatches.1), channel_id=1, replica_groups=mesh['segment'=4,'chan'=16,'dp'=8] {'dp'}, dimensions={0} | all-to-all | bytes 1572864 | tf_op jit(solution)/shard_map/all_to_all | solution.py:509
  252.8 1.2 widen.1
  (3 shorter events, 0.1 us)
Async XLA Ops:
  7.2 107.8 %all-gather.3.cloned.1.call-start = ((), (), s32[]{:S(2)}) async-start(), calls=%async_computation.2 | async-start | bytes 7962624 | tf_op jit(solution)/shard_map/all_gather | solution.py:429
  7.2 1.1 copy-start.2
  8.3 0.9 copy-start.4
  9.2 0.8 copy-start.6
  10.0 0.8 copy-start.7
  10.8 0.7 copy-start.10
  11.5 0.7 copy-start.11
  12.2 1.3 copy-start.12
  13.4 20.3 %copy-start.3 = (bf16[1,2,96,1536]{3,2,1,0:T(8,128)(2,1)S(1)}, bf16[1,2,96,1536]{3,2,1,0:T(8,128)(2,1)}, u32[]{:S(2)}) copy-start(bf16[1,2,96,1536]{3,2,1,0:T(8,128)(2,1)} %refs_2_.5) | copy-start | bytes 1769476
  13.4 20.3 %copy-start.5 = (bf16[1,2,96,432]{3,2,1,0:T(8,128)(2,1)S(1)}, bf16[1,2,96,432]{3,2,1,0:T(8,128)(2,1)}, u32[]{:S(2)}) copy-start(bf16[1,2,96,432]{3,2,1,0:T(8,128)(2,1)} %refs_3_.5) | copy-start | bytes 497668
  115.0 3.0 %copy-start = (bf16[16,96,2304]{2,1,0:T(8,128)(2,1)S(1)}, bf16[16,96,2304]{2,1,0:T(8,128)(2,1)}, u32[]{:S(2)}) copy-start(bf16[16,96,2304]{2,1,0:T(8,128)(2,1)} %all-gather.3.cloned.1.call-done) | copy-start | bytes 21233668
  118.0 4.4 %copy-start.1 = (bf16[16,96,2304]{2,1,0:T(8,128)(2,1)S(1)}, bf16[16,96,2304]{2,1,0:T(8,128)(2,1)}, u32[]{:S(2)}) copy-start(bf16[16,96,2304]{2,1,0:T(8,128)(2,1)} %all-gather.3.cloned.1.call-done) | copy-start | bytes 21233668
  185.7 9.6 %copy-start.8 = (bf16[1,1,96,256]{3,2,1,0:T(8,128)(2,1)S(1)}, bf16[1,1,96,256]{3,2,1,0:T(8,128)(2,1)}, u32[]{:S(2)}) copy-start(bf16[1,1,96,256]{3,2,1,0:T(8,128)(2,1)} %refs_6_.1) | copy-start | bytes 147460
  185.7 9.6 %copy-start.9 = (bf16[1,1,96,256]{3,2,1,0:T(8,128)(2,1)S(1)}, bf16[1,1,96,256]{3,2,1,0:T(8,128)(2,1)}, u32[]{:S(2)}) copy-start(bf16[1,1,96,256]{3,2,1,0:T(8,128)(2,1)} %refs_7_.1) | copy-start | bytes 147460
Sparse Core Ops, SparseCore 0:
  13.6 101.3 all-gather.2

commit v3 on v2

--- a/solution.py
+++ b/solution.py
@@ -48,16 +48,24 @@
     return jnp.sum(jnp.where(down == across, line, 0.0), axis=1, keepdims=True)
 
 
-def prepare_kernel(
-    w_ref, wc_ref, h1_ref, h2_ref, gain_ref, bias_ref,
-    pack_ref, xhat_ref, slope_ref, rate_ref, act_ref,
-):
+def prepare_kernel(*refs):
+    pack_refs = (refs[6], refs[7])
+    xhat_ref, slope_ref, rate_ref, act_ref = refs[8:12]
+    w_ref, wc_ref, h1_ref, h2_ref, gain_ref, bias_ref, sems = refs[12:]
+    copies = [
+        pltpu.make_async_copy(refs[i], refs[12 + i], sems.at[i]) for i in range(6)
+    ]
+    for copy in copies:
+        copy.start()
+    for copy in copies:
+        copy.wait()
     chans, width = w_ref.shape[2:]
     taps = wc_ref.shape[3]
     lane = lax.broadcasted_iota(jnp.int32, (chans, TAIL - 384), 1)
-    for b, h_ref in enumerate((h1_ref, h2_ref)):
-        pack_ref[b, :, :width] = w_ref[0, b]
-        pack_ref[b, :, width : width + 384] = wc_ref[0, b, :, :384]
+    for b, h_ref in ((1, h2_ref), (0, h1_ref)):
+        pack_ref = pack_refs[b]
+        pack_ref[:, :width] = w_ref[0, b]
+        pack_ref[:, width : width + 384] = wc_ref[0, b, :, :384]
         last = wc_ref[0, b, :, 384:].astype(F32)
         last = jnp.concatenate(
             [last, jnp.zeros((chans, TAIL - taps), F32)], axis=1
@@ -72,8 +80,8 @@
                 rest = rest - piece
                 last = jnp.where(lane == at, piece, last)
                 at += 1
-        pack_ref[b, :, width + 384 : width + TAIL] = last.astype(BF16)
-        pack_ref[b, :, width + TAIL :] = h_ref[0, 0]
+        pack_ref[:, width + 384 : width + TAIL] = last.astype(BF16)
+        pack_ref[:, width + TAIL :] = h_ref[0, 0]
         for q in range(0, chans, GS):
             rows = slice(q, q + GS)
             xhat, n, sig, slope, inv_std = norm_group(
@@ -85,62 +93,46 @@
             act_ref[b, rows, :] = (n * sig).astype(BF16)
 
 
-def prepare(proj_weight, conv_weight, conv_one, conv_two, gain, bias):
-    chans, width = proj_weight.shape[2:]
-    positions = conv_one.shape[3]
+def prepare(*operands):
+    chans, width = operands[0].shape[2:]
+    positions = operands[2].shape[3]
     full = shape_of((2, chans, positions), F32)
+    pack = shape_of((chans, width + TAIL + positions), BF16)
     return pl.pallas_call(
         prepare_kernel,
-        out_shape=(
-            shape_of((2, chans, width + TAIL + positions), BF16),
-            full,
-            full,
-            full,
-            shape_of((2, chans, positions), BF16),
-        ),
-        in_specs=[VMEM] * 6,
-        out_specs=[VMEM] * 5,
+        out_shape=(pack, pack, full, full, full, shape_of((2, chans, positions), BF16)),
+        in_specs=[pl.BlockSpec(memory_space=pltpu.HBM)] * 6,
+        out_specs=[VMEM] * 6,
+        scratch_shapes=[pltpu.VMEM(x.shape, x.dtype) for x in operands]
+        + [pltpu.SemaphoreType.DMA((6,))],
         compiler_params=PARAMS,
         name="prepare",
-    )(proj_weight, conv_weight, conv_one, conv_two, gain, bias)
-
-
-def wide_norm_kernel(taps, tail_ref, h_ref, xhat_ref, rate_ref):
-    count, _, chans, _ = tail_ref.shape
-    at = taps - 384
-    for b in range(2):
-        for y in range(count):
-            side = tail_ref[y, b, :, 384:].astype(F32)
-            gain = side[:, at : at + 1] + side[:, at + 1 : at + 2] + side[:, at + 2 : at + 3]
-            bias = side[:, at + 3 : at + 4] + side[:, at + 4 : at + 5] + side[:, at + 5 : at + 6]
-            for q in range(0, chans, GS):
-                rows = slice(q, q + GS)
-                xhat, _, _, slope, inv_std = norm_group(
-                    h_ref[y, b, rows, :], gain[rows], bias[rows]
-                )
-                to = slice(y * chans + q, y * chans + q + GS)
-                xhat_ref[b, to, :] = xhat
-                rate_ref[b, to, :] = slope * (gain[rows] * inv_std)
-
-
-def wide_norm(packs, width, positions):
-    count, _, chans, _ = packs.shape
-    full = shape_of((2, count * chans, positions), F32)
+    )(*operands)
+
+
+def wide_norm_kernel(width, pack_ref, xhat_ref, rate_ref):
+    chans = pack_ref.shape[0]
+    at = 9 * GS - 384
+    for q in range(0, chans, GS):
+        rows = slice(q, q + GS)
+        side = pack_ref[rows, width + 384 : width + TAIL].astype(F32)
+        gain = side[:, at : at + 1] + side[:, at + 1 : at + 2] + side[:, at + 2 : at + 3]
+        bias = side[:, at + 3 : at + 4] + side[:, at + 4 : at + 5] + side[:, at + 5 : at + 6]
+        xhat, _, _, slope, inv_std = norm_group(pack_ref[rows, width + TAIL :], gain, bias)
+        xhat_ref[0, rows, :] = xhat
+        rate_ref[0, rows, :] = slope * (gain * inv_std)
+
+
+def wide_norm(pack, width, positions):
+    full = shape_of((1, pack.shape[0], positions), F32)
     return pl.pallas_call(
-        functools.partial(wide_norm_kernel, 9 * GS),
+        functools.partial(wide_norm_kernel, width),
         out_shape=(full, full),
-        grid=(1,),
-        in_specs=[
-            pl.BlockSpec((count, 2, chans, TAIL), lambda i: (0, 0, 0, width // TAIL)),
-            pl.BlockSpec(
-                (count, 2, chans, positions),
-                lambda i: (0, 0, 0, (width + TAIL) // positions),
-            ),
-        ],
+        in_specs=[VMEM],
         out_specs=[VMEM] * 2,
         compiler_params=PARAMS,
         name="wide_norm",
-    )(packs, packs)
+    )(pack)
 
 
 def shifted(value, step_row, step_col, row, col):
@@ -171,10 +163,13 @@
     return lax.dot_general(pick, g, NT, preferred_element_type=F32).astype(BF16)
 
 
-def block(b, wide, flags, g, ordered, params, state, saved, latent, make_latent):
+def block(
+    b, wide, flags, g, ordered, own_chans, params, state, saved, latent, make_latent
+):
     xhat, rate = state
     chans, positions = xhat.shape[1:]
-    own_rows = params[0].shape[-2]
+    own_rows = own_chans
+    at_b = 0 if wide else b
     whole = g.shape[0]
     slab = positions // (whole // own_rows)
     first = saved is None
@@ -217,10 +212,9 @@
         if wide:
             (pack_ref,) = weights
             width = whole
-            for y in range(per):
-                ga_buf[y * own_rows : (y + 1) * own_rows, :] = jnp.dot(
-                    pack_ref[y, b, :, :width], src[...], preferred_element_type=F32
-                )
+            ga_buf[...] = jnp.dot(
+                pack_ref[:, :width], src[...], preferred_element_type=F32
+            )
         else:
             w_ref, wc_ref = weights
             ga_buf[...] = jnp.dot(w_ref[0, b], src[...], preferred_element_type=F32)
@@ -229,13 +223,13 @@
             y, q = divmod(at, own_rows)
             rows = slice(at, at + GS)
             if wide:
-                taps_w = pack_ref[y, b, q : q + GS, width : width + 9 * GS]
+                taps_w = pack_ref[rows, width : width + 9 * GS]
                 mine_at = (2 * y + core) * own_rows + q
             else:
                 taps_w = wc_ref[0, b, q : q + GS, :]
                 mine_at = chan_at * own_rows + q
-            xhat_q = xhat_ref[b, rows, :]
-            rw = ga_buf[rows, :] * rate_ref[b, rows, :]
+            xhat_q = xhat_ref[at_b, rows, :]
+            rw = ga_buf[rows, :] * rate_ref[at_b, rows, :]
             gh = rw - total(rw) * scale - xhat_q * (total(rw * xhat_q) * scale)
             gh = gh.astype(BF16)
             gh_buf[rows, :] = gh
@@ -306,40 +300,87 @@
     return result[0], tuple(result[1:4]), result[4] if has_latent else latent
 
 
-def weights_kernel(*refs):
-    flags_ref, last_ref, lat_in_ref = refs[:3]
-    act_ref, xhat_ref, slope_ref = refs[3:6]
-    x_refs = refs[6:8]
-    saved_refs = (refs[8:11], refs[11:14])
-    out_ref, lat_ref, stack, g_buf = refs[14:]
-    chans, positions = x_refs[0].shape[2:]
-    width = out_ref.shape[1] - TAIL
+def weight_blocks(b, act_ref, xhat_ref, slope_ref, x_ref, saved_refs, stack, store):
+    g_ref, gh_ref, ga_ref = saved_refs
+    chans, positions = x_ref.shape[2:]
+    width = g_ref.shape[0]
     row, col = grid_of((GS, positions))
     lane = lax.broadcasted_iota(jnp.int32, (GS, TAIL), 1)
     stack[9 * GS :, :] = jnp.zeros((TAIL - 9 * GS, positions), BF16)
-    for b in range(2):
-        g_ref, gh_ref, ga_ref = saved_refs[b]
-        x_ref = x_refs[b]
-        at = b * chans
-        out_ref[at : at + chans, :width] = lax.dot_general(
-            act_ref[b], g_ref[...], NT, preferred_element_type=F32
-        ).astype(BF16)
-        for q in range(0, chans, GS):
-            rows = slice(q, q + GS)
-            x = x_ref[0, 0, rows, :].astype(F32)
-            for step_row in (-1, 0, 1):
-                for step_col in (-1, 0, 1):
-                    tap = 3 * (step_row + 1) + step_col + 1
-                    stack[tap * GS : (tap + 1) * GS, :] = shifted(
-                        x, step_row, step_col, row, col
-                    ).astype(BF16)
-            taps = lax.dot_general(gh_ref[rows, :], stack[...], NT, preferred_element_type=F32)
-            gn = ga_ref[rows, :] * slope_ref[b, rows, :]
-            by_gain = jnp.sum(gn * xhat_ref[b, rows, :], axis=1, keepdims=True)
-            by_bias = jnp.sum(gn, axis=1, keepdims=True)
-            taps = jnp.where(lane == 9 * GS, by_gain, taps)
-            taps = jnp.where(lane == 9 * GS + 1, by_bias, taps)
-            out_ref[at + q : at + q + GS, width:] = taps.astype(BF16)
+    store(
+        slice(0, chans),
+        0,
+        lax.dot_general(act_ref[b], g_ref[...], NT, preferred_element_type=F32).astype(BF16),
+    )
+    for q in range(0, chans, GS):
+        rows = slice(q, q + GS)
+        x = x_ref[0, 0, rows, :].astype(F32)
+        for step_row in (-1, 0, 1):
+            for step_col in (-1, 0, 1):
+                tap = 3 * (step_row + 1) + step_col + 1
+                stack[tap * GS : (tap + 1) * GS, :] = shifted(
+                    x, step_row, step_col, row, col
+                ).astype(BF16)
+        taps = lax.dot_general(gh_ref[rows, :], stack[...], NT, preferred_element_type=F32)
+        gn = ga_ref[rows, :] * slope_ref[b, rows, :]
+        by_gain = jnp.sum(gn * xhat_ref[b, rows, :], axis=1, keepdims=True)
+        by_bias = jnp.sum(gn, axis=1, keepdims=True)
+        taps = jnp.where(lane == 9 * GS, by_gain, taps)
+        taps = jnp.where(lane == 9 * GS + 1, by_bias, taps)
+        store(rows, width, taps.astype(BF16))
+
+
+def storer(out_ref, first_row):
+    step = out_ref.shape[2]
+
+    def store(rows, at, value):
+        to = slice(first_row + rows.start, first_row + rows.stop)
+        for i in range(value.shape[1] // step):
+            out_ref[at // step + i, to, :] = value[:, i * step : (i + 1) * step]
+
+    return store
+
+
+def early_kernel(act_ref, xhat_ref, slope_ref, x_ref, g_ref, gh_ref, ga_ref, out_ref, stack):
+    weight_blocks(
+        1, act_ref, xhat_ref, slope_ref, x_ref, (g_ref, gh_ref, ga_ref), stack,
+        storer(out_ref, 0),
+    )
+
+
+def early_grads(members, act, xhat, slope, x, saved):
+    chans, positions = act.shape[1:]
+    step = (saved[0].shape[0] + TAIL) // members
+    return pl.pallas_call(
+        early_kernel,
+        out_shape=shape_of((members, chans, step), BF16),
+        in_specs=[VMEM] * 7,
+        out_specs=VMEM,
+        scratch_shapes=[pltpu.VMEM((TAIL, positions), BF16)],
+        compiler_params=PARAMS,
+        name="early_weight_grads",
+    )(act, xhat, slope, x, *saved)
+
+
+def summed(in_ref, rows):
+    acc = in_ref[0, rows, :].astype(F32)
+    for m in range(1, in_ref.shape[0]):
+        acc = acc + in_ref[m, rows, :].astype(F32)
+    return acc.astype(BF16)
+
+
+def late_kernel(
+    flags_ref, last_ref, lat_in_ref, parts_ref, act_ref, xhat_ref, slope_ref, x_ref,
+    g_ref, gh_ref, ga_ref, out_ref, lat_ref, stack, g_buf,
+):
+    chans = x_ref.shape[2]
+    weight_blocks(
+        0, act_ref, xhat_ref, slope_ref, x_ref, (g_ref, gh_ref, ga_ref), stack,
+        storer(out_ref, chans),
+    )
+    done = summed(parts_ref, slice(0, chans))
+    for m in range(out_ref.shape[0]):
+        out_ref[m, :chans, :] = done
     lat_ref[...] = lat_in_ref[...]
 
     @pl.when(flags_ref[0] > 0)
@@ -353,40 +394,38 @@
         lat_ref[...] = own_positions(g_buf[...], flags_ref[2], lat_ref.shape[0])
 
 
-def weight_grads(flags, last, latent, act, xhat, slope, inputs, saved):
-    chans, positions = act.shape[1:]
-    width = last.shape[0]
+def late_grads(flags, last, latent, parts, act, xhat, slope, x, saved):
+    members, chans, step = parts.shape
+    positions = act.shape[2]
     return pl.pallas_call(
-        weights_kernel,
+        late_kernel,
         out_shape=(
-            shape_of((2 * chans, width + TAIL), BF16),
+            shape_of((members, 2 * chans, step), BF16),
             shape_of(latent.shape, BF16),
         ),
-        in_specs=[SMEM] + [VMEM] * 13,
+        in_specs=[SMEM] + [VMEM] * 10,
         out_specs=[VMEM] * 2,
         scratch_shapes=[
             pltpu.VMEM((TAIL, positions), BF16),
-            pltpu.VMEM((width, positions), BF16),
+            pltpu.VMEM(last.shape, BF16),
         ],
         compiler_params=PARAMS,
-        name="weight_grads",
-    )(flags, last, latent, act, xhat, slope, *inputs, *saved[0], *saved[1])
-
-
-def reduce_kernel(in_ref, out_ref):
-    count = in_ref.shape[0]
-    acc = in_ref[0].astype(F32)
-    for m in range(1, count):
-        acc = acc + in_ref[m].astype(F32)
-    done = acc.astype(BF16)
-    for m in range(count):
+        name="late_weight_grads",
+    )(flags, last, latent, parts, act, xhat, slope, x, *saved)
+
+
+def sum_kernel(in_ref, out_ref):
+    chans = out_ref.shape[1]
+    done = summed(in_ref, slice(chans, 2 * chans))
+    for m in range(out_ref.shape[0]):
         out_ref[m] = done
 
 
-def spread_sum(parts):
+def late_sums(parts):
+    members, rows, step = parts.shape
     return pl.pallas_call(
-        reduce_kernel,
-        out_shape=shape_of(parts.shape, BF16),
+        sum_kernel,
+        out_shape=shape_of((members, rows // 2, step), BF16),
         in_specs=[VMEM],
         out_specs=VMEM,
         compiler_params=PARAMS,
@@ -394,22 +433,26 @@
     )(parts)
 
 
-def widen_kernel(in_ref, proj_ref, conv_ref, gain_ref, bias_ref):
+def widen_kernel(late_ref, early_ref, proj_ref, conv_ref, gain_ref, bias_ref):
     chans, width = proj_ref.shape[2:]
+    step = late_ref.shape[2]
     down = lax.broadcasted_iota(jnp.int32, (chans, chans), 0)
     across = lax.broadcasted_iota(jnp.int32, (chans, chans), 1)
-    at = 9 * GS - (TAIL - 128)
-    for b in range(2):
-        rows = slice(b * chans, (b + 1) * chans)
-        proj_ref[0, b] = in_ref[rows, :width].astype(F32)
-        conv_ref[0, b] = in_ref[rows, width : width + 9 * GS].astype(F32)
-        tail = in_ref[rows, width + TAIL - 128 :].astype(F32)
-        for i, ref in enumerate((gain_ref, bias_ref)):
-            lined = jnp.where(down == across, tail[:, at + i : at + i + 1], 0.0)
-            ref[0, b : b + 1, :] = jnp.sum(lined, axis=0, keepdims=True)
-
-
-def widen(sums, chans, width):
+    first = width // step
+    for b, ref in ((0, late_ref), (1, early_ref)):
+        for i in range(first):
+            proj_ref[0, b, :, i * step : (i + 1) * step] = ref[i, :chans, :].astype(F32)
+        conv_ref[0, b, :, :step] = ref[first, :chans, :].astype(F32)
+        side = ref[first + 1, :chans, :].astype(F32)
+        conv_ref[0, b, :, step:] = side[:, : 9 * GS - step]
+        for i, to in enumerate((gain_ref, bias_ref)):
+            at = 9 * GS - step + i
+            lined = jnp.where(down == across, side[:, at : at + 1], 0.0)
+            to[0, b : b + 1, :] = jnp.sum(lined, axis=0, keepdims=True)
+
+
+def widen(late, early, width):
+    chans = late.shape[1]
     return pl.pallas_call(
         widen_kernel,
         out_shape=(
@@ -418,11 +461,11 @@
             shape_of((1, 2, chans), F32),
             shape_of((1, 2, chans), F32),
         ),
-        in_specs=[VMEM],
+        in_specs=[VMEM] * 2,
         out_specs=[VMEM] * 4,
         compiler_params=PARAMS,
         name="widen",
-    )(sums)
+    )(late, early)
 
 
 def gather(block_, axis, groups=None):
@@ -450,15 +493,26 @@
     cores = [[2 * y, 2 * y + 1] for y in range(shards // 2)]
     columns = [[2 * y + c for y in range(shards // 2)] for c in range(2)]
 
-    pack, xhat, slope, rate, act = prepare(
+    def near(own_only):
+        return ("chan", None) if own_only else ("chan", cores)
+
+    def exchange(blocks):
+        return lax.all_to_all(blocks, "dp", split_axis=0, concat_axis=0, tiled=True)
+
+    first_pack, second_pack, xhat, slope, rate, act = prepare(
         proj_weight, conv_weight, conv_one, conv_two, norm_gain, norm_bias
     )
-    packs = gather(pack, "chan", columns).reshape((shards // 2,) + pack.shape)
+    packs = [None, gather(second_pack, "chan", columns)]
+    packs[0] = lax.all_gather(
+        first_pack[None], "chan", axis=1, tiled=True, axis_index_groups=columns
+    )[0]
     own = (proj_weight, conv_weight)
-    wide_state = None
+    wide_state = [None, None]
     saved = [None, None]
     latent = None
     out = None
+    ordered = True
+    parts = None
     for tick in range(segments):
         flags = jnp.stack(
             [
@@ -476,38 +530,40 @@
                 [[lower, lower + 1]] + [rest[i : i + 2] for i in range(0, len(rest), 2)]
             )
             half = out.shape[0]
-            moved = gather(out, "segment", groups)[half:]
-            g = gather(moved, "chan", None if half == chans else cores)
+            g = gather(gather(out, "segment", groups)[half:], *near(half == chans))
         for b in (1, 0):
-            ordered = tick == 0 or out.shape[0] == chans
-            wide = tick > 1 or (tick == 1 and b == 0)
-            if wide and wide_state is None:
-                packs, g = lax.optimization_barrier((packs, g))
-                wide_state = wide_norm(packs, width, positions)
+            wide = tick > 1 or (tick == 1 and b == 1)
+            if wide and wide_state[b] is None:
+                packs[b], g = lax.optimization_barrier((packs[b], g))
+                wide_state[b] = wide_norm(packs[b], width, positions)
             out, saved[b], kept = block(
                 b,
                 wide,
                 flags,
                 g,
                 ordered,
-                (packs,) if wide else own,
-                wide_state if wide else (xhat, rate),
+                chans,
+                (packs[b],) if wide else own,
+                wide_state[b] if wide else (xhat, rate),
                 saved[b],
                 latent if b == 1 else None,
                 b == 1 and tick == 1,
             )
             latent = kept if b == 1 else latent
+            ordered = out.shape[0] == chans
+            if b == 1 and tick == segments - 1:
+                parts = exchange(
+                    early_grads(members, act, xhat, slope, inputs_two, saved[1])
+                )
             if b == 1 or tick == segments - 1:
-                g = gather(out, "chan", None if out.shape[0] == chans else cores)
-
-    grads, latent = weight_grads(
-        flags, g, latent, act, xhat, slope, (inputs_one, inputs_two), saved
+                g = gather(out, *near(ordered))
+
+    both, latent = late_grads(
+        flags, g, latent, parts, act, xhat, slope, inputs_one, saved[0]
     )
-    parts = grads.reshape(members, 2 * chans // members, width + TAIL)
-    parts = lax.all_to_all(parts, "dp", split_axis=0, concat_axis=0, tiled=True)
-    parts = spread_sum(parts)
-    parts = lax.all_to_all(parts, "dp", split_axis=0, concat_axis=0, tiled=True)
-    proj, conv, by_gain, by_bias = widen(parts.reshape(2 * chans, width + TAIL), chans, width)
+    both = exchange(both)
+    late = exchange(late_sums(both))
+    proj, conv, by_gain, by_bias = widen(late, both, width)
     return latent.T[None, None], proj, conv, by_gain, by_bias
 
 

time: 261 us -> 270 us (1.034)
  local copies, waits for them, and re-layouts: 8.29 us -> 43.5 us
  blocking collectives: 181 us -> 163 us
  Pallas kernels: 50.2 us -> 35.2 us
  starting transfers between devices: 0.04 us -> 10.4 us
  waiting for transfers between devices: 6.49 us -> 0.72 us
    unnamed x26 -> x166, local copies, waits for them, and re-layouts: 7.97 us -> 43.2 us
    pallas_call x8, Pallas kernels: 41.2 us -> 24.5 us  [block(): pl.pallas_call(kernel, out_shape=shapes, in_specs=in_specs, out_specs=out...]
    all_to_all x0 -> x1, starting transfers between devices: none -> 10.3 us  [exchange(): return lax.all_to_all(blocks, 'dp', split_axis=0, concat_axis=0, tiled=True)]
    all_gather x11, blocking collectives: 106 us -> 96.6 us  [gather(): lax.all_gather(block_, axis, axis=0, tiled=True, axis_index_groups=groups)]
    all_to_all x2, blocking collectives: 55.3 us -> 46.7 us  [exchange(): return lax.all_to_all(blocks, 'dp', split_axis=0, concat_axis=0, tiled=True)]
    all_gather x1, waiting for transfers between devices: 6.47 us -> 0.01 us  [gather(): lax.all_gather(block_, axis, axis=0, tiled=True, axis_index_groups=groups)]
    pallas_call x4 -> x6, Pallas kernels: 7.86 us -> 9.51 us  [the longest x2 4.98 us: wide_norm(): pl.pallas_call(functools.partial(wide_norm_kernel, width), out_shape=(ful...]
  transfers between devices with their start and end apart: 1 -> 3, of which waited for: 1 -> 0; matrix products, arithmetic and copies ran while one was open for 0% -> 0% of each run, Pallas kernels for 2% -> 7%
where the time goes in v3:
time: 270 us; the launch traced here: 268 us
  blocking collectives  163 us (60%)
  local copies, waits for them, and re-layouts  43.5 us (16%)
  Pallas kernels  35.2 us (13%)
  between operations  14.6 us (5%)
  starting transfers between devices  10.4 us (4%)
    all_gather x11, blocking collectives, gather(): lax.all_gather(block_, axis, axis=0, tiled=True, axis_index_groups=groups)  96.6 us
    all_to_all x2, blocking collectives, exchange(): return lax.all_to_all(blocks, 'dp', split_axis=0, concat_axis=0, tiled=True)  46.7 us
    unnamed x166, local copies, waits for them, and re-layouts  43.2 us
    pallas_call x8, Pallas kernels, block(): pl.pallas_call(kernel, out_shape=shapes, in_specs=in_specs, out_specs=out...  24.5 us
    all_gather x1, blocking collectives, per_device(): g = lax.all_gather(grad_top[0], 'chan', axis=1, tiled=True)  20 us
    all_to_all x1, starting transfers between devices, exchange(): return lax.all_to_all(blocks, 'dp', split_axis=0, concat_axis=0, tiled=True)  10.3 us
  transfers between devices with their start and end apart: 3, of which 0 were waited for; matrix products, arithmetic and copies ran while one was open for 0% of the time, Pallas kernels for 7%

profile of v3, /device:TPU:6, one launch (start us, length us, event | category | flops | bytes accessed | tf_op | source)
XLA Modules:
  0.0 268.0 jit_solution(14781978229029621259)
XLA Ops:
  7.2 1.1 copy-done.19
  8.3 0.9 copy-done.30
  9.2 0.8 copy-done.77
  10.0 0.8 copy-done.78
  12.2 1.8 prepare.1
  14.0 0.7 copy-done.66
  15.4 0.7 all-gather.7.cloned.1.call-update
  16.1 20.0 %all-gather.1 = bf16[1,1536,256]{1,2,0:T(8,128)(2,1)S(1)} all-gather(bf16[1,1536,16]{1,2,0:T(8,128)(2,1)} %param.9), channel_id=3, replica_groups=mesh['segment'=4,'chan'=16,'dp'=8] {'chan'}, dimensions={2}, use_global_device_ids=true | all-gather | bytes 835584 | tf_op jit(solution)/shard_map/all_gather | solution.py:525
  36.5 1.5 own_block.3
  38.0 0.9 copy-done.13
  40.2 21.6 %all_gather.45.refs_1_ = bf16[1536,256]{1,0:T(8,128)(2,1)S(1)} all-gather(bf16[96,256]{1,0:T(8,128)(2,1)S(1)} %get-tuple-element.64), channel_id=1, replica_groups=mesh['segment'=4,'chan'=16,'dp'=8] {'chan'}, dimensions={0}, use_global_device_ids=true | all-gather | bytes 835584 | tf_op jit(solution)/shard_map/all_gather | solution.py:472
  61.7 1.5 own_block.4
  63.3 0.9 copy-done.5
  64.8 4.8 %all_gather.46 = bf16[192,256]{1,0:T(8,128)(2,1)S(1)} all-gather(bf16[96,256]{1,0:T(8,128)(2,1)S(1)} %get-tuple-element.65), channel_id=1, replica_groups={{0,128},{256,384},{1,129},{257,385},{2,130},{258,386},{3,131},{259,387}..., dimensions={0}, use_global_device_ids=true | all-gather | bytes 147456 | tf_op jit(solution)/shard_map/all_gather | solution.py:472
  69.8 19.1 %all_gather.47.refs_1_ = bf16[1536,256]{1,0:T(8,128)(2,1)} all-gather(bf16[96,256]{1,0:T(8,128)(2,1)S(1)} %slice.12), channel_id=1, replica_groups=mesh['segment'=4,'chan'=16,'dp'=8] {'chan'}, dimensions={0}, use_global_device_ids=true | all-gather | bytes 835584 | tf_op jit(solution)/shard_map/all_gather | solution.py:472
  88.9 2.0 copy-done
  90.9 2.5 wide_norm.2
  93.4 1.7 copy-done.14
  95.1 1.1 copy-done.33
  96.2 0.9 copy-done.51
  97.1 0.8 copy-done.55
  98.0 4.2 %wide_block.5 = (bf16[768,256]{1,0:T(8,128)(2,1)S(1)}, bf16[1536,256]{1,0:T(8,128)(2,1)S(1)}, bf16[96,256]{1,0:T(8,128)(2,1)S(1)}, f32[96,256]{1,0:T(8,128)S(1)}, bf16[16,1536]{1,0:T(8,128)(2,1)S(1)}) custom-call(s32[3]{0:T(128)S(1)} %add_add_fusion.2.refs_0_, ...), custom_call_target="tpu_custom_call", output_to_operand_aliasing={{1}: (5, {}), {2}: (6, {}), {3}: (7, {})} | custom-call | tf_op jit(solution)/shard_map/wide_block/pallas_call | solution.py:285
  102.2 2.4 all_gather.48.refs_1_
  104.7 1.5 own_block.5
  106.2 6.1 %all_gather.49 = bf16[192,256]{1,0:T(8,128)(2,1)S(1)} all-gather(bf16[96,256]{1,0:T(8,128)(2,1)S(1)} %get-tuple-element.77), channel_id=1, replica_groups={{0,384},{128,256},{1,385},{129,257},{2,386},{130,258},{3,387},{131,259}..., dimensions={0}, use_global_device_ids=true | all-gather | bytes 147456 | tf_op jit(solution)/shard_map/all_gather | solution.py:472
  112.3 20.7 %all_gather.50.refs_1_ = bf16[1536,256]{1,0:T(8,128)(2,1)S(1)} all-gather(bf16[96,256]{1,0:T(8,128)(2,1)S(1)} %slice.13), channel_id=1, replica_groups=mesh['segment'=4,'chan'=16,'dp'=8] {'chan'}, dimensions={0}, use_global_device_ids=true | all-gather | bytes 835584 | tf_op jit(solution)/shard_map/all_gather | solution.py:472
  133.0 3.9 %wide_block.6 = (bf16[768,256]{1,0:T(8,128)(2,1)S(1)}, bf16[1536,256]{1,0:T(8,128)(2,1)S(1)}, bf16[96,256]{1,0:T(8,128)(2,1)S(1)}, f32[96,256]{1,0:T(8,128)S(1)}, bf16[16,1536]{1,0:T(8,128)(2,1)S(1)}) custom-call(s32[3]{0:T(128)S(1)} %add_add_fusion.1.refs_0_, ...), custom_call_target="tpu_custom_call", output_to_operand_aliasing={{1}: (5, {}), {2}: (6, {}), {3}: (7, {}), {4}: (8, {})} | custom-call | tf_op jit(solution)/shard_map/wide_block/pallas_call | solution.py:285
  137.0 0.9 copy-done.17
  139.7 2.7 all_gather.51.refs_1_
  142.4 2.0 copy-done.2
  144.4 2.5 wide_norm.3
  147.0 1.7 copy-done.8
  148.6 1.1 copy-done.34
  149.8 0.9 copy-done.44
  150.7 0.8 copy-done.61
  151.5 3.9 %wide_block.7 = (bf16[768,256]{1,0:T(8,128)(2,1)S(1)}, bf16[1536,256]{1,0:T(8,128)(2,1)S(1)}, bf16[96,256]{1,0:T(8,128)(2,1)S(1)}, f32[96,256]{1,0:T(8,128)S(1)}) custom-call(s32[3]{0:T(128)S(1)} %add_add_fusion.1.refs_0_, bf16[1536,256]{1,0:T(8,128)(2,1)S(1)} %copy-done.34, ...), custom_call_target="tpu_custom_call", output_to_operand_aliasing={{1}: (5, {}), {2}: (6, {}), {3}: (7, {})} | custom-call | tf_op jit(solution)/shard_map/wide_block/pallas_call | solution.py:285
  155.5 0.9 copy-done.9
  156.4 12.0 %all_gather.52 = bf16[1536,256]{1,0:T(8,128)(2,1)S(1)} all-gather(bf16[768,256]{1,0:T(8,128)(2,1)S(1)} %get-tuple-element.90), channel_id=1, replica_groups={{0,128},{256,384},{1,129},{257,385},{2,130},{258,386},{3,131},{259,387}..., dimensions={0}, use_global_device_ids=true | all-gather | bytes 1179648 | tf_op jit(solution)/shard_map/all_gather | solution.py:472
  168.4 2.4 all_gather.53.refs_1_
  170.9 3.9 %wide_block.8 = (bf16[768,256]{1,0:T(8,128)(2,1)S(1)}, bf16[1536,256]{1,0:T(8,128)(2,1)S(1)}, bf16[96,256]{1,0:T(8,128)(2,1)S(1)}, f32[96,256]{1,0:T(8,128)S(1)}, bf16[16,1536]{1,0:T(8,128)(2,1)S(1)}) custom-call(s32[3]{0:T(128)S(1)} %add_add_fusion.refs_0_.flags_ref, ...), custom_call_target="tpu_custom_call", output_to_operand_aliasing={{1}: (5, {}), {2}: (6, {}), {3}: (7, {}), {4}: (8, {})} | custom-call | tf_op jit(solution)/shard_map/wide_block/pallas_call | solution.py:285
  175.5 0.7 copy-done.76
  176.8 0.8 copy-done.49
  177.5 10.3 %all-to-all-start = ((bf16[8,96,256]{2,1,0:T(8,128)(2,1)}), bf16[8,96,256]{2,1,0:T(8,128)(2,1)}, u32[]{:S(2)}, u32[]{:S(2)}) async-start(bf16[8,96,256]{2,1,0:T(8,128)(2,1)} %copy-done.49), calls=%async_computation | async-start | bytes 786432 | tf_op jit(solution)/shard_map/all_to_all | solution.py:500
  187.8 2.6 all_gather.54.refs_1_
  190.4 1.1 copy-done.10
  191.5 1.1 copy-done.36
  192.6 1.1 copy-done.38
  193.8 0.9 copy-done.46
  194.6 0.8 copy-done.63
  195.4 3.9 %wide_block.9 = (bf16[768,256]{1,0:T(8,128)(2,1)S(1)}, bf16[1536,256]{1,0:T(8,128)(2,1)S(1)}, bf16[96,256]{1,0:T(8,128)(2,1)S(1)}, f32[96,256]{1,0:T(8,128)S(1)}) custom-call(s32[3]{0:T(128)S(1)} %add_add_fusion.refs_0_.flags_ref, bf16[1536,256]{1,0:T(8,128)(2,1)S(1)} %all_gather.54.refs_1_, ...), custom_call_target="tpu_custom_call", output_to_operand_aliasing={{1}: (5, {}), {2}: (6, {}), {3}: (7, {})} | custom-call | tf_op jit(solution)/shard_map/wide_block/pallas_call | solution.py:285
  199.4 0.9 copy-done.11
  201.5 2.4 all_gather.55.last_ref
  203.9 1.1 copy-done.12
  205.0 0.9 copy-done.29
  206.0 0.9 copy-done.48
  206.9 0.8 copy-done.65
  207.7 0.9 copy-done.68
  208.6 0.8 copy-done.72
  209.4 0.9 copy-done.75
  210.3 0.8 copy-done.80
  211.1 2.1 late_weight_grads.1
  213.2 30.4 %all_to_all.15.in_ref.early_ref = bf16[8,192,256]{2,1,0:T(8,128)(2,1)S(1)} all-to-all(bf16[8,192,256]{2,1,0:T(8,128)(2,1)S(1)} %get-tuple-element.110), channel_id=1, replica_groups=mesh['segment'=4,'chan'=16,'dp'=8] {'dp'}, dimensions={0} | all-to-all | bytes 1572864 | tf_op jit(solution)/shard_map/all_to_all | solution.py:500
  243.7 16.3 %all_to_all.16.late_ref = bf16[8,96,256]{2,1,0:T(8,128)(2,1)S(1)} all-to-all(bf16[8,96,256]{2,1,0:T(8,128)(2,1)S(1)} %sum_microbatches.1), channel_id=1, replica_groups=mesh['segment'=4,'chan'=16,'dp'=8] {'dp'}, dimensions={0} | all-to-all | bytes 786432 | tf_op jit(solution)/shard_map/all_to_all | solution.py:500
  260.0 1.2 widen.1
  (147 shorter events, 9.1 us)
Async XLA Ops:
  7.2 81.7 %all-gather.5.cloned.1.call-start = ((), (), s32[]{:S(2)}) async-start(), calls=%async_computation.3 | async-start | bytes 3981312 | tf_op jit(solution)/shard_map/all_gather | solution.py:472
  7.2 1.1 copy-start.19
  8.3 0.9 copy-start.30
  12.2 24.3 %copy-start.20 = (bf16[1,2,96,1536]{3,2,1,0:T(8,128)(2,1)S(1)}, bf16[1,2,96,1536]{3,2,1,0:T(8,128)(2,1)}, u32[]{:S(2)}) copy-start(bf16[1,2,96,1536]{3,2,1,0:T(8,128)(2,1)} %refs_2_.7) | copy-start | bytes 1769476
  12.2 24.3 %copy-start.31 = (bf16[1,2,96,432]{3,2,1,0:T(8,128)(2,1)S(1)}, bf16[1,2,96,432]{3,2,1,0:T(8,128)(2,1)}, u32[]{:S(2)}) copy-start(bf16[1,2,96,432]{3,2,1,0:T(8,128)(2,1)} %refs_3_.7) | copy-start | bytes 497668
  15.3 48.0 %copy-start.26 = (f32[2,96,256]{2,1,0:T(8,128)}, f32[2,96,256]{2,1,0:T(8,128)S(1)}, u32[]{:S(2)}) copy-start(f32[2,96,256]{2,1,0:T(8,128)S(1)} %get-tuple-element.62.refs_4_.xhat_ref) | copy-start | bytes 589828
  15.3 48.0 %copy-start.39 = (f32[2,96,256]{2,1,0:T(8,128)}, f32[2,96,256]{2,1,0:T(8,128)S(1)}, u32[]{:S(2)}) copy-start(f32[2,96,256]{2,1,0:T(8,128)S(1)} %get-tuple-element.63.refs_5_) | copy-start | bytes 589828
  15.4 127.1 %all-gather.7.cloned.1.call-start = ((), (), s32[]{:S(2)}) async-start(), calls=%async_computation.4 | async-start | bytes 3981312 | tf_op jit(solution)/shard_map/all_gather | solution.py:506
  38.0 0.9 copy-start.13
  63.3 0.9 copy-start.5
  64.8 24.0 %copy-start.41 = (f32[96,256]{1,0:T(8,128)}, f32[96,256]{1,0:T(8,128)S(1)}, u32[]{:S(2)}) copy-start(f32[96,256]{1,0:T(8,128)S(1)} %get-tuple-element.76.refs_8_) | copy-start | bytes 294916
  88.9 2.0 copy-start
  90.9 2.5 copy-start.1
  93.4 39.7 %copy-start.22 = (f32[1,768,256]{2,1,0:T(8,128)}, f32[1,768,256]{2,1,0:T(8,128)S(1)}, u32[]{:S(2)}) copy-start(f32[1,768,256]{2,1,0:T(8,128)S(1)} %get-tuple-element.68.refs_3_) | copy-start | bytes 2359300
  93.4 39.6 %copy-start.24 = (f32[1,768,256]{2,1,0:T(8,128)}, f32[1,768,256]{2,1,0:T(8,128)S(1)}, u32[]{:S(2)}) copy-start(f32[1,768,256]{2,1,0:T(8,128)S(1)} %get-tuple-element.69.refs_4_) | copy-start | bytes 2359300
  93.4 1.7 copy-start.14
  95.1 1.1 copy-start.33
  96.2 0.9 copy-start.51
  97.9 6.7 %copy-start.6 = (bf16[1536,256]{1,0:T(8,128)(2,1)S(1)}, bf16[1536,256]{1,0:T(8,128)(2,1)}, u32[]{:S(2)}) copy-start(bf16[1536,256]{1,0:T(8,128)(2,1)} %copy-done.5) | copy-start | bytes 2359300
  97.9 6.7 %copy-start.21 = (bf16[1,2,96,1536]{3,2,1,0:T(8,128)(2,1)S(1)}, bf16[1,2,96,1536]{3,2,1,0:T(8,128)(2,1)}, u32[]{:S(2)}) copy-start(bf16[1,2,96,1536]{3,2,1,0:T(8,128)(2,1)} %refs_2_.7) | copy-start | bytes 1769476
  97.9 6.7 %copy-start.27 = (f32[2,96,256]{2,1,0:T(8,128)S(1)}, f32[2,96,256]{2,1,0:T(8,128)}, u32[]{:S(2)}) copy-start(f32[2,96,256]{2,1,0:T(8,128)} %copy-done.26) | copy-start | bytes 589828
  97.9 6.7 %copy-start.32 = (bf16[1,2,96,432]{3,2,1,0:T(8,128)(2,1)S(1)}, bf16[1,2,96,432]{3,2,1,0:T(8,128)(2,1)}, u32[]{:S(2)}) copy-start(bf16[1,2,96,432]{3,2,1,0:T(8,128)(2,1)} %refs_3_.7) | copy-start | bytes 497668
  97.9 6.7 %copy-start.40 = (f32[2,96,256]{2,1,0:T(8,128)S(1)}, f32[2,96,256]{2,1,0:T(8,128)}, u32[]{:S(2)}) copy-start(f32[2,96,256]{2,1,0:T(8,128)} %copy-done.39) | copy-start | bytes 589828
  98.0 6.7 %copy-start.42 = (f32[96,256]{1,0:T(8,128)S(1)}, f32[96,256]{1,0:T(8,128)}, u32[]{:S(2)}) copy-start(f32[96,256]{1,0:T(8,128)} %copy-done.41) | copy-start | bytes 294916
  98.0 6.7 %copy-start.59 = (bf16[96,256]{1,0:T(8,128)(2,1)S(1)}, bf16[96,256]{1,0:T(8,128)(2,1)}, u32[]{:S(2)}) copy-start(bf16[96,256]{1,0:T(8,128)(2,1)} %copy-done.58) | copy-start | bytes 147460
  102.2 2.4 copy-start.15
  104.7 28.4 %copy-start.16 = (bf16[1536,256]{1,0:T(8,128)(2,1)S(1)}, bf16[1536,256]{1,0:T(8,128)(2,1)}, u32[]{:S(2)}) copy-start(bf16[1536,256]{1,0:T(8,128)(2,1)} %copy-done.15) | copy-start | bytes 2359300
  106.2 30.8 %copy-start.7 = (bf16[1536,256]{1,0:T(8,128)(2,1)}, bf16[1536,256]{1,0:T(8,128)(2,1)S(1)}, u32[]{:S(2)}) copy-start(bf16[1536,256]{1,0:T(8,128)(2,1)S(1)} %get-tuple-element.87.refs_5_) | copy-start | bytes 2359300
  106.2 30.8 %copy-start.43 = (f32[96,256]{1,0:T(8,128)}, f32[96,256]{1,0:T(8,128)S(1)}, u32[]{:S(2)}) copy-start(f32[96,256]{1,0:T(8,128)S(1)} %get-tuple-element.89.refs_7_) | copy-start | bytes 294916
  106.2 30.8 %copy-start.60 = (bf16[96,256]{1,0:T(8,128)(2,1)}, bf16[96,256]{1,0:T(8,128)(2,1)S(1)}, u32[]{:S(2)}) copy-start(bf16[96,256]{1,0:T(8,128)(2,1)S(1)} %get-tuple-element.88.refs_6_) | copy-start | bytes 147460
  137.0 0.9 copy-start.17
  142.4 2.0 copy-start.2
  144.4 2.5 copy-start.3
  146.9 21.5 %copy-start.35 = (f32[1,768,256]{2,1,0:T(8,128)}, f32[1,768,256]{2,1,0:T(8,128)S(1)}, u32[]{:S(2)}) copy-start(f32[1,768,256]{2,1,0:T(8,128)S(1)} %get-tuple-element.85.refs_3_) | copy-start | bytes 2359300
  146.9 21.5 %copy-start.37 = (f32[1,768,256]{2,1,0:T(8,128)}, f32[1,768,256]{2,1,0:T(8,128)S(1)}, u32[]{:S(2)}) copy-start(f32[1,768,256]{2,1,0:T(8,128)S(1)} %get-tuple-element.86.refs_4_) | copy-start | bytes 2359300
  147.0 1.7 copy-start.8
  148.6 1.1 copy-start.34
  149.8 0.9 copy-start.44
  151.5 19.4 %copy-start.18 = (bf16[1536,256]{1,0:T(8,128)(2,1)S(1)}, bf16[1536,256]{1,0:T(8,128)(2,1)}, u32[]{:S(2)}) copy-start(bf16[1536,256]{1,0:T(8,128)(2,1)} %copy-done.17) | copy-start | bytes 2359300
  151.5 19.4 %copy-start.23 = (f32[1,768,256]{2,1,0:T(8,128)S(1)}, f32[1,768,256]{2,1,0:T(8,128)}, u32[]{:S(2)}) copy-start(f32[1,768,256]{2,1,0:T(8,128)} %copy-done.22) | copy-start | bytes 2359300
  151.5 19.4 %copy-start.25 = (f32[1,768,256]{2,1,0:T(8,128)S(1)}, f32[1,768,256]{2,1,0:T(8,128)}, u32[]{:S(2)}) copy-start(f32[1,768,256]{2,1,0:T(8,128)} %copy-done.24) | copy-start | bytes 2359300
  151.5 19.4 %copy-start.53 = (f32[96,256]{1,0:T(8,128)S(1)}, f32[96,256]{1,0:T(8,128)}, u32[]{:S(2)}) copy-start(f32[96,256]{1,0:T(8,128)} %copy-done.52) | copy-start | bytes 294916
  151.5 19.4 %copy-start.57 = (bf16[96,256]{1,0:T(8,128)(2,1)S(1)}, bf16[96,256]{1,0:T(8,128)(2,1)}, u32[]{:S(2)}) copy-start(bf16[96,256]{1,0:T(8,128)(2,1)} %copy-done.56) | copy-start | bytes 147460
  151.5 19.4 %copy-start.70 = (bf16[16,1536]{1,0:T(8,128)(2,1)S(1)}, bf16[16,1536]{1,0:T(8,128)(2,1)}, u32[]{:S(2)}) copy-start(bf16[16,1536]{1,0:T(8,128)(2,1)} %copy-done.69) | copy-start | bytes 147460
  155.5 0.9 copy-start.9
  156.3 12.1 %copy-start.62 = (bf16[96,256]{1,0:T(8,128)(2,1)}, bf16[96,256]{1,0:T(8,128)(2,1)S(1)}, u32[]{:S(2)}) copy-start(bf16[96,256]{1,0:T(8,128)(2,1)S(1)} %get-tuple-element.97.refs_6_) | copy-start | bytes 147460
  156.4 14.5 %copy-start.45 = (f32[96,256]{1,0:T(8,128)}, f32[96,256]{1,0:T(8,128)S(1)}, u32[]{:S(2)}) copy-start(f32[96,256]{1,0:T(8,128)S(1)} %get-tuple-element.98.refs_7_) | copy-start | bytes 294916
  170.8 5.4 %copy-start.28 = (f32[2,96,256]{2,1,0:T(8,128)S(1)}, f32[2,96,256]{2,1,0:T(8,128)}, u32[]{:S(2)}) copy-start(f32[2,96,256]{2,1,0:T(8,128)} %copy-done.26) | copy-start | bytes 589828
  170.8 5.4 %copy-start.67 = (f32[2,96,256]{2,1,0:T(8,128)S(1)}, f32[2,96,256]{2,1,0:T(8,128)}, u32[]{:S(2)}) copy-start(f32[2,96,256]{2,1,0:T(8,128)} %copy-done.66) | copy-start | bytes 589828
  170.8 5.4 %copy-start.74 = (bf16[2,96,256]{2,1,0:T(8,128)(2,1)S(1)}, bf16[2,96,256]{2,1,0:T(8,128)(2,1)}, u32[]{:S(2)}) copy-start(bf16[2,96,256]{2,1,0:T(8,128)(2,1)} %copy-done.73) | copy-start | bytes 294916
  170.8 5.4 %copy-start.79 = (bf16[1,1,96,256]{3,2,1,0:T(8,128)(2,1)S(1)}, bf16[1,1,96,256]{3,2,1,0:T(8,128)(2,1)}, u32[]{:S(2)}) copy-start(bf16[1,1,96,256]{3,2,1,0:T(8,128)(2,1)} %x_ref.2) | copy-start | bytes 147460
  176.2 14.1 %copy-start.4 = (bf16[768,2304]{1,0:T(8,128)(2,1)S(1)}, bf16[768,2304]{1,0:T(8,128)(2,1)}, u32[]{:S(2)}) copy-start(bf16[768,2304]{1,0:T(8,128)(2,1)} %all-gather.7.cloned.1.call-done.pack_ref.refs_2_) | copy-start | bytes 10616836
  177.5 26.4 %all-to-all-start = ((bf16[8,96,256]{2,1,0:T(8,128)(2,1)}), bf16[8,96,256]{2,1,0:T(8,128)(2,1)}, u32[]{:S(2)}, u32[]{:S(2)}) async-start(bf16[8,96,256]{2,1,0:T(8,128)(2,1)} %copy-done.49), calls=%async_computation | async-start | bytes 786432 | tf_op jit(solution)/shard_map/all_to_all | solution.py:500
  190.4 1.1 copy-start.10
  191.5 1.1 copy-start.36
  192.6 1.1 copy-start.38
  193.8 0.9 copy-start.46
  194.6 0.8 copy-start.63
  199.4 0.9 copy-start.11
  203.9 1.1 copy-start.12
  205.0 0.9 copy-start.29
  206.0 0.9 copy-start.48
  207.6 0.9 copy-start.68
  209.4 0.9 copy-start.75
  (22 other events, 15.4 us)
Sparse Core Ops, SparseCore 0:
  15.5 60.3 all-gather.4
  77.9 53.7 all-gather.6

commit v4 on v3

v4 whole, which is shorter than its diff:
```python
import functools

import jax
import jax.numpy as jnp
from jax import lax
from jax.experimental import pallas as pl
from jax.experimental.pallas import tpu as pltpu
from jax.sharding import PartitionSpec as P

GS = 48
WW = 64
NORM_EPS = 1e-05
TAIL = 512
F32 = jnp.float32
BF16 = jnp.bfloat16
VMEM = pl.BlockSpec(memory_space=pltpu.VMEM)
SMEM = pl.BlockSpec(memory_space=pltpu.SMEM)
ANY = pl.BlockSpec(memory_space=pl.ANY)
NT = (((1,), (1,)), ((), ()))
TN = (((0,), (0,)), ((), ()))


def vmem(mebibytes):
    return pltpu.CompilerParams(vmem_limit_bytes=mebibytes * 1024 * 1024)


def shape_of(shape, dtype):
    return jax.ShapeDtypeStruct(shape, dtype)


def total(block):
    return jnp.sum(jnp.sum(block, axis=1, keepdims=True), axis=0, keepdims=True)


def norm_group(h, gain, bias):
    scale = 1.0 / (h.shape[0] * h.shape[1])
    pre = h.astype(F32)
    pre = pre - total(pre) * scale
    inv_std = lax.rsqrt(total(pre * pre) * scale + NORM_EPS)
    xhat = pre * inv_std
    n = xhat * gain + bias
    sig = jax.nn.sigmoid(n)
    slope = sig * (1.0 + n * (1.0 - sig))
    return xhat, n, sig, slope, inv_std


def column(line):
    count = line.shape[1]
    down = lax.broadcasted_iota(jnp.int32, (count, count), 0)
    across = lax.broadcasted_iota(jnp.int32, (count, count), 1)
    return jnp.sum(jnp.where(down == across, line, 0.0), axis=1, keepdims=True)


def prepare_kernel(*refs):
    pack_refs = (refs[6], refs[7])
    xhat_ref, slope_ref, rate_ref, act_ref = refs[8:12]
    w_ref, wc_ref, h1_ref, h2_ref, gain_ref, bias_ref, sems = refs[12:]
    copies = [
        pltpu.make_async_copy(refs[i], refs[12 + i], sems.at[i]) for i in range(6)
    ]
    for copy in copies:
        copy.start()
    for copy in copies:
        copy.wait()
    chans, width = w_ref.shape[2:]
    taps = wc_ref.shape[3]
    lane = lax.broadcasted_iota(jnp.int32, (chans, TAIL - 384), 1)
    for b, h_ref in ((1, h2_ref), (0, h1_ref)):
        pack_ref = pack_refs[b]
        pack_ref[:, :width] = w_ref[0, b]
        pack_ref[:, width : width + 384] = wc_ref[0, b, :, :384]
        last = wc_ref[0, b, :, 384:].astype(F32)
        last = jnp.concatenate(
            [last, jnp.zeros((chans, TAIL - taps), F32)], axis=1
        )
        gain = column(gain_ref[0, b : b + 1, :])
        bias = column(bias_ref[0, b : b + 1, :])
        at = taps - 384
        for whole in (gain, bias):
            rest = whole
            for _ in range(3):
                piece = rest.astype(BF16).astype(F32)
                rest = rest - piece
                last = jnp.where(lane == at, piece, last)
                at += 1
        pack_ref[:, width + 384 : width + TAIL] = last.astype(BF16)
        pack_ref[:, width + TAIL :] = h_ref[0, 0]
        for q in range(0, chans, GS):
            rows = slice(q, q + GS)
            xhat, n, sig, slope, inv_std = norm_group(
                h_ref[0, 0, rows, :], gain[rows], bias[rows]
            )
            xhat_ref[b, rows, :] = xhat
            slope_ref[b, rows, :] = slope
            rate_ref[b, rows, :] = slope * (gain[rows] * inv_std)
            act_ref[b, rows, :] = (n * sig).astype(BF16)


def prepare(*operands):
    chans, width = operands[0].shape[2:]
    positions = operands[2].shape[3]
    full = shape_of((2, chans, positions), F32)
    pack = shape_of((chans, width + TAIL + positions), BF16)
    return pl.pallas_call(
        prepare_kernel,
        out_shape=(pack, pack, full, full, full, shape_of((2, chans, positions), BF16)),
        in_specs=[pl.BlockSpec(memory_space=pltpu.HBM)] * 6,
        out_specs=[VMEM] * 6,
        scratch_shapes=[pltpu.VMEM(x.shape, x.dtype) for x in operands]
        + [pltpu.SemaphoreType.DMA((6,))],
        compiler_params=vmem(56),
        name="prepare",
    )(*operands)


def shifted(value, step_row, step_col, row, col):
    length = value.shape[1]
    rows = length // WW
    by = step_row * WW + step_col
    if by == 0:
        return value
    moved = pltpu.roll(value, (-by) % length, axis=1)
    inside = None
    if step_row:
        inside = row < rows - 1 if step_row > 0 else row > 0
    if step_col:
        here = col < WW - 1 if step_col > 0 else col > 0
        inside = here if inside is None else inside & here
    return jnp.where(inside, moved, 0.0)


def grid_of(shape):
    lane = lax.broadcasted_iota(jnp.int32, shape, 1)
    return lane // WW, lane % WW


def own_positions(g, chan_at, count):
    down = lax.broadcasted_iota(jnp.int32, (count, g.shape[1]), 0)
    across = lax.broadcasted_iota(jnp.int32, (count, g.shape[1]), 1)
    pick = jnp.where(across == down + chan_at * count, 1.0, 0.0).astype(BF16)
    return lax.dot_general(pick, g, NT, preferred_element_type=F32).astype(BF16)


def block(b, mode, flags, g, ordered, own_rows, params, state):
    whole, positions = g.shape
    per = whole // 2 // own_rows
    chans = own_rows if mode == "own" else per * own_rows
    width = whole
    scale = 1.0 / (GS * positions)
    at_b = b if mode == "own" else 0

    def kernel(*refs):
        refs = list(refs)
        take = lambda k: [refs.pop(0) for _ in range(k)]
        flags_ref, g_ref = take(2)
        weights = take(len(params))
        state_refs = take(0 if mode == "first" else 2)
        out_ref, gh_ref, ga_ref = take(3)
        if mode == "first":
            xhat_ref, rate_ref = take(2)
            w_ref, taps_ref, h_ref, sems = take(4)
            (pack_ref,) = weights
            loads = [
                pltpu.make_async_copy(pack_ref.at[:, at : at + n], to, sems.at[i])
                for i, (at, n, to) in enumerate(
                    (
                        (width + TAIL, positions, h_ref),
                        (width, TAIL, taps_ref),
                        (0, width, w_ref),
                    )
                )
            ]
            for load in loads:
                load.start()
        else:
            xhat_ref, rate_ref = state_refs
        (g_buf,) = refs
        chan_at = flags_ref[1]
        core = chan_at & 1
        if ordered:
            src = g_ref
        else:
            for c in range(2):
                for y in range(per):
                    to = (2 * y + c) * own_rows
                    at = (c * per + y) * own_rows
                    g_buf[to : to + own_rows, :] = g_ref[at : at + own_rows, :]
            src = g_buf

        if mode == "first":
            loads[0].wait()
            loads[1].wait()
            at = 9 * GS - 384
            for q in range(0, chans, GS):
                rows = slice(q, q + GS)
                side = taps_ref[rows, 384:].astype(F32)
                gain, bias = (
                    side[:, i : i + 1] + side[:, i + 1 : i + 2] + side[:, i + 2 : i + 3]
                    for i in (at, at + 3)
                )
                xhat, _, _, slope, inv_std = norm_group(h_ref[rows, :], gain, bias)
                xhat_ref[0, rows, :] = xhat
                rate_ref[0, rows, :] = slope * (gain * inv_std)
            loads[2].wait()
            matrix = w_ref[...]
        elif mode == "wide":
            (pack_ref,) = weights
            matrix = pack_ref[:, :width]
        else:
            matrix = weights[0][0, b]
        ga_ref[...] = jnp.dot(matrix, src[...], preferred_element_type=F32)
        row, col = grid_of((GS, positions))
        for at in range(0, chans, GS):
            y, q = divmod(at, own_rows)
            rows = slice(at, at + GS)
            if mode == "first":
                taps_w = taps_ref[rows, : 9 * GS]
            elif mode == "wide":
                taps_w = pack_ref[rows, width : width + 9 * GS]
            else:
                taps_w = weights[1][0, b, rows, :]
            mine_at = (chan_at if mode == "own" else 2 * y + core) * own_rows + q
            xhat = xhat_ref[at_b, rows, :]
            rw = ga_ref[rows, :] * rate_ref[at_b, rows, :]
            gh = rw - total(rw) * scale - xhat * (total(rw * xhat) * scale)
            gh = gh.astype(BF16)
            gh_ref[rows, :] = gh
            spread = lax.dot_general(taps_w, gh, TN, preferred_element_type=F32)
            branch = None
            for step_col in (-1, 0, 1):
                part = None
                for step_row in (-1, 0, 1):
                    tap = 3 * (step_row + 1) + step_col + 1
                    term = shifted(spread[tap * GS : (tap + 1) * GS, :], -step_row, 0, row, col)
                    part = term if part is None else part + term
                part = shifted(part, 0, -step_col, row, col)
                branch = part if branch is None else branch + part
            mine = src[pl.ds(pl.multiple_of(mine_at, GS), GS), :].astype(F32)
            out_ref[rows, :] = (mine + branch.astype(BF16).astype(F32)).astype(BF16)

    shapes = [
        shape_of((chans, positions), BF16),
        shape_of((chans, positions), BF16),
        shape_of((chans, positions), F32),
    ]
    scratch = []
    if mode == "first":
        shapes += [shape_of((1, chans, positions), F32)] * 2
        scratch += [
            pltpu.VMEM((chans, width), BF16),
            pltpu.VMEM((chans, TAIL), BF16),
            pltpu.VMEM((chans, positions), BF16),
            pltpu.SemaphoreType.DMA((3,)),
        ]
    scratch.append(pltpu.VMEM((16, 128) if ordered else (whole, positions), BF16))
    operands = [flags, g, *params, *(() if mode == "first" else state)]
    in_specs = [SMEM] + [VMEM] * (len(operands) - 1)
    if mode == "first":
        in_specs[2] = ANY
    result = pl.pallas_call(
        kernel,
        out_shape=shapes,
        in_specs=in_specs,
        out_specs=[VMEM] * len(shapes),
        scratch_shapes=scratch,
        compiler_params=vmem({"own": 6, "wide": 14, "first": 56}[mode]),
        name=mode + "_block",
    )(*operands)
    return result[:3], tuple(result[3:]) if mode == "first" else state


def weight_blocks(b, act_ref, xhat_ref, slope_ref, x_ref, saved_refs, stack, store):
    g, gh_ref, ga_ref = saved_refs
    chans, positions = x_ref.shape[2:]
    width = g.shape[0]
    row, col = grid_of((GS, positions))
    lane = lax.broadcasted_iota(jnp.int32, (GS, TAIL), 1)
    stack[9 * GS :, :] = jnp.zeros((TAIL - 9 * GS, positions), BF16)
    store(
        slice(0, chans),
        0,
        lax.dot_general(act_ref[b], g, NT, preferred_element_type=F32).astype(BF16),
    )
    for q in range(0, chans, GS):
        rows = slice(q, q + GS)
        x = x_ref[0, 0, rows, :].astype(F32)
        for step_row in (-1, 0, 1):
            for step_col in (-1, 0, 1):
                tap = 3 * (step_row + 1) + step_col + 1
                stack[tap * GS : (tap + 1) * GS, :] = shifted(
                    x, step_row, step_col, row, col
                ).astype(BF16)
        taps = lax.dot_general(gh_ref[rows, :], stack[...], NT, preferred_element_type=F32)
        gn = ga_ref[rows, :] * slope_ref[b, rows, :]
        by_gain = jnp.sum(gn * xhat_ref[b, rows, :], axis=1, keepdims=True)
        by_bias = jnp.sum(gn, axis=1, keepdims=True)
        taps = jnp.where(lane == 9 * GS, by_gain, taps)
        taps = jnp.where(lane == 9 * GS + 1, by_bias, taps)
        store(rows, width, taps.astype(BF16))


def storer(out_ref, first_row):
    step = out_ref.shape[2]

    def store(rows, at, value):
        to = slice(first_row + rows.start, first_row + rows.stop)
        for i in range(value.shape[1] // step):
            out_ref[at // step + i, to, :] = value[:, i * step : (i + 1) * step]

    return store


def summed(in_ref, rows):
    acc = in_ref[0, rows, :].astype(F32)
    for m in range(1, in_ref.shape[0]):
        acc = acc + in_ref[m, rows, :].astype(F32)
    return acc.astype(BF16)


def weight_grads(flags, orders, kept, latents, act, xhat, slope, inputs):
    ticks = len(latents)
    chans, positions = act.shape[1:]
    width = kept[0][0][0].shape[0]
    shards = width // chans
    slab = positions // shards
    members = lax.axis_size("dp")
    step = (width + TAIL) // members
    pairs = shards // 2

    def split(g, in_order):
        return g.reshape((pairs, 2, chans, positions) if in_order else (2, pairs, chans, positions))

    operands = []
    for b in range(2):
        for t in range(ticks):
            g, gh, ga = kept[b][t]
            operands += [split(g, orders[b][t]), gh, ga]
    operands += [split(g, in_order) for in_order, g in latents]

    def kernel(*refs):
        refs = list(refs)
        take = lambda k: [refs.pop(0) for _ in range(k)]
        (flags_ref,) = take(1)
        fetched = take(len(operands))
        act_ref, xhat_ref, slope_ref, *x_refs = take(5)
        out_ref, lat_ref, stack, g_bufs, gh_bufs, ga_bufs, sems = refs
        segment_at, chan_at = flags_ref[0], flags_ref[1]

        def copies(t):
            made = []

            def put(src, to):
                made.append(pltpu.make_async_copy(src, to, sems.at[len(made)]))

            for b in range(2):
                g, gh, ga = fetched[3 * (ticks * b + t) :][:3]
                for c in range(2):
                    put(g.at[:, c] if orders[b][t] else g.at[c], g_bufs.at[b, :, c])
                at = 0
                if gh.shape[0] > chans:
                    at = pl.multiple_of((chan_at >> 1) * chans, chans)
                put(gh.at[pl.ds(at, chans)], gh_bufs.at[b])
                put(ga.at[pl.ds(at, chans)], ga_bufs.at[b])
            g = fetched[6 * ticks + t]
            for c in range(2):
                put(g.at[:, c] if latents[t][0] else g.at[c], g_bufs.at[2, :, c])
            return made

        for t in range(ticks):

            @pl.when(segment_at == ticks - 1 - t)
            def _():
                for copy in copies(t):
                    copy.start()
                for copy in copies(t):
                    copy.wait()

        whole = lambda i: g_bufs[i].reshape(width, positions)
        for b in range(2):
            weight_blocks(
                b, act_ref, xhat_ref, slope_ref, x_refs[b],
                (whole(b), gh_bufs.at[b], ga_bufs.at[b]), stack, storer(out_ref, b * chans),
            )
        lat_ref[...] = own_positions(whole(2), chan_at, slab)

    return pl.pallas_call(
        kernel,
        out_shape=(
            shape_of((members, 2 * chans, step), BF16),
            shape_of((slab, width), BF16),
        ),
        in_specs=[SMEM] + [ANY] * len(operands) + [VMEM] * 5,
        out_specs=[VMEM] * 2,
        scratch_shapes=[
            pltpu.VMEM((TAIL, positions), BF16),
            pltpu.VMEM((3, pairs, 2, chans, positions), BF16),
            pltpu.VMEM((2, chans, positions), BF16),
            pltpu.VMEM((2, chans, positions), F32),
            pltpu.SemaphoreType.DMA((10,)),
        ],
        compiler_params=vmem(56),
        name="weight_grads",
    )(flags, *operands, act, xhat, slope, *inputs)


def sum_kernel(in_ref, out_ref):
    done = summed(in_ref, slice(0, out_ref.shape[1]))
    for m in range(out_ref.shape[0]):
        out_ref[m] = done


def spread_sums(parts):
    return pl.pallas_call(
        sum_kernel,
        out_shape=shape_of(parts.shape, BF16),
        in_specs=[VMEM],
        out_specs=VMEM,
        compiler_params=vmem(6),
        name="sum_microbatches",
    )(parts)


def widen_kernel(in_ref, proj_ref, conv_ref, gain_ref, bias_ref):
    chans, width = proj_ref.shape[2:]
    step = in_ref.shape[2]
    down = lax.broadcasted_iota(jnp.int32, (chans, chans), 0)
    across = lax.broadcasted_iota(jnp.int32, (chans, chans), 1)
    first = width // step
    for b in range(2):
        rows = slice(b * chans, (b + 1) * chans)
        for i in range(first):
            proj_ref[0, b, :, i * step : (i + 1) * step] = in_ref[i, rows, :].astype(F32)
        conv_ref[0, b, :, :step] = in_ref[first, rows, :].astype(F32)
        side = in_ref[first + 1, rows, :].astype(F32)
        conv_ref[0, b, :, step:] = side[:, : 9 * GS - step]
        for i, to in enumerate((gain_ref, bias_ref)):
            at = 9 * GS - step + i
            lined = jnp.where(down == across, side[:, at : at + 1], 0.0)
            to[0, b : b + 1, :] = jnp.sum(lined, axis=0, keepdims=True)


def widen(sums, width):
    chans = sums.shape[1] // 2
    return pl.pallas_call(
        widen_kernel,
        out_shape=(
            shape_of((1, 2, chans, width), F32),
            shape_of((1, 2, chans, 9 * GS), F32),
            shape_of((1, 2, chans), F32),
            shape_of((1, 2, chans), F32),
        ),
        in_specs=[VMEM],
        out_specs=[VMEM] * 4,
        compiler_params=vmem(8),
        name="widen",
    )(sums)


def gather(block_, axis, groups=None):
    return lax.all_gather(block_, axis, axis=0, tiled=True, axis_index_groups=groups)


def per_device(
    grad_top,
    inputs_one,
    conv_one,
    inputs_two,
    conv_two,
    proj_weight,
    conv_weight,
    norm_gain,
    norm_bias,
):
    segments = lax.axis_size("segment")
    segment_at = lax.axis_index("segment")
    chan_at = lax.axis_index("chan")
    members = lax.axis_size("dp")
    shards = lax.axis_size("chan")
    chans, positions = conv_one.shape[2:]
    width = proj_weight.shape[3]
    cores = [[2 * y, 2 * y + 1] for y in range(shards // 2)]
    columns = [[2 * y + c for y in range(shards // 2)] for c in range(2)]

    def exchange(blocks):
        return lax.all_to_all(blocks, "dp", split_axis=0, concat_axis=0, tiled=True)

    first_pack, second_pack, xhat, slope, rate, act = prepare(
        proj_weight, conv_weight, conv_one, conv_two, norm_gain, norm_bias
    )
    packs = [None, gather(second_pack, "chan", columns)]
    packs[0] = lax.all_gather(
        first_pack[None], "chan", axis=1, tiled=True, axis_index_groups=columns
    )[0]
    own = (proj_weight, conv_weight)
    states = [None, None]
    kept = [[], []]
    orders = [[], []]
    latents = []
    flags = jnp.stack([segment_at.astype(jnp.int32), chan_at.astype(jnp.int32)])
    for tick in range(segments):
        if tick == 0:
            g = lax.all_gather(grad_top[0], "chan", axis=1, tiled=True)
            ordered = True
        else:
            lower = segments - 1 - tick
            rest = [s for s in range(segments) if s not in (lower, lower + 1)]
            groups = sorted(
                [[lower, lower + 1]] + [rest[i : i + 2] for i in range(0, len(rest), 2)]
            )
            ordered = out.shape[0] == chans
            moved = gather(out, "segment", groups)[out.shape[0] :]
            g = gather(moved, "chan", None if ordered else cores)
            latents.append((ordered, g))
        for b in (1, 0):
            if tick > 1 or (tick == 1 and b == 1):
                mode = "wide" if states[b] is not None else "first"
            else:
                mode = "own"
            if mode == "first":
                packs[b], g = lax.optimization_barrier((packs[b], g))
            (out, gh, ga), state = block(
                b,
                mode,
                flags,
                g,
                ordered,
                chans,
                own if mode == "own" else (packs[b],),
                (xhat, rate) if mode == "own" else states[b],
            )
            if mode != "own":
                states[b] = state
            kept[b].append((g, gh, ga))
            orders[b].append(ordered)
            if b == 1 or tick == segments - 1:
                ordered = out.shape[0] == chans
                g = gather(out, "chan", None if ordered else cores)
    latents.append((ordered, g))

    parts, latent = weight_grads(
        flags, orders, kept, latents, act, xhat, slope, (inputs_one, inputs_two)
    )
    sums = exchange(spread_sums(exchange(parts)))
    proj, conv, by_gain, by_bias = widen(sums, width)
    return latent.T[None, None], proj, conv, by_gain, by_bias


def solution(mesh):
    return jax.shard_map(
        per_device,
        mesh=mesh,
        in_specs=(
            P("dp", None, "chan"),
            P("segment", "dp", "chan", None),
            P("segment", "dp", "chan", None),
            P("segment", "dp", "chan", None),
            P("segment", "dp", "chan", None),
            P("segment", None, "chan", None),
            P("segment", None, "chan", None),
            P("segment", None, "chan"),
            P("segment", None, "chan"),
        ),
        out_specs=(
            P("segment", "dp", None, "chan"),
            P("segment", None, "chan", None),
            P("segment", None, "chan", None),
            P("segment", None, "chan"),
            P("segment", None, "chan"),
        ),
        check_vma=False,
    )
```

time: 270 us -> 247 us (0.915)
  local copies, waits for them, and re-layouts: 43.5 us -> 12.6 us
  blocking collectives: 163 us -> 175 us
  starting transfers between devices: 10.4 us -> 0.08 us
  Pallas kernels: 35.2 us -> 44 us
    unnamed x166 -> x76, local copies, waits for them, and re-layouts: 43.2 us -> 12.3 us
    all_to_all x2, blocking collectives: 46.7 us -> 58.1 us  [exchange(): return lax.all_to_all(blocks, 'dp', split_axis=0, concat_axis=0, tiled=True)]
    all_to_all x1 -> x0, starting transfers between devices: 10.3 us -> none  [exchange(): return lax.all_to_all(blocks, 'dp', split_axis=0, concat_axis=0, tiled=True)]
    pallas_call x13 -> x10, Pallas kernels: 32.2 us -> 40.2 us  [the longest x8 35.3 us: block(): pl.pallas_call(kernel, out_shape=shapes, in_specs=in_specs, out_specs=[VM...]
  transfers between devices with their start and end apart: 3 -> 2, of which waited for: 0 -> 0; matrix products, arithmetic and copies ran while one was open for 0% -> 0% of each run, Pallas kernels for 7% -> 7%
where the time goes in v4:
time: 247 us
  blocking collectives  175 us (71%)
  Pallas kernels  44 us (18%)
  between operations  14.4 us (6%)
  local copies, waits for them, and re-layouts  12.6 us (5%)
    all_gather x11, blocking collectives, gather(): lax.all_gather(block_, axis, axis=0, tiled=True, axis_index_groups=groups)  96.5 us
    all_to_all x2, blocking collectives, exchange(): return lax.all_to_all(blocks, 'dp', split_axis=0, concat_axis=0, tiled=True)  58.1 us
    pallas_call x8, Pallas kernels, block(): pl.pallas_call(kernel, out_shape=shapes, in_specs=in_specs, out_specs=[VM...  35.3 us
    all_gather x1, blocking collectives, per_device(): g = lax.all_gather(grad_top[0], 'chan', axis=1, tiled=True)  20 us
    unnamed x76, local copies, waits for them, and re-layouts  12.3 us
  transfers between devices with their start and end apart: 2, of which 0 were waited for; matrix products, arithmetic and copies ran while one was open for 0% of the time, Pallas kernels for 7%

profile of v4, /device:TPU:6, one launch (start us, length us, event | category | flops | bytes accessed | tf_op | source)
XLA Modules:
  0.0 246.5 jit_solution(16769697248672334338)
XLA Ops:
  7.2 0.0 copy-start.16
  7.2 0.0 copy-start.4
  7.2 0.0 all-gather.5.cloned.1.call-start
  7.2 2.7 %prepare.1 = (bf16[96,2304]{1,0:T(8,128)(2,1)}, bf16[96,2304]{1,0:T(8,128)(2,1)}, f32[2,96,256]{2,1,0:T(8,128)}, f32[2,96,256]{2,1,0:T(8,128)}, f32[2,96,256]{2,1,0:T(8,128)}, /*index=5*/bf16[2,96,256]{2,1,0:T(8,128)(2,1)}) custom-call(bf16[1,2,96,1536]{3,2,1,0:T(8,128)(2,1)} %refs_2_.7, bf16[1,2,96,432]{3,2,1,0:T(8,128)(2,1)} %refs_3_.7, ...), custom_call_target="tpu_custom_call" | custom-call | tf_op jit(solution)/shard_map/prepare/pallas_call | solution.py:104
  9.9 0.0 all-gather.5.cloned.1.call-update
  9.9 0.0 all-gather.7.cloned.1.call-start
  10.0 0.7 all-gather.7.cloned.1.call-update
  10.7 20.0 %all-gather = bf16[1,1536,256]{1,2,0:T(8,128)(2,1)S(1)} all-gather(bf16[1,1536,16]{1,2,0:T(8,128)(2,1)} %param.9), channel_id=2, replica_groups=mesh['segment'=4,'chan'=16,'dp'=8] {'chan'}, dimensions={2}, use_global_device_ids=true | all-gather | bytes 835584 | tf_op jit(solution)/shard_map/all_gather | solution.py:502
  30.7 0.3 copy.15
  31.0 0.0 copy-start.6
  31.0 0.1 pad_add_fusion.refs_0_
  31.1 0.0 copy-done.16
  31.1 0.0 copy-done.4
  31.1 1.1 copy-done.10
  32.2 0.9 copy-done.18
  33.1 1.5 own_block.3
  34.6 0.6 copy-done.31
  35.2 21.6 %all_gather.43.refs_1_ = bf16[1536,256]{1,0:T(8,128)(2,1)S(1)} all-gather(bf16[96,256]{1,0:T(8,128)(2,1)S(1)} %get-tuple-element.51), channel_id=1, replica_groups=mesh['segment'=4,'chan'=16,'dp'=8] {'chan'}, dimensions={0}, use_global_device_ids=true | all-gather | bytes 835584 | tf_op jit(solution)/shard_map/all_gather | solution.py:460
  56.8 1.5 own_block.4
  58.3 0.6 copy-done.29
  58.9 0.6 copy-done.32
  59.5 4.8 %all_gather.45 = bf16[192,256]{1,0:T(8,128)(2,1)S(1)} all-gather(bf16[96,256]{1,0:T(8,128)(2,1)S(1)} %get-tuple-element.55), channel_id=1, replica_groups={{0,128},{256,384},{1,129},{257,385},{2,130},{258,386},{3,131},{259,387}..., dimensions={0}, use_global_device_ids=true | all-gather | bytes 147456 | tf_op jit(solution)/shard_map/all_gather | solution.py:460
  64.3 19.2 %all_gather.46.refs_1_ = bf16[1536,256]{1,0:T(8,128)(2,1)} all-gather(bf16[96,256]{1,0:T(8,128)(2,1)S(1)} %slice.12), channel_id=1, replica_groups=mesh['segment'=4,'chan'=16,'dp'=8] {'chan'}, dimensions={0}, use_global_device_ids=true | all-gather | bytes 835584 | tf_op jit(solution)/shard_map/all_gather | solution.py:460
  83.5 0.0 copy-done.6
  83.5 9.7 %first_block.2 = (bf16[768,256]{1,0:T(8,128)(2,1)}, bf16[768,256]{1,0:T(8,128)(2,1)}, f32[768,256]{1,0:T(8,128)}, f32[1,768,256]{2,1,0:T(8,128)}, f32[1,768,256]{2,1,0:T(8,128)}) custom-call(s32[2]{0:T(128)} %copy-done.34, bf16[1536,256]{1,0:T(8,128)(2,1)} %all_gather.46.refs_1_, bf16[768,2304]{1,0:T(8,128)(2,1)} %all-gather.5.cloned.1.call-done.refs_2_), custom_call_target="tpu_custom_call" | custom-call | tf_op jit(solution)/shard_map/first_block/pallas_call | solution.py:260
  93.3 0.0 copy-start.36
  93.3 2.7 %all_gather.47.refs_1_ = bf16[1536,256]{1,0:T(8,128)(2,1)S(1)} all-gather(bf16[768,256]{1,0:T(8,128)(2,1)} %get-tuple-element.58), channel_id=1, replica_groups={{0,8},{16,24},{32,40},{48,56},{64,72},{80,88},{96,104},{112,120},{1,9},..., dimensions={0}, use_global_device_ids=true | all-gather | bytes 1179648 | tf_op jit(solution)/shard_map/all_gather | solution.py:460
  96.0 1.1 copy-done.5
  97.1 0.9 copy-done.11
  98.0 0.9 copy-done.17
  98.9 0.9 copy-done.19
  99.9 0.7 copy-done.35
  100.5 1.5 own_block.5
  102.0 0.6 copy-done.30
  102.6 0.6 copy-done.33
  103.3 6.0 %all_gather.49 = bf16[192,256]{1,0:T(8,128)(2,1)S(1)} all-gather(bf16[96,256]{1,0:T(8,128)(2,1)S(1)} %get-tuple-element.62), channel_id=1, replica_groups={{0,384},{128,256},{1,385},{129,257},{2,386},{130,258},{3,387},{131,259}..., dimensions={0}, use_global_device_ids=true | all-gather | bytes 147456 | tf_op jit(solution)/shard_map/all_gather | solution.py:460
  109.3 20.1 %all_gather.50.refs_1_ = bf16[1536,256]{1,0:T(8,128)(2,1)S(1)} all-gather(bf16[96,256]{1,0:T(8,128)(2,1)S(1)} %slice.13), channel_id=1, replica_groups=mesh['segment'=4,'chan'=16,'dp'=8] {'chan'}, dimensions={0}, use_global_device_ids=true | all-gather | bytes 835584 | tf_op jit(solution)/shard_map/all_gather | solution.py:460
  129.4 0.0 copy-done.14
  129.4 3.9 %wide_block.3 = (bf16[768,256]{1,0:T(8,128)(2,1)S(1)}, bf16[768,256]{1,0:T(8,128)(2,1)S(1)}, f32[768,256]{1,0:T(8,128)S(1)}) custom-call(s32[2]{0:T(128)S(1)} %copy-done.36, bf16[1536,256]{1,0:T(8,128)(2,1)S(1)} %all_gather.50.refs_1_, bf16[768,2304]{1,0:T(8,128)(2,1)S(1)} %copy-done, f32[1,768,256]{2,1,0:T(8,128)S(1)} %copy-done.12, ...), custom_call_target="tpu_custom_call" | custom-call | tf_op jit(solution)/shard_map/wide_block/pallas_call | solution.py:260
  133.3 0.9 copy-done.2
  134.2 0.9 copy-done.20
  135.1 0.7 copy-done.25
  135.8 2.7 %all_gather.51.refs_1_ = bf16[1536,256]{1,0:T(8,128)(2,1)} all-gather(bf16[768,256]{1,0:T(8,128)(2,1)S(1)} %get-tuple-element.65), channel_id=1, replica_groups={{0,8},{16,24},{32,40},{48,56},{64,72},{80,88},{96,104},{112,120},{1,9},..., dimensions={0}, use_global_device_ids=true | all-gather | bytes 1179648 | tf_op jit(solution)/shard_map/all_gather | solution.py:460
  138.5 9.6 %first_block.3 = (bf16[768,256]{1,0:T(8,128)(2,1)}, bf16[768,256]{1,0:T(8,128)(2,1)}, f32[768,256]{1,0:T(8,128)}, f32[1,768,256]{2,1,0:T(8,128)}, f32[1,768,256]{2,1,0:T(8,128)}) custom-call(s32[2]{0:T(128)} %copy-done.34, bf16[1536,256]{1,0:T(8,128)(2,1)} %all_gather.51.refs_1_, bf16[768,2304]{1,0:T(8,128)(2,1)} %all-gather.7.cloned.1.call-done.refs_2_), custom_call_target="tpu_custom_call" | custom-call | tf_op jit(solution)/shard_map/first_block/pallas_call | solution.py:260
  148.1 12.3 %all_gather.52 = bf16[1536,256]{1,0:T(8,128)(2,1)S(1)} all-gather(bf16[768,256]{1,0:T(8,128)(2,1)} %get-tuple-element.70), channel_id=1, replica_groups={{0,128},{256,384},{1,129},{257,385},{2,130},{258,386},{3,131},{259,387}..., dimensions={0}, use_global_device_ids=true | all-gather | bytes 1179648 | tf_op jit(solution)/shard_map/all_gather | solution.py:460
  160.4 2.4 all_gather.53.refs_1_
  162.8 0.0 copy-start.3
  162.8 0.0 copy-start.1
  162.8 0.0 copy-start.23
  162.8 0.0 copy-start.24
  162.8 3.9 %wide_block.4 = (bf16[768,256]{1,0:T(8,128)(2,1)S(1)}, bf16[768,256]{1,0:T(8,128)(2,1)S(1)}, f32[768,256]{1,0:T(8,128)S(1)}) custom-call(s32[2]{0:T(128)S(1)} %copy-done.37, bf16[1536,256]{1,0:T(8,128)(2,1)S(1)} %all_gather.53.refs_1_, bf16[768,2304]{1,0:T(8,128)(2,1)S(1)} %copy-done, f32[1,768,256]{2,1,0:T(8,128)S(1)} %copy-done.13, ...), custom_call_target="tpu_custom_call" | custom-call | tf_op jit(solution)/shard_map/wide_block/pallas_call | solution.py:260
  166.7 2.4 all_gather.54.refs_1_
  169.1 0.0 copy-done.21
  169.1 0.0 copy-done.23
  169.1 0.0 copy-done.24
  169.1 3.9 %wide_block.5 = (bf16[768,256]{1,0:T(8,128)(2,1)S(1)}, bf16[768,256]{1,0:T(8,128)(2,1)S(1)}, f32[768,256]{1,0:T(8,128)S(1)}) custom-call(s32[2]{0:T(128)S(1)} %copy-done.37, bf16[1536,256]{1,0:T(8,128)(2,1)S(1)} %all_gather.54.refs_1_, bf16[768,2304]{1,0:T(8,128)(2,1)S(1)} %copy-done.1, f32[1,768,256]{2,1,0:T(8,128)S(1)} %copy-done.23, ...), custom_call_target="tpu_custom_call" | custom-call | tf_op jit(solution)/shard_map/wide_block/pallas_call | solution.py:260
  173.0 0.0 copy-start.27
  173.1 2.5 %all_gather.55 = bf16[1536,256]{1,0:T(8,128)(2,1)} all-gather(bf16[768,256]{1,0:T(8,128)(2,1)S(1)} %get-tuple-element.84), channel_id=1, replica_groups={{0,8},{16,24},{32,40},{48,56},{64,72},{80,88},{96,104},{112,120},{1,9},..., dimensions={0}, use_global_device_ids=true | all-gather | bytes 1179648 | tf_op jit(solution)/shard_map/all_gather | solution.py:460
  175.6 0.0 copy-done.27
  175.6 4.7 %weight_grads.1 = (bf16[8,192,256]{2,1,0:T(8,128)(2,1)}, bf16[16,1536]{1,0:T(8,128)(2,1)}) custom-call(s32[2]{0:T(128)} %copy-done.34, bf16[8,2,96,256]{3,2,1,0:T(8,128)(2,1)} %bitcast.22, bf16[96,256]{1,0:T(8,128)(2,1)} %copy-done.32, f32[96,256]{1,0:T(8,128)} %copy-done.29, bf16[2,8,96,256]{3,2,1,0:T(8,128)(2,1)} %bitcast.23, bf16[96,256]{1,0:T(8,128)(2,1)} %copy-done.33, ...), custom_call_target="tpu_custom_call" | custom-call | tf_op jit(solution)/shard_map/weight_grads/pallas_call | solution.py:386
  180.3 33.3 %all_to_all.10.in_ref = bf16[8,192,256]{2,1,0:T(8,128)(2,1)S(1)} all-to-all(bf16[8,192,256]{2,1,0:T(8,128)(2,1)} %get-tuple-element.88), channel_id=1, replica_groups=mesh['segment'=4,'chan'=16,'dp'=8] {'dp'}, dimensions={0} | all-to-all | bytes 1572864 | tf_op jit(solution)/shard_map/all_to_all | solution.py:485
  213.6 0.1 sum_microbatches.1
  213.8 24.7 %all_to_all.11.in_ref = bf16[8,192,256]{2,1,0:T(8,128)(2,1)S(1)} all-to-all(bf16[8,192,256]{2,1,0:T(8,128)(2,1)S(1)} %sum_microbatches.1), channel_id=1, replica_groups=mesh['segment'=4,'chan'=16,'dp'=8] {'dp'}, dimensions={0} | all-to-all | bytes 1572864 | tf_op jit(solution)/shard_map/all_to_all | solution.py:485
  238.5 1.2 widen.1
  (49 shorter events, 0.1 us)
Async XLA Ops:
  7.2 23.9 %copy-start.16 = (bf16[1,2,96,432]{3,2,1,0:T(8,128)(2,1)S(1)}, bf16[1,2,96,432]{3,2,1,0:T(8,128)(2,1)}, u32[]{:S(2)}) copy-start(bf16[1,2,96,432]{3,2,1,0:T(8,128)(2,1)} %refs_3_.7) | copy-start | bytes 497668
  7.2 23.9 %copy-start.4 = (bf16[1,2,96,1536]{3,2,1,0:T(8,128)(2,1)S(1)}, bf16[1,2,96,1536]{3,2,1,0:T(8,128)(2,1)}, u32[]{:S(2)}) copy-start(bf16[1,2,96,1536]{3,2,1,0:T(8,128)(2,1)} %refs_2_.7) | copy-start | bytes 1769476
  7.2 76.3 %all-gather.5.cloned.1.call-start = ((), (), s32[]{:S(2)}) async-start(), calls=%async_computation.2 | async-start | bytes 3981312 | tf_op jit(solution)/shard_map/all_gather | solution.py:460
  9.9 128.5 %all-gather.7.cloned.1.call-start = ((), (), s32[]{:S(2)}) async-start(), calls=%async_computation.3 | async-start | bytes 3981312 | tf_op jit(solution)/shard_map/all_gather | solution.py:491
  31.0 52.5 %copy-start.6 = (bf16[1,1536,256]{2,1,0:T(8,128)(2,1)}, bf16[1,1536,256]{2,1,0:T(8,128)(2,1)S(1)}, u32[]{:S(2)}) copy-start(bf16[1,1536,256]{2,1,0:T(8,128)(2,1)S(1)} %copy.15) | copy-start | bytes 2359300
  31.1 52.5 %copy-start.34 = (s32[2]{0:T(128)}, s32[2]{0:T(128)S(1)}, u32[]{:S(2)}) copy-start(s32[2]{0:T(128)S(1)} %pad_add_fusion.refs_0_) | copy-start | bytes 28
  31.1 1.1 copy-start.10
  32.2 0.9 copy-start.18
  34.6 0.6 copy-start.31
  35.2 24.3 %copy-start.28 = (f32[96,256]{1,0:T(8,128)}, f32[96,256]{1,0:T(8,128)S(1)}, u32[]{:S(2)}) copy-start(f32[96,256]{1,0:T(8,128)S(1)} %get-tuple-element.77.refs_15_) | copy-start | bytes 294916
  56.8 1.5 copy-start.7
  58.3 0.7 copy-start.29
  58.9 0.6 copy-start.32
  83.5 45.8 %copy-start = (bf16[768,2304]{1,0:T(8,128)(2,1)S(1)}, bf16[768,2304]{1,0:T(8,128)(2,1)}, u32[]{:S(2)}) copy-start(bf16[768,2304]{1,0:T(8,128)(2,1)} %all-gather.5.cloned.1.call-done.refs_2_) | copy-start | bytes 10616836
  93.2 36.1 %copy-start.12 = (f32[1,768,256]{2,1,0:T(8,128)S(1)}, f32[1,768,256]{2,1,0:T(8,128)}, u32[]{:S(2)}) copy-start(f32[1,768,256]{2,1,0:T(8,128)} %get-tuple-element.63.refs_3_) | copy-start | bytes 2359300
  93.3 36.1 %copy-start.36 = (s32[2]{0:T(128)S(1)}, s32[2]{0:T(128)}, u32[]{:S(2)}) copy-start(s32[2]{0:T(128)} %copy-done.34) | copy-start | bytes 28
  96.0 1.1 copy-start.5
  97.1 0.9 copy-start.11
  98.0 0.9 copy-start.17
  98.9 0.9 copy-start.19
  99.9 0.7 copy-start.35
  100.5 1.5 copy-start.8
  100.5 28.8 %copy-start.14 = (f32[1,768,256]{2,1,0:T(8,128)S(1)}, f32[1,768,256]{2,1,0:T(8,128)}, u32[]{:S(2)}) copy-start(f32[1,768,256]{2,1,0:T(8,128)} %get-tuple-element.64.refs_4_) | copy-start | bytes 2359300
  102.0 0.6 copy-start.30
  102.6 0.6 copy-start.33
  133.3 0.9 copy-start.2
  134.2 0.9 copy-start.20
  135.1 0.7 copy-start.25
  138.5 24.3 %copy-start.37 = (s32[2]{0:T(128)S(1)}, s32[2]{0:T(128)}, u32[]{:S(2)}) copy-start(s32[2]{0:T(128)} %copy-done.34) | copy-start | bytes 28
  138.5 24.3 %copy-start.13 = (f32[1,768,256]{2,1,0:T(8,128)S(1)}, f32[1,768,256]{2,1,0:T(8,128)}, u32[]{:S(2)}) copy-start(f32[1,768,256]{2,1,0:T(8,128)} %get-tuple-element.63.refs_3_) | copy-start | bytes 2359300
  138.5 24.3 %copy-start.15 = (f32[1,768,256]{2,1,0:T(8,128)S(1)}, f32[1,768,256]{2,1,0:T(8,128)}, u32[]{:S(2)}) copy-start(f32[1,768,256]{2,1,0:T(8,128)} %get-tuple-element.64.refs_4_) | copy-start | bytes 2359300
  162.8 6.3 %copy-start.3 = (bf16[1536,256]{1,0:T(8,128)(2,1)}, bf16[1536,256]{1,0:T(8,128)(2,1)S(1)}, u32[]{:S(2)}) copy-start(bf16[1536,256]{1,0:T(8,128)(2,1)S(1)} %all_gather.53.refs_1_) | copy-start | bytes 2359300
  162.8 6.3 %copy-start.1 = (bf16[768,2304]{1,0:T(8,128)(2,1)S(1)}, bf16[768,2304]{1,0:T(8,128)(2,1)}, u32[]{:S(2)}) copy-start(bf16[768,2304]{1,0:T(8,128)(2,1)} %all-gather.7.cloned.1.call-done.refs_2_) | copy-start | bytes 10616836
  162.8 6.3 %copy-start.23 = (f32[1,768,256]{2,1,0:T(8,128)S(1)}, f32[1,768,256]{2,1,0:T(8,128)}, u32[]{:S(2)}) copy-start(f32[1,768,256]{2,1,0:T(8,128)} %get-tuple-element.72.refs_3_) | copy-start | bytes 2359300
  162.8 6.3 %copy-start.24 = (f32[1,768,256]{2,1,0:T(8,128)S(1)}, f32[1,768,256]{2,1,0:T(8,128)}, u32[]{:S(2)}) copy-start(f32[1,768,256]{2,1,0:T(8,128)} %get-tuple-element.73.refs_4_) | copy-start | bytes 2359300
  166.7 2.4 copy-start.21
  166.7 6.3 %copy-start.26 = (bf16[768,256]{1,0:T(8,128)(2,1)}, bf16[768,256]{1,0:T(8,128)(2,1)S(1)}, u32[]{:S(2)}) copy-start(bf16[768,256]{1,0:T(8,128)(2,1)S(1)} %get-tuple-element.82.refs_23_) | copy-start | bytes 1179652
  169.1 6.5 %copy-start.9 = (bf16[1536,256]{1,0:T(8,128)(2,1)}, bf16[1536,256]{1,0:T(8,128)(2,1)S(1)}, u32[]{:S(2)}) copy-start(bf16[1536,256]{1,0:T(8,128)(2,1)S(1)} %all_gather.54.refs_1_) | copy-start | bytes 2359300
  173.0 2.5 %copy-start.22 = (f32[768,256]{1,0:T(8,128)}, f32[768,256]{1,0:T(8,128)S(1)}, u32[]{:S(2)}) copy-start(f32[768,256]{1,0:T(8,128)S(1)} %get-tuple-element.75.refs_12_) | copy-start | bytes 2359300
  173.0 2.5 %copy-start.27 = (bf16[768,256]{1,0:T(8,128)(2,1)}, bf16[768,256]{1,0:T(8,128)(2,1)S(1)}, u32[]{:S(2)}) copy-start(bf16[768,256]{1,0:T(8,128)(2,1)S(1)} %get-tuple-element.74.refs_11_) | copy-start | bytes 1179652
Sparse Core Ops, SparseCore 0:
  10.1 60.4 all-gather.4
  72.6 52.8 all-gather.6

commit v5 on v4

v5 whole, which is shorter than its diff:
```python
import functools

import jax
import jax.numpy as jnp
from jax import lax
from jax.experimental import pallas as pl
from jax.experimental.pallas import tpu as pltpu
from jax.sharding import PartitionSpec as P

GS = 48
WW = 64
NORM_EPS = 1e-05
TAIL = 512
F32 = jnp.float32
BF16 = jnp.bfloat16
VMEM = pl.BlockSpec(memory_space=pltpu.VMEM)
SMEM = pl.BlockSpec(memory_space=pltpu.SMEM)
ANY = pl.BlockSpec(memory_space=pl.ANY)
NT = (((1,), (1,)), ((), ()))
TN = (((0,), (0,)), ((), ()))


def vmem(mebibytes):
    return pltpu.CompilerParams(vmem_limit_bytes=mebibytes * 1024 * 1024)


def shape_of(shape, dtype):
    return jax.ShapeDtypeStruct(shape, dtype)


def total(block):
    return jnp.sum(jnp.sum(block, axis=1, keepdims=True), axis=0, keepdims=True)


def norm_group(h, gain, bias):
    scale = 1.0 / (h.shape[0] * h.shape[1])
    pre = h.astype(F32)
    pre = pre - total(pre) * scale
    inv_std = lax.rsqrt(total(pre * pre) * scale + NORM_EPS)
    xhat = pre * inv_std
    n = xhat * gain + bias
    sig = jax.nn.sigmoid(n)
    slope = sig * (1.0 + n * (1.0 - sig))
    return xhat, n, sig, slope, inv_std


def column(line):
    count = line.shape[1]
    down = lax.broadcasted_iota(jnp.int32, (count, count), 0)
    across = lax.broadcasted_iota(jnp.int32, (count, count), 1)
    return jnp.sum(jnp.where(down == across, line, 0.0), axis=1, keepdims=True)


def columns_of(gain_ref, bias_ref, b):
    return column(gain_ref[0, b : b + 1, :]), column(bias_ref[0, b : b + 1, :])


def prepare_kernel(*refs):
    pack_refs = (refs[6], refs[7])
    w_ref, wc_ref, h1_ref, h2_ref, gain_ref, bias_ref, sems = refs[8:]
    copies = [
        pltpu.make_async_copy(refs[i], refs[8 + i], sems.at[i]) for i in range(6)
    ]
    for copy in copies:
        copy.start()
    for copy in copies:
        copy.wait()
    chans, width = w_ref.shape[2:]
    taps = wc_ref.shape[3]
    lane = lax.broadcasted_iota(jnp.int32, (chans, TAIL - 384), 1)
    for b, h_ref in ((1, h2_ref), (0, h1_ref)):
        pack_ref = pack_refs[b]
        pack_ref[:, :width] = w_ref[0, b]
        pack_ref[:, width : width + 384] = wc_ref[0, b, :, :384]
        last = wc_ref[0, b, :, 384:].astype(F32)
        last = jnp.concatenate(
            [last, jnp.zeros((chans, TAIL - taps), F32)], axis=1
        )
        at = taps - 384
        for whole in columns_of(gain_ref, bias_ref, b):
            rest = whole
            for _ in range(3):
                piece = rest.astype(BF16).astype(F32)
                rest = rest - piece
                last = jnp.where(lane == at, piece, last)
                at += 1
        pack_ref[:, width + 384 : width + TAIL] = last.astype(BF16)
        pack_ref[:, width + TAIL :] = h_ref[0, 0]


def prepare(*operands):
    chans, width = operands[0].shape[2:]
    positions = operands[2].shape[3]
    pack = shape_of((chans, width + TAIL + positions), BF16)
    return pl.pallas_call(
        prepare_kernel,
        out_shape=(pack, pack),
        in_specs=[ANY] * 6,
        out_specs=[VMEM] * 2,
        scratch_shapes=[pltpu.VMEM(x.shape, x.dtype) for x in operands]
        + [pltpu.SemaphoreType.DMA((6,))],
        compiler_params=vmem(56),
        name="prepare",
    )(*operands)


def shifted(value, step_row, step_col, row, col):
    length = value.shape[1]
    rows = length // WW
    by = step_row * WW + step_col
    if by == 0:
        return value
    moved = pltpu.roll(value, (-by) % length, axis=1)
    inside = None
    if step_row:
        inside = row < rows - 1 if step_row > 0 else row > 0
    if step_col:
        here = col < WW - 1 if step_col > 0 else col > 0
        inside = here if inside is None else inside & here
    return jnp.where(inside, moved, 0.0)


def grid_of(shape):
    lane = lax.broadcasted_iota(jnp.int32, shape, 1)
    return lane // WW, lane % WW


def own_positions(g, chan_at, count):
    down = lax.broadcasted_iota(jnp.int32, (count, g.shape[1]), 0)
    across = lax.broadcasted_iota(jnp.int32, (count, g.shape[1]), 1)
    pick = jnp.where(across == down + chan_at * count, 1.0, 0.0).astype(BF16)
    return lax.dot_general(pick, g, NT, preferred_element_type=F32).astype(BF16)


def gh_of(ga, xhat, rate):
    scale = 1.0 / (ga.shape[0] * ga.shape[1])
    rw = ga * rate
    gh = rw - total(rw) * scale - xhat * (total(rw * xhat) * scale)
    return gh.astype(BF16)


def conv_back(taps_w, gh, row, col):
    spread = lax.dot_general(taps_w, gh, TN, preferred_element_type=F32)
    branch = None
    for step_col in (-1, 0, 1):
        part = None
        for step_row in (-1, 0, 1):
            tap = 3 * (step_row + 1) + step_col + 1
            term = shifted(spread[tap * GS : (tap + 1) * GS, :], -step_row, 0, row, col)
            part = term if part is None else part + term
        part = shifted(part, 0, -step_col, row, col)
        branch = part if branch is None else branch + part
    return branch.astype(BF16)


def in_order(g_buf, g_ref, own_rows):
    per = g_ref.shape[0] // 2 // own_rows
    for c in range(2):
        for y in range(per):
            to = (2 * y + c) * own_rows
            at = (c * per + y) * own_rows
            g_buf[to : to + own_rows, :] = g_ref[at : at + own_rows, :]


def add_branch(out_ref, rows, src, mine_at, branch):
    mine = src[pl.ds(pl.multiple_of(mine_at, GS), GS), :].astype(F32)
    out_ref[rows, :] = (mine + branch.astype(F32)).astype(BF16)


def own_block(b, alone, flags, g, ordered, params):
    whole, positions = g.shape
    proj_weight, conv_weight, h, gain, bias = params
    chans = proj_weight.shape[2]

    def kernel(flags_ref, g_ref, w_ref, wc_ref, h_ref, gain_ref, bias_ref, out_ref, g_buf):
        src = g_ref
        if not ordered:
            in_order(g_buf, g_ref, chans)
            src = g_buf
        ga = jnp.dot(w_ref[0, 0], src[...], preferred_element_type=F32)
        row, col = grid_of((GS, positions))
        gains, biases = columns_of(gain_ref, bias_ref, b)
        for at in range(0, chans, GS):
            rows = slice(at, at + GS)
            xhat, _, _, slope, inv_std = norm_group(h_ref[0, 0, rows, :], gains[rows], biases[rows])
            gh = gh_of(ga[rows, :], xhat, slope * (gains[rows] * inv_std))
            branch = conv_back(wc_ref[0, 0, rows, :], gh, row, col)
            add_branch(out_ref, rows, src, flags_ref[1] * chans + at, branch)

    def at_block(shape):
        return pl.BlockSpec((1, 1) + shape[2:], lambda i: (0, b, 0, 0))

    return pl.pallas_call(
        kernel,
        out_shape=shape_of((chans, positions), BF16),
        grid=(1,),
        in_specs=[SMEM, VMEM, at_block(proj_weight.shape), at_block(conv_weight.shape)]
        + [VMEM] * 3,
        out_specs=VMEM,
        scratch_shapes=[pltpu.VMEM((16, 128) if ordered else (whole, positions), BF16)],
        compiler_params=vmem(56 if alone else 8),
        name="own_block",
    )(flags, g, *params)


def first_block(flags, g, ordered, own_rows, pack):
    whole, positions = g.shape
    chans = pack.shape[0]
    width = whole
    per = whole // 2 // own_rows
    shape = (per, 2, own_rows, positions)
    g = g.reshape(shape if ordered else (2, per, own_rows, positions))

    def kernel(
        flags_ref, g_ref, pack_ref, out_ref, xhat_out, rate_out,
        w_ref, taps_ref, h_ref, g_buf, src, xhat_ref, rate_ref, sems,
    ):
        def copy(i, a, to):
            return pltpu.make_async_copy(a, to, sems.at[i])

        loads = [
            copy(0, pack_ref.at[:, width + TAIL : width + TAIL + positions], h_ref),
            copy(1, pack_ref.at[:, width : width + TAIL], taps_ref),
            copy(2, pack_ref.at[:, :width], w_ref),
        ] + [
            copy(3 + c, g_ref.at[:, c] if ordered else g_ref.at[c], g_buf.at[:, c])
            for c in range(2)
        ]
        for load in loads:
            load.start()
        loads[0].wait()
        loads[1].wait()
        at = 9 * GS - 384
        for q in range(0, chans, GS):
            rows = slice(q, q + GS)
            side = taps_ref[rows, 384:].astype(F32)
            gain, bias = (
                side[:, i : i + 1] + side[:, i + 1 : i + 2] + side[:, i + 2 : i + 3]
                for i in (at, at + 3)
            )
            xhat, _, _, slope, inv_std = norm_group(h_ref[rows, :], gain, bias)
            xhat_ref[rows, :] = xhat
            rate_ref[rows, :] = slope * (gain * inv_std)
        stores = [copy(5, xhat_ref, xhat_out), copy(6, rate_ref, rate_out)]
        for store in stores:
            store.start()
        for load in loads[2:]:
            load.wait()
        src[...] = g_buf[...].reshape(whole, positions)
        wide_body(
            flags_ref, src, w_ref[...], lambda rows: taps_ref[rows, : 9 * GS],
            xhat_ref, rate_ref, out_ref, own_rows,
        )
        for store in stores:
            store.wait()

    full = shape_of((chans, positions), F32)
    return pl.pallas_call(
        kernel,
        out_shape=(shape_of((chans, positions), BF16), full, full),
        in_specs=[SMEM, ANY, ANY],
        out_specs=[VMEM, ANY, ANY],
        scratch_shapes=[
            pltpu.VMEM((chans, width), BF16),
            pltpu.VMEM((chans, TAIL), BF16),
            pltpu.VMEM((chans, positions), BF16),
            pltpu.VMEM(shape, BF16),
            pltpu.VMEM((whole, positions), BF16),
            pltpu.VMEM((chans, positions), F32),
            pltpu.VMEM((chans, positions), F32),
            pltpu.SemaphoreType.DMA((7,)),
        ],
        compiler_params=vmem(56),
        name="first_block",
    )(flags, g, pack)


def wide_body(flags_ref, src, matrix, taps_of, xhat_ref, rate_ref, out_ref, own_rows):
    chans, positions = xhat_ref.shape
    ga = jnp.dot(matrix, src[...], preferred_element_type=F32)
    core = flags_ref[1] & 1
    row, col = grid_of((GS, positions))
    for at in range(0, chans, GS):
        y, q = divmod(at, own_rows)
        rows = slice(at, at + GS)
        gh = gh_of(ga[rows, :], xhat_ref[rows, :], rate_ref[rows, :])
        branch = conv_back(taps_of(rows), gh, row, col)
        add_branch(out_ref, rows, src, (2 * y + core) * own_rows + q, branch)


def wide_block(flags, g, ordered, own_rows, pack, state):
    whole, positions = g.shape
    chans = pack.shape[0]

    def kernel(flags_ref, g_ref, pack_ref, xhat_ref, rate_ref, out_ref, g_buf):
        src = g_ref
        if not ordered:
            in_order(g_buf, g_ref, own_rows)
            src = g_buf
        wide_body(
            flags_ref, src, pack_ref[:, :whole],
            lambda rows: pack_ref[rows, whole : whole + 9 * GS],
            xhat_ref, rate_ref, out_ref, own_rows,
        )

    return pl.pallas_call(
        kernel,
        out_shape=shape_of((chans, positions), BF16),
        in_specs=[SMEM] + [VMEM] * 4,
        out_specs=VMEM,
        scratch_shapes=[pltpu.VMEM((16, 128) if ordered else (whole, positions), BF16)],
        compiler_params=vmem(14),
        name="wide_block",
    )(flags, g, pack, *state)


def storer(out_ref):
    step = out_ref.shape[2]

    def store(first_row, at, value):
        for i in range(value.shape[1] // step):
            out_ref[at // step + i, first_row : first_row + value.shape[0], :] = value[
                :, i * step : (i + 1) * step
            ]

    return store


def summed(in_ref, rows):
    acc = in_ref[0, rows, :].astype(F32)
    for m in range(1, in_ref.shape[0]):
        acc = acc + in_ref[m, rows, :].astype(F32)
    return acc.astype(BF16)


def weight_grads(flags, orders, kept, latents, params, inputs):
    proj_weight, conv_weight, h_one, h_two, gain, bias = params
    ticks = len(latents)
    chans, width = proj_weight.shape[2:]
    positions = h_one.shape[3]
    shards = width // chans
    slab = positions // shards
    members = lax.axis_size("dp")
    step = (width + TAIL) // members
    pairs = shards // 2

    def split(g, ordered):
        return g.reshape((pairs, 2, chans, positions) if ordered else (2, pairs, chans, positions))

    operands = [split(g, o) for b in range(2) for g, o in zip(kept[b], orders[b])]
    operands += [split(g, o) for o, g in latents]
    order_of = [*orders[0], *orders[1], *(o for o, _ in latents)]

    def kernel(*refs):
        flags_ref = refs[0]
        fetched = refs[1 : 1 + len(operands)]
        w_ref, h1_ref, h2_ref, gain_ref, bias_ref, *x_refs = refs[1 + len(operands) : -6]
        out_ref, lat_ref, stacks, g_bufs, g_flat, sems = refs[-6:]
        segment_at, chan_at = flags_ref[0], flags_ref[1]

        def copies(t):
            made = []
            for i in range(3):
                g = fetched[ticks * i + t]
                for c in range(2):
                    made.append(
                        pltpu.make_async_copy(
                            g.at[:, c] if order_of[ticks * i + t] else g.at[c],
                            g_bufs.at[i, :, c],
                            sems.at[len(made)],
                        )
                    )
            return made

        def each(act):
            for t in range(ticks):

                @pl.when(segment_at == ticks - 1 - t)
                def _():
                    for made in copies(t):
                        act(made)

        each(lambda made: made.start())
        row, col = grid_of((GS, positions))
        lane = lax.broadcasted_iota(jnp.int32, (GS, TAIL), 1)
        for b in range(2):
            for q in range(0, chans, GS):
                x = x_refs[b][0, 0, q : q + GS, :].astype(F32)
                for step_row in (-1, 0, 1):
                    for step_col in (-1, 0, 1):
                        tap = 3 * (step_row + 1) + step_col + 1
                        stacks[b, q // GS, tap * GS : (tap + 1) * GS, :] = shifted(
                            x, step_row, step_col, row, col
                        ).astype(BF16)
                stacks[b, q // GS, 9 * GS :, :] = jnp.zeros((TAIL - 9 * GS, positions), BF16)
        each(lambda made: made.wait())
        store = storer(out_ref)
        for b, h_ref in enumerate((h1_ref, h2_ref)):
            g_flat[...] = g_bufs[b].reshape(width, positions)
            ga = jnp.dot(w_ref[0, b], g_flat[...], preferred_element_type=F32)
            gains, biases = columns_of(gain_ref, bias_ref, b)
            acts = []
            for q in range(0, chans, GS):
                rows = slice(q, q + GS)
                xhat, n, sig, slope, inv_std = norm_group(
                    h_ref[0, 0, rows, :], gains[rows], biases[rows]
                )
                acts.append((n * sig).astype(BF16))
                gh = gh_of(ga[rows, :], xhat, slope * (gains[rows] * inv_std))
                taps = lax.dot_general(
                    gh, stacks[b, q // GS], NT, preferred_element_type=F32
                )
                gn = ga[rows, :] * slope
                by_gain = jnp.sum(gn * xhat, axis=1, keepdims=True)
                by_bias = jnp.sum(gn, axis=1, keepdims=True)
                taps = jnp.where(lane == 9 * GS, by_gain, taps)
                taps = jnp.where(lane == 9 * GS + 1, by_bias, taps)
                store(b * chans + q, width, taps.astype(BF16))
            act = jnp.concatenate(acts, axis=0)
            proj = lax.dot_general(act, g_flat[...], NT, preferred_element_type=F32)
            store(b * chans, 0, proj.astype(BF16))
        lat_ref[...] = own_positions(g_bufs[2].reshape(width, positions), chan_at, slab)

    return pl.pallas_call(
        kernel,
        out_shape=(
            shape_of((members, 2 * chans, step), BF16),
            shape_of((slab, width), BF16),
        ),
        in_specs=[SMEM] + [ANY] * len(operands) + [VMEM] * 7,
        out_specs=[VMEM] * 2,
        scratch_shapes=[
            pltpu.VMEM((2, chans // GS, TAIL, positions), BF16),
            pltpu.VMEM((3, pairs, 2, chans, positions), BF16),
            pltpu.VMEM((width, positions), BF16),
            pltpu.SemaphoreType.DMA((6,)),
        ],
        compiler_params=vmem(56),
        name="weight_grads",
    )(flags, *operands, proj_weight, h_one, h_two, gain, bias, *inputs)


def sum_kernel(in_ref, out_ref):
    done = summed(in_ref, slice(0, out_ref.shape[1]))
    for m in range(out_ref.shape[0]):
        out_ref[m] = done


def spread_sums(parts):
    return pl.pallas_call(
        sum_kernel,
        out_shape=shape_of(parts.shape, BF16),
        in_specs=[VMEM],
        out_specs=VMEM,
        compiler_params=vmem(6),
        name="sum_microbatches",
    )(parts)


def widen_kernel(in_ref, proj_ref, conv_ref, gain_ref, bias_ref):
    chans, width = proj_ref.shape[2:]
    step = in_ref.shape[2]
    down = lax.broadcasted_iota(jnp.int32, (chans, chans), 0)
    across = lax.broadcasted_iota(jnp.int32, (chans, chans), 1)
    first = width // step
    for b in range(2):
        rows = slice(b * chans, (b + 1) * chans)
        for i in range(first):
            proj_ref[0, b, :, i * step : (i + 1) * step] = in_ref[i, rows, :].astype(F32)
        conv_ref[0, b, :, :step] = in_ref[first, rows, :].astype(F32)
        side = in_ref[first + 1, rows, :].astype(F32)
        conv_ref[0, b, :, step:] = side[:, : 9 * GS - step]
        for i, to in enumerate((gain_ref, bias_ref)):
            at = 9 * GS - step + i
            lined = jnp.where(down == across, side[:, at : at + 1], 0.0)
            to[0, b : b + 1, :] = jnp.sum(lined, axis=0, keepdims=True)


def widen(sums, width):
    chans = sums.shape[1] // 2
    return pl.pallas_call(
        widen_kernel,
        out_shape=(
            shape_of((1, 2, chans, width), F32),
            shape_of((1, 2, chans, 9 * GS), F32),
            shape_of((1, 2, chans), F32),
            shape_of((1, 2, chans), F32),
        ),
        in_specs=[VMEM],
        out_specs=[VMEM] * 4,
        compiler_params=vmem(8),
        name="widen",
    )(sums)


def gather(block_, axis, groups=None):
    return lax.all_gather(block_, axis, axis=0, tiled=True, axis_index_groups=groups)


def per_device(
    grad_top,
    inputs_one,
    conv_one,
    inputs_two,
    conv_two,
    proj_weight,
    conv_weight,
    norm_gain,
    norm_bias,
):
    segments = lax.axis_size("segment")
    segment_at = lax.axis_index("segment")
    chan_at = lax.axis_index("chan")
    members = lax.axis_size("dp")
    shards = lax.axis_size("chan")
    chans, positions = conv_one.shape[2:]
    width = proj_weight.shape[3]
    cores = [[2 * y, 2 * y + 1] for y in range(shards // 2)]
    columns = [[2 * y + c for y in range(shards // 2)] for c in range(2)]

    def exchange(blocks):
        return lax.all_to_all(blocks, "dp", split_axis=0, concat_axis=0, tiled=True)

    params = (proj_weight, conv_weight, conv_one, conv_two, norm_gain, norm_bias)
    first_pack, second_pack = prepare(*params)
    packs = [None, gather(second_pack, "chan", columns)]
    packs[0] = lax.all_gather(
        first_pack[None], "chan", axis=1, tiled=True, axis_index_groups=columns
    )[0]
    states = [None, None]
    kept = [[], []]
    orders = [[], []]
    latents = []
    flags = jnp.stack([segment_at.astype(jnp.int32), chan_at.astype(jnp.int32)])
    for tick in range(segments):
        if tick == 0:
            g = lax.all_gather(grad_top[0], "chan", axis=1, tiled=True)
            ordered = True
        else:
            lower = segments - 1 - tick
            rest = [s for s in range(segments) if s not in (lower, lower + 1)]
            groups = sorted(
                [[lower, lower + 1]] + [rest[i : i + 2] for i in range(0, len(rest), 2)]
            )
            ordered = out.shape[0] == chans
            moved = gather(out, "segment", groups)[out.shape[0] :]
            g = gather(moved, "chan", None if ordered else cores)
            latents.append((ordered, g))
        for b in (1, 0):
            kept[b].append(g)
            if tick == 0 or (tick == 1 and b == 0):
                h = conv_two if b == 1 else conv_one
                out = own_block(
                    b, tick == 1, flags, g, ordered,
                    (proj_weight, conv_weight, h, norm_gain, norm_bias),
                )
            elif states[b] is None:
                packs[b], g = lax.optimization_barrier((packs[b], g))
                out, *states[b] = first_block(flags, g, ordered, chans, packs[b])
            else:
                out = wide_block(flags, g, ordered, chans, packs[b], states[b])
            orders[b].append(ordered)
            if b == 1 or tick == segments - 1:
                ordered = out.shape[0] == chans
                g = gather(out, "chan", None if ordered else cores)
    latents.append((ordered, g))

    parts, latent = weight_grads(
        flags, orders, kept, latents, params, (inputs_one, inputs_two)
    )
    sums = exchange(spread_sums(exchange(parts)))
    proj, conv, by_gain, by_bias = widen(sums, width)
    return latent.T[None, None], proj, conv, by_gain, by_bias


def solution(mesh):
    return jax.shard_map(
        per_device,
        mesh=mesh,
        in_specs=(
            P("dp", None, "chan"),
            P("segment", "dp", "chan", None),
            P("segment", "dp", "chan", None),
            P("segment", "dp", "chan", None),
            P("segment", "dp", "chan", None),
            P("segment", None, "chan", None),
            P("segment", None, "chan", None),
            P("segment", None, "chan"),
            P("segment", None, "chan"),
        ),
        out_specs=(
            P("segment", "dp", None, "chan"),
            P("segment", None, "chan", None),
            P("segment", None, "chan", None),
            P("segment", None, "chan"),
            P("segment", None, "chan"),
        ),
        check_vma=False,
    )
```

time: 247 us -> 240 us (0.972)
  local copies, waits for them, and re-layouts: 12.6 us -> 1.32 us
  blocking collectives: 175 us -> 179 us
    unnamed x76 -> x44, local copies, waits for them, and re-layouts: 12.3 us -> 1.02 us
    all_gather x11, blocking collectives: 96.5 us -> 101 us  [gather(): lax.all_gather(block_, axis, axis=0, tiled=True, axis_index_groups=groups)]
  transfers between devices with their start and end apart: 2 -> 2, of which waited for: 0 -> 0; matrix products, arithmetic and copies ran while one was open for 0% -> 0% of each run, Pallas kernels for 7% -> 8%
where the time goes in v5:
time: 240 us
  blocking collectives  179 us (75%)
  Pallas kernels  44.3 us (18%)
  between operations  14.3 us (6%)
    all_gather x11, blocking collectives, gather(): lax.all_gather(block_, axis, axis=0, tiled=True, axis_index_groups=groups)  101 us
    all_to_all x2, blocking collectives, exchange(): return lax.all_to_all(blocks, 'dp', split_axis=0, concat_axis=0, tiled=True)  57.9 us
    all_gather x1, blocking collectives, per_device(): g = lax.all_gather(grad_top[0], 'chan', axis=1, tiled=True)  20 us
    pallas_call x2, Pallas kernels, first_block(): pl.pallas_call(kernel, out_shape=(shape_of((chans, positions), BF16), ful...  17.6 us
    pallas_call x3, Pallas kernels, wide_block(): pl.pallas_call(kernel, out_shape=shape_of((chans, positions), BF16), in_s...  11.7 us
    pallas_call x3, Pallas kernels, own_block(): pl.pallas_call(kernel, out_shape=shape_of((chans, positions), BF16), grid...  5.82 us
    pallas_call x1, Pallas kernels, weight_grads(): pl.pallas_call(kernel, out_shape=(shape_of((members, 2 * chans, step), BF...  5.69 us
  transfers between devices with their start and end apart: 2, of which 0 were waited for; matrix products, arithmetic and copies ran while one was open for 0% of the time, Pallas kernels for 8%

profile of v5, /device:TPU:6, one launch (start us, length us, event | category | flops | bytes accessed | tf_op | source)
XLA Modules:
  0.0 239.8 jit_solution(12359768301959504586)
XLA Ops:
  7.2 0.0 copy-start.21
  7.2 0.0 copy-start.20
  7.2 0.0 copy-start.1
  7.2 0.0 copy-start.12
  7.2 0.0 copy-start.13
  7.2 0.0 copy-start.16
  7.2 0.0 all-gather.5.cloned.1.call-start
  7.3 2.3 prepare.1
  9.6 0.0 all-gather.5.cloned.1.call-update
  9.6 0.0 all-gather.7.cloned.1.call-start
  9.7 0.7 all-gather.7.cloned.1.call-update
  10.4 20.0 %all-gather = bf16[1,1536,256]{1,2,0:T(8,128)(2,1)S(1)} all-gather(bf16[1,1536,16]{1,2,0:T(8,128)(2,1)} %param.9), channel_id=2, replica_groups=mesh['segment'=4,'chan'=16,'dp'=8] {'chan'}, dimensions={2}, use_global_device_ids=true | all-gather | bytes 835584 | tf_op jit(solution)/shard_map/all_gather | solution.py:537
  30.4 0.3 copy.15
  30.7 0.0 copy-start.6
  30.7 0.1 pad_add_fusion.flags_ref.refs_0_
  30.8 0.0 copy-done.21
  30.8 0.0 copy-done.20
  30.8 0.0 copy-done.1
  30.8 0.0 copy-done.12
  30.8 0.0 copy-done.16
  30.8 1.5 own_block.3
  32.3 21.3 %all_gather.43.g_ref = bf16[1536,256]{1,0:T(8,128)(2,1)S(1)} all-gather(bf16[96,256]{1,0:T(8,128)(2,1)S(1)} %own_block.3), channel_id=1, replica_groups=mesh['segment'=4,'chan'=16,'dp'=8] {'chan'}, dimensions={0}, use_global_device_ids=true | all-gather | bytes 835584 | tf_op jit(solution)/shard_map/all_gather | solution.py:497
  53.6 0.0 copy-done.13
  53.6 1.5 own_block.4
  55.1 0.0 copy-done.7
  55.1 4.8 %all_gather.45 = bf16[192,256]{1,0:T(8,128)(2,1)S(1)} all-gather(bf16[96,256]{1,0:T(8,128)(2,1)S(1)} %own_block.4), channel_id=1, replica_groups={{0,128},{256,384},{1,129},{257,385},{2,130},{258,386},{3,131},{259,387}..., dimensions={0}, use_global_device_ids=true | all-gather | bytes 147456 | tf_op jit(solution)/shard_map/all_gather | solution.py:497
  59.9 20.9 %all_gather.46 = bf16[1536,256]{1,0:T(8,128)(2,1)} all-gather(bf16[96,256]{1,0:T(8,128)(2,1)S(1)} %slice.12), channel_id=1, replica_groups=mesh['segment'=4,'chan'=16,'dp'=8] {'chan'}, dimensions={0}, use_global_device_ids=true | all-gather | bytes 835584 | tf_op jit(solution)/shard_map/all_gather | solution.py:497
  80.8 0.0 copy-done.6
  80.8 0.0 copy-done.17
  80.8 8.9 %first_block.2 = (bf16[768,256]{1,0:T(8,128)(2,1)}, f32[768,256]{1,0:T(8,128)}, f32[768,256]{1,0:T(8,128)}) custom-call(s32[2]{0:T(128)} %copy-done.17, bf16[8,2,96,256]{3,2,1,0:T(8,128)(2,1)} %bitcast.25, bf16[768,2304]{1,0:T(8,128)(2,1)} %all-gather.5.cloned.1.call-done.pack_ref), custom_call_target="tpu_custom_call" | custom-call | tf_op jit(solution)/shard_map/first_block/pallas_call | solution.py:258
  89.7 0.0 copy-start.8
  89.7 0.0 copy-start.10
  89.7 0.0 copy-start.18
  89.7 4.4 %all_gather.47.g_ref = bf16[1536,256]{1,0:T(8,128)(2,1)} all-gather(bf16[768,256]{1,0:T(8,128)(2,1)} %get-tuple-element.26), channel_id=1, replica_groups={{0,8},{16,24},{32,40},{48,56},{64,72},{80,88},{96,104},{112,120},{1,9},..., dimensions={0}, use_global_device_ids=true | all-gather | bytes 1179648 | tf_op jit(solution)/shard_map/all_gather | solution.py:497
  94.2 2.9 %own_block.5 = bf16[96,256]{1,0:T(8,128)(2,1)} custom-call(s32[2]{0:T(128)} %copy-done.17, bf16[1536,256]{1,0:T(8,128)(2,1)} %all_gather.47.g_ref, bf16[1,2,96,1536]{3,2,1,0:T(8,128)(2,1)} %refs_13_.1, bf16[1,2,96,432]{3,2,1,0:T(8,128)(2,1)} %wc_ref.5, bf16[1,1,96,256]{3,2,1,0:T(8,128)(2,1)} %refs_14_.1, f32[1,2,96]{2,1,0:T(2,128)} %refs_16_.1, ...), custom_call_target="tpu_custom_call" | custom-call | tf_op jit(solution)/shard_map/own_block/pallas_call | solution.py:193
  97.0 6.2 %all_gather.48 = bf16[192,256]{1,0:T(8,128)(2,1)S(1)} all-gather(bf16[96,256]{1,0:T(8,128)(2,1)} %own_block.5), channel_id=1, replica_groups={{0,384},{128,256},{1,385},{129,257},{2,386},{130,258},{3,387},{131,259}..., dimensions={0}, use_global_device_ids=true | all-gather | bytes 147456 | tf_op jit(solution)/shard_map/all_gather | solution.py:497
  103.2 21.4 %all_gather.49.g_ref = bf16[1536,256]{1,0:T(8,128)(2,1)S(1)} all-gather(bf16[96,256]{1,0:T(8,128)(2,1)S(1)} %slice.13), channel_id=1, replica_groups=mesh['segment'=4,'chan'=16,'dp'=8] {'chan'}, dimensions={0}, use_global_device_ids=true | all-gather | bytes 835584 | tf_op jit(solution)/shard_map/all_gather | solution.py:497
  124.6 0.0 copy-done
  124.6 0.0 copy-done.8
  124.6 0.0 copy-done.10
  124.6 0.0 copy-done.18
  124.6 3.9 %wide_block.3 = bf16[768,256]{1,0:T(8,128)(2,1)S(1)} custom-call(s32[2]{0:T(128)S(1)} %copy-done.18, bf16[1536,256]{1,0:T(8,128)(2,1)S(1)} %all_gather.49.g_ref, bf16[768,2304]{1,0:T(8,128)(2,1)S(1)} %copy-done, f32[768,256]{1,0:T(8,128)S(1)} %copy-done.8, f32[768,256]{1,0:T(8,128)S(1)} %copy-done.10), custom_call_target="tpu_custom_call" | custom-call | tf_op jit(solution)/shard_map/wide_block/pallas_call | solution.py:306
  128.4 0.0 copy-start.3
  128.5 0.9 copy-done.3
  129.4 2.7 %all_gather.50 = bf16[1536,256]{1,0:T(8,128)(2,1)} all-gather(bf16[768,256]{1,0:T(8,128)(2,1)S(1)} %wide_block.3), channel_id=1, replica_groups={{0,8},{16,24},{32,40},{48,56},{64,72},{80,88},{96,104},{112,120},{1,9},..., dimensions={0}, use_global_device_ids=true | all-gather | bytes 1179648 | tf_op jit(solution)/shard_map/all_gather | solution.py:497
  132.1 8.7 %first_block.3 = (bf16[768,256]{1,0:T(8,128)(2,1)}, f32[768,256]{1,0:T(8,128)}, f32[768,256]{1,0:T(8,128)}) custom-call(s32[2]{0:T(128)} %copy-done.17, bf16[2,8,96,256]{3,2,1,0:T(8,128)(2,1)} %bitcast.28, bf16[768,2304]{1,0:T(8,128)(2,1)} %all-gather.7.cloned.1.call-done.pack_ref), custom_call_target="tpu_custom_call" | custom-call | tf_op jit(solution)/shard_map/first_block/pallas_call | solution.py:258
  140.7 12.3 %all_gather.52 = bf16[1536,256]{1,0:T(8,128)(2,1)S(1)} all-gather(bf16[768,256]{1,0:T(8,128)(2,1)} %get-tuple-element.32), channel_id=1, replica_groups={{0,128},{256,384},{1,129},{257,385},{2,130},{258,386},{3,131},{259,387}..., dimensions={0}, use_global_device_ids=true | all-gather | bytes 1179648 | tf_op jit(solution)/shard_map/all_gather | solution.py:497
  153.0 2.4 all_gather.53.g_ref
  155.4 0.0 copy-done.9
  155.4 0.0 copy-done.11
  155.4 0.0 copy-done.19
  155.4 0.0 copy-start.4
  155.4 3.9 %wide_block.4 = bf16[768,256]{1,0:T(8,128)(2,1)S(1)} custom-call(s32[2]{0:T(128)S(1)} %copy-done.19, bf16[1536,256]{1,0:T(8,128)(2,1)S(1)} %all_gather.53.g_ref, bf16[768,2304]{1,0:T(8,128)(2,1)S(1)} %copy-done, f32[768,256]{1,0:T(8,128)S(1)} %copy-done.9, f32[768,256]{1,0:T(8,128)S(1)} %copy-done.11), custom_call_target="tpu_custom_call" | custom-call | tf_op jit(solution)/shard_map/wide_block/pallas_call | solution.py:306
  159.3 2.4 all_gather.54.g_ref
  161.7 0.0 copy-done.4
  161.7 0.0 copy-done.15
  161.7 3.9 %wide_block.5 = bf16[768,256]{1,0:T(8,128)(2,1)S(1)} custom-call(s32[2]{0:T(128)S(1)} %copy-done.19, bf16[1536,256]{1,0:T(8,128)(2,1)S(1)} %all_gather.54.g_ref, bf16[768,2304]{1,0:T(8,128)(2,1)S(1)} %copy-done.2, f32[768,256]{1,0:T(8,128)S(1)} %copy-done.14, f32[768,256]{1,0:T(8,128)S(1)} %copy-done.15), custom_call_target="tpu_custom_call" | custom-call | tf_op jit(solution)/shard_map/wide_block/pallas_call | solution.py:306
  165.6 2.5 %all_gather.55 = bf16[1536,256]{1,0:T(8,128)(2,1)} all-gather(bf16[768,256]{1,0:T(8,128)(2,1)S(1)} %wide_block.5), channel_id=1, replica_groups={{0,8},{16,24},{32,40},{48,56},{64,72},{80,88},{96,104},{112,120},{1,9},..., dimensions={0}, use_global_device_ids=true | all-gather | bytes 1179648 | tf_op jit(solution)/shard_map/all_gather | solution.py:497
  168.1 0.0 copy-done.5
  168.1 5.7 %weight_grads.1 = (bf16[8,192,256]{2,1,0:T(8,128)(2,1)}, bf16[16,1536]{1,0:T(8,128)(2,1)}) custom-call(s32[2]{0:T(128)} %copy-done.17, bf16[8,2,96,256]{3,2,1,0:T(8,128)(2,1)} %bitcast.24, bf16[2,8,96,256]{3,2,1,0:T(8,128)(2,1)} %bitcast.30, bf16[2,8,96,256]{3,2,1,0:T(8,128)(2,1)} %bitcast.29, bf16[2,8,96,256]{3,2,1,0:T(8,128)(2,1)} %bitcast.21, ...), custom_call_target="tpu_custom_call" | custom-call | tf_op jit(solution)/shard_map/weight_grads/pallas_call | solution.py:424
  173.8 33.2 %all_to_all.10.in_ref = bf16[8,192,256]{2,1,0:T(8,128)(2,1)S(1)} all-to-all(bf16[8,192,256]{2,1,0:T(8,128)(2,1)} %get-tuple-element.36), channel_id=1, replica_groups=mesh['segment'=4,'chan'=16,'dp'=8] {'dp'}, dimensions={0} | all-to-all | bytes 1572864 | tf_op jit(solution)/shard_map/all_to_all | solution.py:522
  207.0 0.1 sum_microbatches.1
  207.1 24.7 %all_to_all.11.in_ref = bf16[8,192,256]{2,1,0:T(8,128)(2,1)S(1)} all-to-all(bf16[8,192,256]{2,1,0:T(8,128)(2,1)S(1)} %sum_microbatches.1), channel_id=1, replica_groups=mesh['segment'=4,'chan'=16,'dp'=8] {'dp'}, dimensions={0} | all-to-all | bytes 1572864 | tf_op jit(solution)/shard_map/all_to_all | solution.py:522
  231.8 1.2 widen.1
  (17 shorter events, 0.1 us)
Async XLA Ops:
  7.2 23.6 %copy-start.21 = (f32[1,2,96]{2,1,0:T(2,128)S(1)}, f32[1,2,96]{2,1,0:T(2,128)}, u32[]{:S(2)}) copy-start(f32[1,2,96]{2,1,0:T(2,128)} %refs_17_.1) | copy-start | bytes 2308
  7.2 23.6 %copy-start.20 = (f32[1,2,96]{2,1,0:T(2,128)S(1)}, f32[1,2,96]{2,1,0:T(2,128)}, u32[]{:S(2)}) copy-start(f32[1,2,96]{2,1,0:T(2,128)} %refs_16_.1) | copy-start | bytes 2308
  7.2 23.6 %copy-start.1 = (bf16[1,2,96,1536]{3,2,1,0:T(8,128)(2,1)S(1)}, bf16[1,2,96,1536]{3,2,1,0:T(8,128)(2,1)}, u32[]{:S(2)}) copy-start(bf16[1,2,96,1536]{3,2,1,0:T(8,128)(2,1)} %refs_13_.1) | copy-start | bytes 1769476
  7.2 23.6 %copy-start.12 = (bf16[1,2,96,432]{3,2,1,0:T(8,128)(2,1)S(1)}, bf16[1,2,96,432]{3,2,1,0:T(8,128)(2,1)}, u32[]{:S(2)}) copy-start(bf16[1,2,96,432]{3,2,1,0:T(8,128)(2,1)} %wc_ref.5) | copy-start | bytes 497668
  7.2 46.4 %copy-start.13 = (bf16[1,1,96,256]{3,2,1,0:T(8,128)(2,1)S(1)}, bf16[1,1,96,256]{3,2,1,0:T(8,128)(2,1)}, u32[]{:S(2)}) copy-start(bf16[1,1,96,256]{3,2,1,0:T(8,128)(2,1)} %refs_14_.1) | copy-start | bytes 147460
  7.2 23.6 %copy-start.16 = (bf16[1,1,96,256]{3,2,1,0:T(8,128)(2,1)S(1)}, bf16[1,1,96,256]{3,2,1,0:T(8,128)(2,1)}, u32[]{:S(2)}) copy-start(bf16[1,1,96,256]{3,2,1,0:T(8,128)(2,1)} %refs_15_.1) | copy-start | bytes 147460
  7.2 73.5 %all-gather.5.cloned.1.call-start = ((), (), s32[]{:S(2)}) async-start(), calls=%async_computation.2 | async-start | bytes 3981312 | tf_op jit(solution)/shard_map/all_gather | solution.py:497
  9.6 122.4 %all-gather.7.cloned.1.call-start = ((), (), s32[]{:S(2)}) async-start(), calls=%async_computation.3 | async-start | bytes 3981312 | tf_op jit(solution)/shard_map/all_gather | solution.py:527
  30.7 50.1 %copy-start.6 = (bf16[1,1536,256]{2,1,0:T(8,128)(2,1)}, bf16[1,1536,256]{2,1,0:T(8,128)(2,1)S(1)}, u32[]{:S(2)}) copy-start(bf16[1,1536,256]{2,1,0:T(8,128)(2,1)S(1)} %copy.15) | copy-start | bytes 2359300
  30.8 50.0 %copy-start.17 = (s32[2]{0:T(128)}, s32[2]{0:T(128)S(1)}, u32[]{:S(2)}) copy-start(s32[2]{0:T(128)S(1)} %pad_add_fusion.flags_ref.refs_0_) | copy-start | bytes 28
  53.6 1.5 copy-start.7
  80.8 43.8 %copy-start = (bf16[768,2304]{1,0:T(8,128)(2,1)S(1)}, bf16[768,2304]{1,0:T(8,128)(2,1)}, u32[]{:S(2)}) copy-start(bf16[768,2304]{1,0:T(8,128)(2,1)} %all-gather.5.cloned.1.call-done.pack_ref) | copy-start | bytes 10616836
  89.7 34.9 %copy-start.8 = (f32[768,256]{1,0:T(8,128)S(1)}, f32[768,256]{1,0:T(8,128)}, u32[]{:S(2)}) copy-start(f32[768,256]{1,0:T(8,128)} %get-tuple-element.27.xhat_ref) | copy-start | bytes 2359300
  89.7 34.8 %copy-start.10 = (f32[768,256]{1,0:T(8,128)S(1)}, f32[768,256]{1,0:T(8,128)}, u32[]{:S(2)}) copy-start(f32[768,256]{1,0:T(8,128)} %get-tuple-element.28.rate_ref) | copy-start | bytes 2359300
  89.7 34.8 %copy-start.18 = (s32[2]{0:T(128)S(1)}, s32[2]{0:T(128)}, u32[]{:S(2)}) copy-start(s32[2]{0:T(128)} %copy-done.17) | copy-start | bytes 28
  128.4 0.9 copy-start.3
  132.0 23.3 %copy-start.9 = (f32[768,256]{1,0:T(8,128)S(1)}, f32[768,256]{1,0:T(8,128)}, u32[]{:S(2)}) copy-start(f32[768,256]{1,0:T(8,128)} %get-tuple-element.27.xhat_ref) | copy-start | bytes 2359300
  132.1 23.3 %copy-start.11 = (f32[768,256]{1,0:T(8,128)S(1)}, f32[768,256]{1,0:T(8,128)}, u32[]{:S(2)}) copy-start(f32[768,256]{1,0:T(8,128)} %get-tuple-element.28.rate_ref) | copy-start | bytes 2359300
  132.1 23.3 %copy-start.19 = (s32[2]{0:T(128)S(1)}, s32[2]{0:T(128)}, u32[]{:S(2)}) copy-start(s32[2]{0:T(128)} %copy-done.17) | copy-start | bytes 28
  155.4 6.3 %copy-start.4 = (bf16[1536,256]{1,0:T(8,128)(2,1)}, bf16[1536,256]{1,0:T(8,128)(2,1)S(1)}, u32[]{:S(2)}) copy-start(bf16[1536,256]{1,0:T(8,128)(2,1)S(1)} %all_gather.53.g_ref) | copy-start | bytes 2359300
  155.4 6.3 %copy-start.2 = (bf16[768,2304]{1,0:T(8,128)(2,1)S(1)}, bf16[768,2304]{1,0:T(8,128)(2,1)}, u32[]{:S(2)}) copy-start(bf16[768,2304]{1,0:T(8,128)(2,1)} %all-gather.7.cloned.1.call-done.pack_ref) | copy-start | bytes 10616836
  155.4 6.3 %copy-start.14 = (f32[768,256]{1,0:T(8,128)S(1)}, f32[768,256]{1,0:T(8,128)}, u32[]{:S(2)}) copy-start(f32[768,256]{1,0:T(8,128)} %get-tuple-element.33.xhat_ref) | copy-start | bytes 2359300
  155.4 6.3 %copy-start.15 = (f32[768,256]{1,0:T(8,128)S(1)}, f32[768,256]{1,0:T(8,128)}, u32[]{:S(2)}) copy-start(f32[768,256]{1,0:T(8,128)} %get-tuple-element.34.rate_ref) | copy-start | bytes 2359300
  161.7 6.4 %copy-start.5 = (bf16[1536,256]{1,0:T(8,128)(2,1)}, bf16[1536,256]{1,0:T(8,128)(2,1)S(1)}, u32[]{:S(2)}) copy-start(bf16[1536,256]{1,0:T(8,128)(2,1)S(1)} %all_gather.54.g_ref) | copy-start | bytes 2359300
Sparse Core Ops, SparseCore 0:
  10.2 61.8 all-gather.4
  74.2 53.3 all-gather.6

commit v6 on v5

--- a/solution.py
+++ b/solution.py
@@ -32,11 +32,19 @@
     return jnp.sum(jnp.sum(block, axis=1, keepdims=True), axis=0, keepdims=True)
 
 
-def norm_group(h, gain, bias):
-    scale = 1.0 / (h.shape[0] * h.shape[1])
-    pre = h.astype(F32)
-    pre = pre - total(pre) * scale
-    inv_std = lax.rsqrt(total(pre * pre) * scale + NORM_EPS)
+def norm_stats(blocks):
+    scale = 1.0 / (blocks[0].shape[0] * blocks[0].shape[1])
+    means = [total(h.astype(F32)) * scale for h in blocks]
+    spreads = []
+    for h, mean in zip(blocks, means):
+        pre = h.astype(F32) - mean
+        spreads.append(lax.rsqrt(total(pre * pre) * scale + NORM_EPS))
+    return list(zip(means, spreads))
+
+
+def norm_group(h, gain, bias, stats=None):
+    mean, inv_std = norm_stats([h])[0] if stats is None else stats
+    pre = h.astype(F32) - mean
     xhat = pre * inv_std
     n = xhat * gain + bias
     sig = jax.nn.sigmoid(n)
@@ -68,14 +76,29 @@
     chans, width = w_ref.shape[2:]
     taps = wc_ref.shape[3]
     lane = lax.broadcasted_iota(jnp.int32, (chans, TAIL - 384), 1)
+    down = lax.broadcasted_iota(jnp.int32, (GS, GS), 0)
+    across = lax.broadcasted_iota(jnp.int32, (GS, GS), 1)
+    same = jnp.where(down == across, 1.0, 0.0).astype(BF16)
     for b, h_ref in ((1, h2_ref), (0, h1_ref)):
         pack_ref = pack_refs[b]
         pack_ref[:, :width] = w_ref[0, b]
-        pack_ref[:, width : width + 384] = wc_ref[0, b, :, :384]
-        last = wc_ref[0, b, :, 384:].astype(F32)
-        last = jnp.concatenate(
-            [last, jnp.zeros((chans, TAIL - taps), F32)], axis=1
-        )
+        turned = []
+        for q in range(0, chans, GS):
+            taps_w = [
+                lax.dot_general(
+                    same,
+                    wc_ref[0, b, q : q + GS, k * GS : (k + 1) * GS],
+                    NT,
+                    preferred_element_type=F32,
+                )
+                for k in range(taps // GS)
+            ]
+            turned.append(
+                jnp.concatenate([*taps_w, jnp.zeros((GS, TAIL - taps), F32)], axis=1)
+            )
+        turned = jnp.concatenate(turned, axis=0)
+        pack_ref[:, width : width + 384] = turned[:, :384].astype(BF16)
+        last = turned[:, 384:]
         at = taps - 384
         for whole in columns_of(gain_ref, bias_ref, b):
             rest = whole
@@ -132,11 +155,15 @@
     return lax.dot_general(pick, g, NT, preferred_element_type=F32).astype(BF16)
 
 
-def gh_of(ga, xhat, rate):
+def gh_means(ga, xhat, rate):
     scale = 1.0 / (ga.shape[0] * ga.shape[1])
     rw = ga * rate
-    gh = rw - total(rw) * scale - xhat * (total(rw * xhat) * scale)
-    return gh.astype(BF16)
+    return total(rw) * scale, total(rw * xhat) * scale
+
+
+def gh_of(ga, xhat, rate, means=None):
+    first, second = gh_means(ga, xhat, rate) if means is None else means
+    return (ga * rate - first - xhat * second).astype(BF16)
 
 
 def conv_back(taps_w, gh, row, col):
@@ -151,6 +178,18 @@
         part = shifted(part, 0, -step_col, row, col)
         branch = part if branch is None else branch + part
     return branch.astype(BF16)
+
+
+def conv_back_stacked(taps_w, gh, row, col, stack):
+    gh = gh.astype(F32)
+    for step_col in (-1, 0, 1):
+        moved = shifted(gh, 0, -step_col, row, col)
+        for step_row in (-1, 0, 1):
+            tap = 3 * (step_row + 1) + step_col + 1
+            stack[tap * GS : (tap + 1) * GS, :] = shifted(
+                moved, -step_row, 0, row, col
+            ).astype(BF16)
+    return jnp.dot(taps_w, stack[...], preferred_element_type=F32).astype(BF16)
 
 
 def in_order(g_buf, g_ref, own_rows):
@@ -213,7 +252,7 @@
 
     def kernel(
         flags_ref, g_ref, pack_ref, out_ref, xhat_out, rate_out,
-        w_ref, taps_ref, h_ref, g_buf, src, xhat_ref, rate_ref, sems,
+        w_ref, taps_ref, h_ref, g_buf, src, xhat_ref, rate_ref, stacks, sems,
     ):
         def copy(i, a, to):
             return pltpu.make_async_copy(a, to, sems.at[i])
@@ -231,6 +270,7 @@
         loads[0].wait()
         loads[1].wait()
         at = 9 * GS - 384
+        stats = norm_stats([h_ref[q : q + GS, :] for q in range(0, chans, GS)])
         for q in range(0, chans, GS):
             rows = slice(q, q + GS)
             side = taps_ref[rows, 384:].astype(F32)
@@ -238,7 +278,7 @@
                 side[:, i : i + 1] + side[:, i + 1 : i + 2] + side[:, i + 2 : i + 3]
                 for i in (at, at + 3)
             )
-            xhat, _, _, slope, inv_std = norm_group(h_ref[rows, :], gain, bias)
+            xhat, _, _, slope, inv_std = norm_group(h_ref[rows, :], gain, bias, stats[q // GS])
             xhat_ref[rows, :] = xhat
             rate_ref[rows, :] = slope * (gain * inv_std)
         stores = [copy(5, xhat_ref, xhat_out), copy(6, rate_ref, rate_out)]
@@ -249,7 +289,7 @@
         src[...] = g_buf[...].reshape(whole, positions)
         wide_body(
             flags_ref, src, w_ref[...], lambda rows: taps_ref[rows, : 9 * GS],
-            xhat_ref, rate_ref, out_ref, own_rows,
+            xhat_ref, rate_ref, out_ref, own_rows, stacks,
         )
         for store in stores:
             store.wait()
@@ -268,6 +308,7 @@
             pltpu.VMEM((whole, positions), BF16),
             pltpu.VMEM((chans, positions), F32),
             pltpu.VMEM((chans, positions), F32),
+            pltpu.VMEM((4, 9 * GS, positions), BF16),
             pltpu.SemaphoreType.DMA((7,)),
         ],
         compiler_params=vmem(56),
@@ -275,16 +316,21 @@
     )(flags, g, pack)
 
 
-def wide_body(flags_ref, src, matrix, taps_of, xhat_ref, rate_ref, out_ref, own_rows):
+def wide_body(flags_ref, src, matrix, taps_of, xhat_ref, rate_ref, out_ref, own_rows, stacks):
     chans, positions = xhat_ref.shape
     ga = jnp.dot(matrix, src[...], preferred_element_type=F32)
     core = flags_ref[1] & 1
     row, col = grid_of((GS, positions))
+    means = [
+        gh_means(ga[at : at + GS, :], xhat_ref[at : at + GS, :], rate_ref[at : at + GS, :])
+        for at in range(0, chans, GS)
+    ]
     for at in range(0, chans, GS):
         y, q = divmod(at, own_rows)
         rows = slice(at, at + GS)
-        gh = gh_of(ga[rows, :], xhat_ref[rows, :], rate_ref[rows, :])
-        branch = conv_back(taps_of(rows), gh, row, col)
+        gh = gh_of(ga[rows, :], xhat_ref[rows, :], rate_ref[rows, :], means[at // GS])
+        stack = stacks.at[at // GS % stacks.shape[0]]
+        branch = conv_back_stacked(taps_of(rows), gh, row, col, stack)
         add_branch(out_ref, rows, src, (2 * y + core) * own_rows + q, branch)
 
 
@@ -292,7 +338,7 @@
     whole, positions = g.shape
     chans = pack.shape[0]
 
-    def kernel(flags_ref, g_ref, pack_ref, xhat_ref, rate_ref, out_ref, g_buf):
+    def kernel(flags_ref, g_ref, pack_ref, xhat_ref, rate_ref, out_ref, g_buf, stacks):
         src = g_ref
         if not ordered:
             in_order(g_buf, g_ref, own_rows)
@@ -300,7 +346,7 @@
         wide_body(
             flags_ref, src, pack_ref[:, :whole],
             lambda rows: pack_ref[rows, whole : whole + 9 * GS],
-            xhat_ref, rate_ref, out_ref, own_rows,
+            xhat_ref, rate_ref, out_ref, own_rows, stacks,
         )
 
     return pl.pallas_call(
@@ -308,7 +354,10 @@
         out_shape=shape_of((chans, positions), BF16),
         in_specs=[SMEM] + [VMEM] * 4,
         out_specs=VMEM,
-        scratch_shapes=[pltpu.VMEM((16, 128) if ordered else (whole, positions), BF16)],
+        scratch_shapes=[
+            pltpu.VMEM((16, 128) if ordered else (whole, positions), BF16),
+            pltpu.VMEM((4, 9 * GS, positions), BF16),
+        ],
         compiler_params=vmem(14),
         name="wide_block",
     )(flags, g, pack, *state)
@@ -354,8 +403,8 @@
     def kernel(*refs):
         flags_ref = refs[0]
         fetched = refs[1 : 1 + len(operands)]
-        w_ref, h1_ref, h2_ref, gain_ref, bias_ref, *x_refs = refs[1 + len(operands) : -6]
-        out_ref, lat_ref, stacks, g_bufs, g_flat, sems = refs[-6:]
+        w_ref, h1_ref, h2_ref, gain_ref, bias_ref, *x_refs = refs[1 + len(operands) : -5]
+        out_ref, lat_ref, stacks, g_bufs, sems = refs[-5:]
         segment_at, chan_at = flags_ref[0], flags_ref[1]
 
         def copies(t):
@@ -396,8 +445,8 @@
         each(lambda made: made.wait())
         store = storer(out_ref)
         for b, h_ref in enumerate((h1_ref, h2_ref)):
-            g_flat[...] = g_bufs[b].reshape(width, positions)
-            ga = jnp.dot(w_ref[0, b], g_flat[...], preferred_element_type=F32)
+            g = g_bufs[b].reshape(width, positions)
+            ga = jnp.dot(w_ref[0, b], g, preferred_element_type=F32)
             gains, biases = columns_of(gain_ref, bias_ref, b)
             acts = []
             for q in range(0, chans, GS):
@@ -417,7 +466,7 @@
                 taps = jnp.where(lane == 9 * GS + 1, by_bias, taps)
                 store(b * chans + q, width, taps.astype(BF16))
             act = jnp.concatenate(acts, axis=0)
-            proj = lax.dot_general(act, g_flat[...], NT, preferred_element_type=F32)
+            proj = lax.dot_general(act, g, NT, preferred_element_type=F32)
             store(b * chans, 0, proj.astype(BF16))
         lat_ref[...] = own_positions(g_bufs[2].reshape(width, positions), chan_at, slab)
 
@@ -432,7 +481,6 @@
         scratch_shapes=[
             pltpu.VMEM((2, chans // GS, TAIL, positions), BF16),
             pltpu.VMEM((3, pairs, 2, chans, positions), BF16),
-            pltpu.VMEM((width, positions), BF16),
             pltpu.SemaphoreType.DMA((6,)),
         ],
         compiler_params=vmem(56),

time: 240 us -> 237 us (0.988)
  Pallas kernels: 44.3 us -> 40.8 us
  transfers between devices with their start and end apart: 2 -> 2, of which waited for: 0 -> 0; matrix products, arithmetic and copies ran while one was open for 0% -> 0% of each run, Pallas kernels for 8% -> 7%
where the time goes in v6:
time: 237 us; the launch traced here: 236 us
  blocking collectives  179 us (76%)
  Pallas kernels  40.8 us (17%)
  between operations  14.3 us (6%)
    all_gather x11, blocking collectives, gather(): lax.all_gather(block_, axis, axis=0, tiled=True, axis_index_groups=groups)  101 us
    all_to_all x2, blocking collectives, exchange(): return lax.all_to_all(blocks, 'dp', split_axis=0, concat_axis=0, tiled=True)  58.5 us
    all_gather x1, blocking collectives, per_device(): g = lax.all_gather(grad_top[0], 'chan', axis=1, tiled=True)  20 us
    pallas_call x2, Pallas kernels, first_block(): pl.pallas_call(kernel, out_shape=(shape_of((chans, positions), BF16), ful...  15.3 us
    pallas_call x3, Pallas kernels, wide_block(): pl.pallas_call(kernel, out_shape=shape_of((chans, positions), BF16), in_s...  10 us
    pallas_call x3, Pallas kernels, own_block(): pl.pallas_call(kernel, out_shape=shape_of((chans, positions), BF16), grid...  5.84 us
    pallas_call x1, Pallas kernels, weight_grads(): pl.pallas_call(kernel, out_shape=(shape_of((members, 2 * chans, step), BF...  5.69 us
  transfers between devices with their start and end apart: 2, of which 0 were waited for; matrix products, arithmetic and copies ran while one was open for 0% of the time, Pallas kernels for 7%

profile of v6, /device:TPU:6, one launch (start us, length us, event | category | flops | bytes accessed | tf_op | source)
XLA Modules:
  0.0 236.5 jit_solution(5777735030956760723)
XLA Ops:
  7.2 0.0 copy-start.21
  7.2 0.0 copy-start.20
  7.2 0.0 copy-start.1
  7.2 0.0 copy-start.12
  7.2 0.0 copy-start.13
  7.2 0.0 copy-start.16
  7.2 0.0 all-gather.5.cloned.1.call-start
  7.3 2.7 %prepare.1 = (bf16[96,2304]{1,0:T(8,128)(2,1)}, bf16[96,2304]{1,0:T(8,128)(2,1)}) custom-call(bf16[1,2,96,1536]{3,2,1,0:T(8,128)(2,1)} %refs_13_.1, bf16[1,2,96,432]{3,2,1,0:T(8,128)(2,1)} %wc_ref.5, bf16[1,1,96,256]{3,2,1,0:T(8,128)(2,1)} %refs_14_.1, bf16[1,1,96,256]{3,2,1,0:T(8,128)(2,1)} %refs_15_.1, f32[1,2,96]{2,1,0:T(2,128)} %refs_16_.1, ...), custom_call_target="tpu_custom_call" | custom-call | tf_op jit(solution)/shard_map/prepare/pallas_call | solution.py:118
  10.0 0.0 all-gather.5.cloned.1.call-update
  10.0 0.0 all-gather.7.cloned.1.call-start
  10.0 0.7 all-gather.7.cloned.1.call-update
  10.7 20.0 %all-gather = bf16[1,1536,256]{1,2,0:T(8,128)(2,1)S(1)} all-gather(bf16[1,1536,16]{1,2,0:T(8,128)(2,1)} %param.9), channel_id=2, replica_groups=mesh['segment'=4,'chan'=16,'dp'=8] {'chan'}, dimensions={2}, use_global_device_ids=true | all-gather | bytes 835584 | tf_op jit(solution)/shard_map/all_gather | solution.py:585
  30.7 0.3 copy.15
  31.0 0.0 copy-start.6
  31.0 0.1 pad_add_fusion.flags_ref.refs_0_
  31.1 0.0 copy-done.21
  31.1 0.0 copy-done.20
  31.1 0.0 copy-done.1
  31.1 0.0 copy-done.12
  31.1 0.0 copy-done.16
  31.1 1.5 own_block.3
  32.6 21.6 %all_gather.43.g_ref = bf16[1536,256]{1,0:T(8,128)(2,1)S(1)} all-gather(bf16[96,256]{1,0:T(8,128)(2,1)S(1)} %own_block.3), channel_id=1, replica_groups=mesh['segment'=4,'chan'=16,'dp'=8] {'chan'}, dimensions={0}, use_global_device_ids=true | all-gather | bytes 835584 | tf_op jit(solution)/shard_map/all_gather | solution.py:545
  54.2 0.0 copy-done.13
  54.2 1.5 own_block.4
  55.7 0.0 copy-done.7
  55.7 4.8 %all_gather.45 = bf16[192,256]{1,0:T(8,128)(2,1)S(1)} all-gather(bf16[96,256]{1,0:T(8,128)(2,1)S(1)} %own_block.4), channel_id=1, replica_groups={{0,128},{256,384},{1,129},{257,385},{2,130},{258,386},{3,131},{259,387}..., dimensions={0}, use_global_device_ids=true | all-gather | bytes 147456 | tf_op jit(solution)/shard_map/all_gather | solution.py:545
  60.5 20.3 %all_gather.46 = bf16[1536,256]{1,0:T(8,128)(2,1)} all-gather(bf16[96,256]{1,0:T(8,128)(2,1)S(1)} %slice.12), channel_id=1, replica_groups=mesh['segment'=4,'chan'=16,'dp'=8] {'chan'}, dimensions={0}, use_global_device_ids=true | all-gather | bytes 835584 | tf_op jit(solution)/shard_map/all_gather | solution.py:545
  80.8 0.0 copy-done.6
  80.8 0.0 copy-done.17
  80.8 7.8 %first_block.2 = (bf16[768,256]{1,0:T(8,128)(2,1)}, f32[768,256]{1,0:T(8,128)}, f32[768,256]{1,0:T(8,128)}) custom-call(s32[2]{0:T(128)} %copy-done.17, bf16[8,2,96,256]{3,2,1,0:T(8,128)(2,1)} %bitcast.25, bf16[768,2304]{1,0:T(8,128)(2,1)} %all-gather.5.cloned.1.call-done.pack_ref), custom_call_target="tpu_custom_call" | custom-call | tf_op jit(solution)/shard_map/first_block/pallas_call | solution.py:298
  88.6 0.0 copy-start.8
  88.6 0.0 copy-start.10
  88.6 0.0 copy-start.18
  88.6 4.4 %all_gather.47.g_ref = bf16[1536,256]{1,0:T(8,128)(2,1)} all-gather(bf16[768,256]{1,0:T(8,128)(2,1)} %get-tuple-element.26), channel_id=1, replica_groups={{0,8},{16,24},{32,40},{48,56},{64,72},{80,88},{96,104},{112,120},{1,9},..., dimensions={0}, use_global_device_ids=true | all-gather | bytes 1179648 | tf_op jit(solution)/shard_map/all_gather | solution.py:545
  93.0 2.9 %own_block.5 = bf16[96,256]{1,0:T(8,128)(2,1)} custom-call(s32[2]{0:T(128)} %copy-done.17, bf16[1536,256]{1,0:T(8,128)(2,1)} %all_gather.47.g_ref, bf16[1,2,96,1536]{3,2,1,0:T(8,128)(2,1)} %refs_13_.1, bf16[1,2,96,432]{3,2,1,0:T(8,128)(2,1)} %wc_ref.5, bf16[1,1,96,256]{3,2,1,0:T(8,128)(2,1)} %refs_14_.1, f32[1,2,96]{2,1,0:T(2,128)} %refs_16_.1, ...), custom_call_target="tpu_custom_call" | custom-call | tf_op jit(solution)/shard_map/own_block/pallas_call | solution.py:232
  95.9 6.2 %all_gather.48 = bf16[192,256]{1,0:T(8,128)(2,1)S(1)} all-gather(bf16[96,256]{1,0:T(8,128)(2,1)} %own_block.5), channel_id=1, replica_groups={{0,384},{128,256},{1,385},{129,257},{2,386},{130,258},{3,387},{131,259}..., dimensions={0}, use_global_device_ids=true | all-gather | bytes 147456 | tf_op jit(solution)/shard_map/all_gather | solution.py:545
  102.1 21.3 %all_gather.49.g_ref = bf16[1536,256]{1,0:T(8,128)(2,1)S(1)} all-gather(bf16[96,256]{1,0:T(8,128)(2,1)S(1)} %slice.13), channel_id=1, replica_groups=mesh['segment'=4,'chan'=16,'dp'=8] {'chan'}, dimensions={0}, use_global_device_ids=true | all-gather | bytes 835584 | tf_op jit(solution)/shard_map/all_gather | solution.py:545
  123.4 0.0 copy-done
  123.4 0.0 copy-done.8
  123.4 0.0 copy-done.10
  123.4 0.0 copy-done.18
  123.4 3.3 %wide_block.3 = bf16[768,256]{1,0:T(8,128)(2,1)S(1)} custom-call(s32[2]{0:T(128)S(1)} %copy-done.18, bf16[1536,256]{1,0:T(8,128)(2,1)S(1)} %all_gather.49.g_ref, bf16[768,2304]{1,0:T(8,128)(2,1)S(1)} %copy-done, f32[768,256]{1,0:T(8,128)S(1)} %copy-done.8, f32[768,256]{1,0:T(8,128)S(1)} %copy-done.10), custom_call_target="tpu_custom_call" | custom-call | tf_op jit(solution)/shard_map/wide_block/pallas_call | solution.py:352
  126.8 0.0 copy-start.3
  126.8 0.9 copy-done.3
  127.7 2.7 %all_gather.50 = bf16[1536,256]{1,0:T(8,128)(2,1)} all-gather(bf16[768,256]{1,0:T(8,128)(2,1)S(1)} %wide_block.3), channel_id=1, replica_groups={{0,8},{16,24},{32,40},{48,56},{64,72},{80,88},{96,104},{112,120},{1,9},..., dimensions={0}, use_global_device_ids=true | all-gather | bytes 1179648 | tf_op jit(solution)/shard_map/all_gather | solution.py:545
  130.4 7.5 %first_block.3 = (bf16[768,256]{1,0:T(8,128)(2,1)}, f32[768,256]{1,0:T(8,128)}, f32[768,256]{1,0:T(8,128)}) custom-call(s32[2]{0:T(128)} %copy-done.17, bf16[2,8,96,256]{3,2,1,0:T(8,128)(2,1)} %bitcast.28, bf16[768,2304]{1,0:T(8,128)(2,1)} %all-gather.7.cloned.1.call-done.pack_ref), custom_call_target="tpu_custom_call" | custom-call | tf_op jit(solution)/shard_map/first_block/pallas_call | solution.py:298
  137.9 12.3 %all_gather.52 = bf16[1536,256]{1,0:T(8,128)(2,1)S(1)} all-gather(bf16[768,256]{1,0:T(8,128)(2,1)} %get-tuple-element.32), channel_id=1, replica_groups={{0,128},{256,384},{1,129},{257,385},{2,130},{258,386},{3,131},{259,387}..., dimensions={0}, use_global_device_ids=true | all-gather | bytes 1179648 | tf_op jit(solution)/shard_map/all_gather | solution.py:545
  150.2 2.4 %all_gather.53.g_ref = bf16[1536,256]{1,0:T(8,128)(2,1)S(1)} all-gather(bf16[768,256]{1,0:T(8,128)(2,1)S(1)} %slice.14), channel_id=1, replica_groups={{0,8},{16,24},{32,40},{48,56},{64,72},{80,88},{96,104},{112,120},{1,9},..., dimensions={0}, use_global_device_ids=true | all-gather | bytes 1179648 | tf_op jit(solution)/shard_map/all_gather | solution.py:545
  152.5 0.0 copy-done.9
  152.6 0.0 copy-done.19
  152.6 0.0 copy-start.4
  152.6 0.0 copy-start.2
  152.6 0.0 copy-start.14
  152.6 0.0 copy-start.15
  152.6 3.3 %wide_block.4 = bf16[768,256]{1,0:T(8,128)(2,1)S(1)} custom-call(s32[2]{0:T(128)S(1)} %copy-done.19, bf16[1536,256]{1,0:T(8,128)(2,1)S(1)} %all_gather.53.g_ref, bf16[768,2304]{1,0:T(8,128)(2,1)S(1)} %copy-done, f32[768,256]{1,0:T(8,128)S(1)} %copy-done.9, f32[768,256]{1,0:T(8,128)S(1)} %copy-done.11), custom_call_target="tpu_custom_call" | custom-call | tf_op jit(solution)/shard_map/wide_block/pallas_call | solution.py:352
  155.9 2.4 %all_gather.54.g_ref = bf16[1536,256]{1,0:T(8,128)(2,1)S(1)} all-gather(bf16[768,256]{1,0:T(8,128)(2,1)S(1)} %wide_block.4), channel_id=1, replica_groups={{0,8},{16,24},{32,40},{48,56},{64,72},{80,88},{96,104},{112,120},{1,9},..., dimensions={0}, use_global_device_ids=true | all-gather | bytes 1179648 | tf_op jit(solution)/shard_map/all_gather | solution.py:545
  158.3 0.0 copy-done.14
  158.3 3.4 %wide_block.5 = bf16[768,256]{1,0:T(8,128)(2,1)S(1)} custom-call(s32[2]{0:T(128)S(1)} %copy-done.19, bf16[1536,256]{1,0:T(8,128)(2,1)S(1)} %all_gather.54.g_ref, bf16[768,2304]{1,0:T(8,128)(2,1)S(1)} %copy-done.2, f32[768,256]{1,0:T(8,128)S(1)} %copy-done.14, f32[768,256]{1,0:T(8,128)S(1)} %copy-done.15), custom_call_target="tpu_custom_call" | custom-call | tf_op jit(solution)/shard_map/wide_block/pallas_call | solution.py:352
  161.7 2.5 %all_gather.55 = bf16[1536,256]{1,0:T(8,128)(2,1)} all-gather(bf16[768,256]{1,0:T(8,128)(2,1)S(1)} %wide_block.5), channel_id=1, replica_groups={{0,8},{16,24},{32,40},{48,56},{64,72},{80,88},{96,104},{112,120},{1,9},..., dimensions={0}, use_global_device_ids=true | all-gather | bytes 1179648 | tf_op jit(solution)/shard_map/all_gather | solution.py:545
  164.2 5.7 %weight_grads.1 = (bf16[8,192,256]{2,1,0:T(8,128)(2,1)}, bf16[16,1536]{1,0:T(8,128)(2,1)}) custom-call(s32[2]{0:T(128)} %copy-done.17, bf16[8,2,96,256]{3,2,1,0:T(8,128)(2,1)} %bitcast.24, bf16[2,8,96,256]{3,2,1,0:T(8,128)(2,1)} %bitcast.30, bf16[2,8,96,256]{3,2,1,0:T(8,128)(2,1)} %bitcast.29, bf16[2,8,96,256]{3,2,1,0:T(8,128)(2,1)} %bitcast.21, ...), custom_call_target="tpu_custom_call" | custom-call | tf_op jit(solution)/shard_map/weight_grads/pallas_call | solution.py:473
  169.9 33.7 %all_to_all.10.in_ref = bf16[8,192,256]{2,1,0:T(8,128)(2,1)S(1)} all-to-all(bf16[8,192,256]{2,1,0:T(8,128)(2,1)} %get-tuple-element.36), channel_id=1, replica_groups=mesh['segment'=4,'chan'=16,'dp'=8] {'dp'}, dimensions={0} | all-to-all | bytes 1572864 | tf_op jit(solution)/shard_map/all_to_all | solution.py:570
  203.6 0.1 sum_microbatches.1
  203.7 24.7 %all_to_all.11.in_ref = bf16[8,192,256]{2,1,0:T(8,128)(2,1)S(1)} all-to-all(bf16[8,192,256]{2,1,0:T(8,128)(2,1)S(1)} %sum_microbatches.1), channel_id=1, replica_groups=mesh['segment'=4,'chan'=16,'dp'=8] {'dp'}, dimensions={0} | all-to-all | bytes 1572864 | tf_op jit(solution)/shard_map/all_to_all | solution.py:570
  228.5 1.2 widen.1
  (17 shorter events, 0.1 us)
Async XLA Ops:
  7.2 23.9 %copy-start.21 = (f32[1,2,96]{2,1,0:T(2,128)S(1)}, f32[1,2,96]{2,1,0:T(2,128)}, u32[]{:S(2)}) copy-start(f32[1,2,96]{2,1,0:T(2,128)} %refs_17_.1) | copy-start | bytes 2308
  7.2 23.9 %copy-start.20 = (f32[1,2,96]{2,1,0:T(2,128)S(1)}, f32[1,2,96]{2,1,0:T(2,128)}, u32[]{:S(2)}) copy-start(f32[1,2,96]{2,1,0:T(2,128)} %refs_16_.1) | copy-start | bytes 2308
  7.2 23.9 %copy-start.1 = (bf16[1,2,96,1536]{3,2,1,0:T(8,128)(2,1)S(1)}, bf16[1,2,96,1536]{3,2,1,0:T(8,128)(2,1)}, u32[]{:S(2)}) copy-start(bf16[1,2,96,1536]{3,2,1,0:T(8,128)(2,1)} %refs_13_.1) | copy-start | bytes 1769476
  7.2 23.9 %copy-start.12 = (bf16[1,2,96,432]{3,2,1,0:T(8,128)(2,1)S(1)}, bf16[1,2,96,432]{3,2,1,0:T(8,128)(2,1)}, u32[]{:S(2)}) copy-start(bf16[1,2,96,432]{3,2,1,0:T(8,128)(2,1)} %wc_ref.5) | copy-start | bytes 497668
  7.2 47.0 %copy-start.13 = (bf16[1,1,96,256]{3,2,1,0:T(8,128)(2,1)S(1)}, bf16[1,1,96,256]{3,2,1,0:T(8,128)(2,1)}, u32[]{:S(2)}) copy-start(bf16[1,1,96,256]{3,2,1,0:T(8,128)(2,1)} %refs_14_.1) | copy-start | bytes 147460
  7.2 23.9 %copy-start.16 = (bf16[1,1,96,256]{3,2,1,0:T(8,128)(2,1)S(1)}, bf16[1,1,96,256]{3,2,1,0:T(8,128)(2,1)}, u32[]{:S(2)}) copy-start(bf16[1,1,96,256]{3,2,1,0:T(8,128)(2,1)} %refs_15_.1) | copy-start | bytes 147460
  7.2 73.5 %all-gather.5.cloned.1.call-start = ((), (), s32[]{:S(2)}) async-start(), calls=%async_computation.2 | async-start | bytes 3981312 | tf_op jit(solution)/shard_map/all_gather | solution.py:545
  10.0 120.4 %all-gather.7.cloned.1.call-start = ((), (), s32[]{:S(2)}) async-start(), calls=%async_computation.3 | async-start | bytes 3981312 | tf_op jit(solution)/shard_map/all_gather | solution.py:575
  31.0 49.8 %copy-start.6 = (bf16[1,1536,256]{2,1,0:T(8,128)(2,1)}, bf16[1,1536,256]{2,1,0:T(8,128)(2,1)S(1)}, u32[]{:S(2)}) copy-start(bf16[1,1536,256]{2,1,0:T(8,128)(2,1)S(1)} %copy.15) | copy-start | bytes 2359300
  31.1 49.7 %copy-start.17 = (s32[2]{0:T(128)}, s32[2]{0:T(128)S(1)}, u32[]{:S(2)}) copy-start(s32[2]{0:T(128)S(1)} %pad_add_fusion.flags_ref.refs_0_) | copy-start | bytes 28
  54.2 1.5 copy-start.7
  80.8 42.6 %copy-start = (bf16[768,2304]{1,0:T(8,128)(2,1)S(1)}, bf16[768,2304]{1,0:T(8,128)(2,1)}, u32[]{:S(2)}) copy-start(bf16[768,2304]{1,0:T(8,128)(2,1)} %all-gather.5.cloned.1.call-done.pack_ref) | copy-start | bytes 10616836
  88.6 34.9 %copy-start.8 = (f32[768,256]{1,0:T(8,128)S(1)}, f32[768,256]{1,0:T(8,128)}, u32[]{:S(2)}) copy-start(f32[768,256]{1,0:T(8,128)} %get-tuple-element.27.xhat_ref) | copy-start | bytes 2359300
  88.6 34.8 %copy-start.10 = (f32[768,256]{1,0:T(8,128)S(1)}, f32[768,256]{1,0:T(8,128)}, u32[]{:S(2)}) copy-start(f32[768,256]{1,0:T(8,128)} %get-tuple-element.28.rate_ref) | copy-start | bytes 2359300
  88.6 34.8 %copy-start.18 = (s32[2]{0:T(128)S(1)}, s32[2]{0:T(128)}, u32[]{:S(2)}) copy-start(s32[2]{0:T(128)} %copy-done.17) | copy-start | bytes 28
  126.8 0.9 copy-start.3
  130.4 22.2 %copy-start.9 = (f32[768,256]{1,0:T(8,128)S(1)}, f32[768,256]{1,0:T(8,128)}, u32[]{:S(2)}) copy-start(f32[768,256]{1,0:T(8,128)} %get-tuple-element.27.xhat_ref) | copy-start | bytes 2359300
  130.4 22.2 %copy-start.11 = (f32[768,256]{1,0:T(8,128)S(1)}, f32[768,256]{1,0:T(8,128)}, u32[]{:S(2)}) copy-start(f32[768,256]{1,0:T(8,128)} %get-tuple-element.28.rate_ref) | copy-start | bytes 2359300
  130.4 22.2 %copy-start.19 = (s32[2]{0:T(128)S(1)}, s32[2]{0:T(128)}, u32[]{:S(2)}) copy-start(s32[2]{0:T(128)} %copy-done.17) | copy-start | bytes 28
  152.6 5.7 %copy-start.4 = (bf16[1536,256]{1,0:T(8,128)(2,1)}, bf16[1536,256]{1,0:T(8,128)(2,1)S(1)}, u32[]{:S(2)}) copy-start(bf16[1536,256]{1,0:T(8,128)(2,1)S(1)} %all_gather.53.g_ref) | copy-start | bytes 2359300
  152.6 5.7 %copy-start.2 = (bf16[768,2304]{1,0:T(8,128)(2,1)S(1)}, bf16[768,2304]{1,0:T(8,128)(2,1)}, u32[]{:S(2)}) copy-start(bf16[768,2304]{1,0:T(8,128)(2,1)} %all-gather.7.cloned.1.call-done.pack_ref) | copy-start | bytes 10616836
  152.6 5.7 %copy-start.14 = (f32[768,256]{1,0:T(8,128)S(1)}, f32[768,256]{1,0:T(8,128)}, u32[]{:S(2)}) copy-start(f32[768,256]{1,0:T(8,128)} %get-tuple-element.33.xhat_ref) | copy-start | bytes 2359300
  152.6 5.7 %copy-start.15 = (f32[768,256]{1,0:T(8,128)S(1)}, f32[768,256]{1,0:T(8,128)}, u32[]{:S(2)}) copy-start(f32[768,256]{1,0:T(8,128)} %get-tuple-element.34.rate_ref) | copy-start | bytes 2359300
  158.3 5.9 %copy-start.5 = (bf16[1536,256]{1,0:T(8,128)(2,1)}, bf16[1536,256]{1,0:T(8,128)(2,1)S(1)}, u32[]{:S(2)}) copy-start(bf16[1536,256]{1,0:T(8,128)(2,1)S(1)} %all_gather.54.g_ref) | copy-start | bytes 2359300
Sparse Core Ops, SparseCore 0:
  10.2 61.7 all-gather.4
  74.0 53.8 all-gather.6

commit v7 on v6

--- a/solution.py
+++ b/solution.py
@@ -237,7 +237,7 @@
         + [VMEM] * 3,
         out_specs=VMEM,
         scratch_shapes=[pltpu.VMEM((16, 128) if ordered else (whole, positions), BF16)],
-        compiler_params=vmem(56 if alone else 8),
+        compiler_params=vmem(8 if alone else 8),
         name="own_block",
     )(flags, g, *params)
 
@@ -311,7 +311,7 @@
             pltpu.VMEM((4, 9 * GS, positions), BF16),
             pltpu.SemaphoreType.DMA((7,)),
         ],
-        compiler_params=vmem(56),
+        compiler_params=vmem(40),
         name="first_block",
     )(flags, g, pack)
 
@@ -403,8 +403,8 @@
     def kernel(*refs):
         flags_ref = refs[0]
         fetched = refs[1 : 1 + len(operands)]
-        w_ref, h1_ref, h2_ref, gain_ref, bias_ref, *x_refs = refs[1 + len(operands) : -5]
-        out_ref, lat_ref, stacks, g_bufs, sems = refs[-5:]
+        w_ref, h1_ref, h2_ref, gain_ref, bias_ref, *x_refs = refs[1 + len(operands) : -7]
+        out_ref, lat_ref, stacks, g_bufs, kept_ref, act_ref, sems = refs[-7:]
         segment_at, chan_at = flags_ref[0], flags_ref[1]
 
         def copies(t):
@@ -421,12 +421,12 @@
                     )
             return made
 
-        def each(act):
+        def each(act, only=slice(None)):
             for t in range(ticks):
 
                 @pl.when(segment_at == ticks - 1 - t)
                 def _():
-                    for made in copies(t):
+                    for made in copies(t)[only]:
                         act(made)
 
         each(lambda made: made.start())
@@ -442,32 +442,39 @@
                             x, step_row, step_col, row, col
                         ).astype(BF16)
                 stacks[b, q // GS, 9 * GS :, :] = jnp.zeros((TAIL - 9 * GS, positions), BF16)
-        each(lambda made: made.wait())
+        norms = []
+        for b, h_ref in enumerate((h1_ref, h2_ref)):
+            gains, biases = columns_of(gain_ref, bias_ref, b)
+            blocks = [h_ref[0, 0, q : q + GS, :] for q in range(0, chans, GS)]
+            stats = norm_stats(blocks)
+            for i, h in enumerate(blocks):
+                rows = slice(i * GS, (i + 1) * GS)
+                xhat, n, sig, slope, inv_std = norm_group(h, gains[rows], biases[rows], stats[i])
+                kept_ref[0, b, rows, :] = xhat
+                kept_ref[1, b, rows, :] = slope
+                kept_ref[2, b, rows, :] = slope * (gains[rows] * inv_std)
+                act_ref[b, rows, :] = (n * sig).astype(BF16)
         store = storer(out_ref)
-        for b, h_ref in enumerate((h1_ref, h2_ref)):
+        for b in range(2):
+            each(lambda made: made.wait(), slice(2 * b, 2 * b + 2))
             g = g_bufs[b].reshape(width, positions)
             ga = jnp.dot(w_ref[0, b], g, preferred_element_type=F32)
-            gains, biases = columns_of(gain_ref, bias_ref, b)
-            acts = []
+            proj = lax.dot_general(act_ref[b], g, NT, preferred_element_type=F32)
+            store(b * chans, 0, proj.astype(BF16))
             for q in range(0, chans, GS):
                 rows = slice(q, q + GS)
-                xhat, n, sig, slope, inv_std = norm_group(
-                    h_ref[0, 0, rows, :], gains[rows], biases[rows]
-                )
-                acts.append((n * sig).astype(BF16))
-                gh = gh_of(ga[rows, :], xhat, slope * (gains[rows] * inv_std))
+                xhat = kept_ref[0, b, rows, :]
+                gh = gh_of(ga[rows, :], xhat, kept_ref[2, b, rows, :])
                 taps = lax.dot_general(
                     gh, stacks[b, q // GS], NT, preferred_element_type=F32
                 )
-                gn = ga[rows, :] * slope
+                gn = ga[rows, :] * kept_ref[1, b, rows, :]
                 by_gain = jnp.sum(gn * xhat, axis=1, keepdims=True)
                 by_bias = jnp.sum(gn, axis=1, keepdims=True)
                 taps = jnp.where(lane == 9 * GS, by_gain, taps)
                 taps = jnp.where(lane == 9 * GS + 1, by_bias, taps)
                 store(b * chans + q, width, taps.astype(BF16))
-            act = jnp.concatenate(acts, axis=0)
-            proj = lax.dot_general(act, g, NT, preferred_element_type=F32)
-            store(b * chans, 0, proj.astype(BF16))
+        each(lambda made: made.wait(), slice(4, 6))
         lat_ref[...] = own_positions(g_bufs[2].reshape(width, positions), chan_at, slab)
 
     return pl.pallas_call(
@@ -481,6 +488,8 @@
         scratch_shapes=[
             pltpu.VMEM((2, chans // GS, TAIL, positions), BF16),
             pltpu.VMEM((3, pairs, 2, chans, positions), BF16),
+            pltpu.VMEM((3, 2, chans, positions), F32),
+            pltpu.VMEM((2, chans, positions), BF16),
             pltpu.SemaphoreType.DMA((6,)),
         ],
         compiler_params=vmem(56),

time: 237 us -> 231 us (0.975)
  Pallas kernels: 40.8 us -> 34.4 us
  blocking collectives: 179 us -> 173 us
  local copies, waits for them, and re-layouts: 1.32 us -> 4.68 us
  waiting for transfers between devices: 0.71 us -> 3.73 us
    all_gather x11, blocking collectives: 101 us -> 96.6 us  [gather(): lax.all_gather(block_, axis, axis=0, tiled=True, axis_index_groups=groups)]
    pallas_call x2, Pallas kernels: 15.3 us -> 11.4 us  [first_block(): pl.pallas_call(kernel, out_shape=(shape_of((chans, positions), BF16), ful...]
    unnamed x44, local copies, waits for them, and re-layouts: 1.02 us -> 4.37 us
    all_gather x1, waiting for transfers between devices: 0.01 us -> 3.02 us  [per_device(): lax.all_gather(first_pack[None], 'chan', axis=1, tiled=True, axis_index_g...]
  transfers between devices with their start and end apart: 2 -> 2, of which waited for: 0 -> 1; matrix products, arithmetic and copies ran while one was open for 0% -> 0% of each run, Pallas kernels for 7% -> 6%
where the time goes in v7:
time: 231 us; the launch traced here: 230 us
  blocking collectives  173 us (75%)
  Pallas kernels  34.4 us (15%)
  between operations  14.3 us (6%)
  local copies, waits for them, and re-layouts  4.68 us (2%)
  waiting for transfers between devices  3.73 us (2%)
    all_gather x11, blocking collectives, gather(): lax.all_gather(block_, axis, axis=0, tiled=True, axis_index_groups=groups)  96.6 us
    all_to_all x2, blocking collectives, exchange(): return lax.all_to_all(blocks, 'dp', split_axis=0, concat_axis=0, tiled=True)  56.4 us
    all_gather x1, blocking collectives, per_device(): g = lax.all_gather(grad_top[0], 'chan', axis=1, tiled=True)  20 us
    pallas_call x2, Pallas kernels, first_block(): pl.pallas_call(kernel, out_shape=(shape_of((chans, positions), BF16), ful...  11.4 us
    pallas_call x3, Pallas kernels, wide_block(): pl.pallas_call(kernel, out_shape=shape_of((chans, positions), BF16), in_s...  10.1 us
  transfers between devices with their start and end apart: 2, of which 1 were waited for; matrix products, arithmetic and copies ran while one was open for 0% of the time, Pallas kernels for 6%

profile of v7, /device:TPU:6, one launch (start us, length us, event | category | flops | bytes accessed | tf_op | source)
XLA Modules:
  0.0 230.3 jit_solution(15081282103804424149)
XLA Ops:
  7.2 0.0 copy-start.21
  7.2 0.0 copy-start.20
  7.2 0.0 copy-start.2
  7.2 0.0 copy-start.16
  7.2 0.0 copy-start.17
  7.2 0.0 copy-start.18
  7.2 0.0 all-gather.5.cloned.1.call-start
  7.3 2.7 %prepare.1 = (bf16[96,2304]{1,0:T(8,128)(2,1)}, bf16[96,2304]{1,0:T(8,128)(2,1)}) custom-call(bf16[1,2,96,1536]{3,2,1,0:T(8,128)(2,1)} %refs_13_.1, bf16[1,2,96,432]{3,2,1,0:T(8,128)(2,1)} %wc_ref.5, bf16[1,1,96,256]{3,2,1,0:T(8,128)(2,1)} %refs_14_.1, bf16[1,1,96,256]{3,2,1,0:T(8,128)(2,1)} %refs_15_.1, f32[1,2,96]{2,1,0:T(2,128)} %refs_16_.1, ...), custom_call_target="tpu_custom_call" | custom-call | tf_op jit(solution)/shard_map/prepare/pallas_call | solution.py:118
  9.9 0.0 all-gather.5.cloned.1.call-update
  10.0 0.0 all-gather.7.cloned.1.call-start
  10.0 0.7 all-gather.7.cloned.1.call-update
  10.7 20.0 %all-gather = bf16[1,1536,256]{1,2,0:T(8,128)(2,1)S(1)} all-gather(bf16[1,1536,16]{1,2,0:T(8,128)(2,1)} %param.9), channel_id=2, replica_groups=mesh['segment'=4,'chan'=16,'dp'=8] {'chan'}, dimensions={2}, use_global_device_ids=true | all-gather | bytes 835584 | tf_op jit(solution)/shard_map/all_gather | solution.py:594
  30.7 0.3 copy.15
  31.0 0.0 copy-start.9
  31.0 0.1 pad_add_fusion.flags_ref.refs_0_
  31.1 0.0 copy-done.21
  31.1 0.0 copy-done.20
  31.1 0.0 copy-done.2
  31.1 0.0 copy-done.16
  31.1 0.0 copy-done.18
  31.1 1.5 own_block.3
  32.6 21.6 %all_gather.43.g_ref = bf16[1536,256]{1,0:T(8,128)(2,1)S(1)} all-gather(bf16[96,256]{1,0:T(8,128)(2,1)S(1)} %own_block.3), channel_id=1, replica_groups=mesh['segment'=4,'chan'=16,'dp'=8] {'chan'}, dimensions={0}, use_global_device_ids=true | all-gather | bytes 835584 | tf_op jit(solution)/shard_map/all_gather | solution.py:554
  54.2 0.0 copy-done.17
  54.2 1.5 own_block.4
  55.7 4.8 %all_gather.45 = bf16[192,256]{1,0:T(8,128)(2,1)S(1)} all-gather(bf16[96,256]{1,0:T(8,128)(2,1)S(1)} %own_block.4), channel_id=1, replica_groups={{0,128},{256,384},{1,129},{257,385},{2,130},{258,386},{3,131},{259,387}..., dimensions={0}, use_global_device_ids=true | all-gather | bytes 147456 | tf_op jit(solution)/shard_map/all_gather | solution.py:554
  60.5 19.2 %all_gather.46 = bf16[1536,256]{1,0:T(8,128)(2,1)S(1)} all-gather(bf16[96,256]{1,0:T(8,128)(2,1)S(1)} %slice.12), channel_id=1, replica_groups=mesh['segment'=4,'chan'=16,'dp'=8] {'chan'}, dimensions={0}, use_global_device_ids=true | all-gather | bytes 835584 | tf_op jit(solution)/shard_map/all_gather | solution.py:554
  79.7 2.3 copy-done
  82.0 5.7 %first_block.2 = (bf16[768,256]{1,0:T(8,128)(2,1)S(1)}, f32[768,256]{1,0:T(8,128)S(1)}, f32[768,256]{1,0:T(8,128)S(1)}) custom-call(s32[2]{0:T(128)S(1)} %pad_add_fusion.flags_ref.refs_0_, bf16[8,2,96,256]{3,2,1,0:T(8,128)(2,1)S(1)} %bitcast.17, bf16[768,2304]{1,0:T(8,128)(2,1)S(1)} %copy-done), custom_call_target="tpu_custom_call" | custom-call | tf_op jit(solution)/shard_map/first_block/pallas_call | solution.py:298
  87.7 0.0 copy-done.9
  87.7 0.0 copy-done.10
  87.7 0.0 copy-start.12
  87.7 0.0 copy-start.14
  87.7 2.4 %all_gather.47.g_ref = bf16[1536,256]{1,0:T(8,128)(2,1)S(1)} all-gather(bf16[768,256]{1,0:T(8,128)(2,1)S(1)} %get-tuple-element.26), channel_id=1, replica_groups={{0,8},{16,24},{32,40},{48,56},{64,72},{80,88},{96,104},{112,120},{1,9},..., dimensions={0}, use_global_device_ids=true | all-gather | bytes 1179648 | tf_op jit(solution)/shard_map/all_gather | solution.py:554
  90.1 1.5 own_block.5
  91.6 0.0 copy-done.4
  91.6 6.0 %all_gather.48 = bf16[192,256]{1,0:T(8,128)(2,1)S(1)} all-gather(bf16[96,256]{1,0:T(8,128)(2,1)S(1)} %own_block.5), channel_id=1, replica_groups={{0,384},{128,256},{1,385},{129,257},{2,386},{130,258},{3,387},{131,259}..., dimensions={0}, use_global_device_ids=true | all-gather | bytes 147456 | tf_op jit(solution)/shard_map/all_gather | solution.py:554
  97.6 21.3 %all_gather.49.g_ref = bf16[1536,256]{1,0:T(8,128)(2,1)S(1)} all-gather(bf16[96,256]{1,0:T(8,128)(2,1)S(1)} %slice.13), channel_id=1, replica_groups=mesh['segment'=4,'chan'=16,'dp'=8] {'chan'}, dimensions={0}, use_global_device_ids=true | all-gather | bytes 835584 | tf_op jit(solution)/shard_map/all_gather | solution.py:554
  118.9 3.4 %wide_block.3 = bf16[768,256]{1,0:T(8,128)(2,1)S(1)} custom-call(s32[2]{0:T(128)S(1)} %pad_add_fusion.flags_ref.refs_0_, bf16[1536,256]{1,0:T(8,128)(2,1)S(1)} %all_gather.49.g_ref, bf16[768,2304]{1,0:T(8,128)(2,1)S(1)} %copy-done, f32[768,256]{1,0:T(8,128)S(1)} %get-tuple-element.27.xhat_ref, f32[768,256]{1,0:T(8,128)S(1)} %get-tuple-element.28.rate_ref), custom_call_target="tpu_custom_call" | custom-call | tf_op jit(solution)/shard_map/wide_block/pallas_call | solution.py:352
  122.3 0.0 copy-done.12
  122.3 0.0 copy-done.14
  122.3 0.0 copy-done.11
  122.3 2.5 %all_gather.50 = bf16[1536,256]{1,0:T(8,128)(2,1)S(1)} all-gather(bf16[768,256]{1,0:T(8,128)(2,1)S(1)} %wide_block.3), channel_id=1, replica_groups={{0,8},{16,24},{32,40},{48,56},{64,72},{80,88},{96,104},{112,120},{1,9},..., dimensions={0}, use_global_device_ids=true | all-gather | bytes 1179648 | tf_op jit(solution)/shard_map/all_gather | solution.py:554
  124.8 0.0 copy-done.5
  124.9 3.0 %all-gather.7.cloned.1.call-done.pack_ref = bf16[768,2304]{1,0:T(8,128)(2,1)} async-done(((bf16[96,2304]{1,0:T(8,128)(2,1)}), bf16[768,2304]{1,0:T(8,128)(2,1)}) %all-gather.7.cloned.1.call-update) | async-done | bytes 3538960 | tf_op jit(solution)/shard_map/all_gather | solution.py:584
  127.9 2.0 copy-done.3
  129.9 5.7 %first_block.3 = (bf16[768,256]{1,0:T(8,128)(2,1)S(1)}, f32[768,256]{1,0:T(8,128)S(1)}, f32[768,256]{1,0:T(8,128)S(1)}) custom-call(s32[2]{0:T(128)S(1)} %pad_add_fusion.flags_ref.refs_0_, bf16[2,8,96,256]{3,2,1,0:T(8,128)(2,1)S(1)} %bitcast.24, bf16[768,2304]{1,0:T(8,128)(2,1)S(1)} %copy-done.3), custom_call_target="tpu_custom_call" | custom-call | tf_op jit(solution)/shard_map/first_block/pallas_call | solution.py:298
  135.6 11.6 %all_gather.52 = bf16[1536,256]{1,0:T(8,128)(2,1)S(1)} all-gather(bf16[768,256]{1,0:T(8,128)(2,1)S(1)} %get-tuple-element.32), channel_id=1, replica_groups={{0,128},{256,384},{1,129},{257,385},{2,130},{258,386},{3,131},{259,387}..., dimensions={0}, use_global_device_ids=true | all-gather | bytes 1179648 | tf_op jit(solution)/shard_map/all_gather | solution.py:554
  147.2 2.4 %all_gather.53.g_ref = bf16[1536,256]{1,0:T(8,128)(2,1)S(1)} all-gather(bf16[768,256]{1,0:T(8,128)(2,1)S(1)} %slice.14), channel_id=1, replica_groups={{0,8},{16,24},{32,40},{48,56},{64,72},{80,88},{96,104},{112,120},{1,9},..., dimensions={0}, use_global_device_ids=true | all-gather | bytes 1179648 | tf_op jit(solution)/shard_map/all_gather | solution.py:554
  149.5 0.0 copy-done.7
  149.5 0.0 copy-done.1
  149.5 0.0 copy-done.13
  149.5 0.0 copy-done.15
  149.6 0.0 copy-start.6
  149.6 3.4 %wide_block.4 = bf16[768,256]{1,0:T(8,128)(2,1)S(1)} custom-call(s32[2]{0:T(128)S(1)} %pad_add_fusion.flags_ref.refs_0_, bf16[1536,256]{1,0:T(8,128)(2,1)S(1)} %all_gather.53.g_ref, bf16[768,2304]{1,0:T(8,128)(2,1)S(1)} %copy-done.1, f32[768,256]{1,0:T(8,128)S(1)} %copy-done.13, f32[768,256]{1,0:T(8,128)S(1)} %copy-done.15), custom_call_target="tpu_custom_call" | custom-call | tf_op jit(solution)/shard_map/wide_block/pallas_call | solution.py:352
  152.9 2.4 %all_gather.54.g_ref = bf16[1536,256]{1,0:T(8,128)(2,1)S(1)} all-gather(bf16[768,256]{1,0:T(8,128)(2,1)S(1)} %wide_block.4), channel_id=1, replica_groups={{0,8},{16,24},{32,40},{48,56},{64,72},{80,88},{96,104},{112,120},{1,9},..., dimensions={0}, use_global_device_ids=true | all-gather | bytes 1179648 | tf_op jit(solution)/shard_map/all_gather | solution.py:554
  155.3 0.0 copy-done.6
  155.3 0.0 copy-done.19
  155.3 3.4 %wide_block.5 = bf16[768,256]{1,0:T(8,128)(2,1)S(1)} custom-call(s32[2]{0:T(128)S(1)} %pad_add_fusion.flags_ref.refs_0_, bf16[1536,256]{1,0:T(8,128)(2,1)S(1)} %all_gather.54.g_ref, bf16[768,2304]{1,0:T(8,128)(2,1)S(1)} %copy-done.3, f32[768,256]{1,0:T(8,128)S(1)} %get-tuple-element.33.xhat_ref, f32[768,256]{1,0:T(8,128)S(1)} %get-tuple-element.34.rate_ref), custom_call_target="tpu_custom_call" | custom-call | tf_op jit(solution)/shard_map/wide_block/pallas_call | solution.py:352
  158.7 2.5 %all_gather.55 = bf16[1536,256]{1,0:T(8,128)(2,1)} all-gather(bf16[768,256]{1,0:T(8,128)(2,1)S(1)} %wide_block.5), channel_id=1, replica_groups={{0,8},{16,24},{32,40},{48,56},{64,72},{80,88},{96,104},{112,120},{1,9},..., dimensions={0}, use_global_device_ids=true | all-gather | bytes 1179648 | tf_op jit(solution)/shard_map/all_gather | solution.py:554
  161.2 4.6 %weight_grads.1 = (bf16[8,192,256]{2,1,0:T(8,128)(2,1)}, bf16[16,1536]{1,0:T(8,128)(2,1)}) custom-call(s32[2]{0:T(128)} %copy-done.19, bf16[8,2,96,256]{3,2,1,0:T(8,128)(2,1)} %bitcast.29, bf16[2,8,96,256]{3,2,1,0:T(8,128)(2,1)} %bitcast.30, bf16[2,8,96,256]{3,2,1,0:T(8,128)(2,1)} %bitcast.25, bf16[2,8,96,256]{3,2,1,0:T(8,128)(2,1)} %bitcast.26, ...), custom_call_target="tpu_custom_call" | custom-call | tf_op jit(solution)/shard_map/weight_grads/pallas_call | solution.py:480
  165.8 31.7 %all_to_all.10.in_ref = bf16[8,192,256]{2,1,0:T(8,128)(2,1)S(1)} all-to-all(bf16[8,192,256]{2,1,0:T(8,128)(2,1)} %get-tuple-element.36), channel_id=1, replica_groups=mesh['segment'=4,'chan'=16,'dp'=8] {'dp'}, dimensions={0} | all-to-all | bytes 1572864 | tf_op jit(solution)/shard_map/all_to_all | solution.py:579
  197.5 0.1 sum_microbatches.1
  197.6 24.7 %all_to_all.11.in_ref = bf16[8,192,256]{2,1,0:T(8,128)(2,1)S(1)} all-to-all(bf16[8,192,256]{2,1,0:T(8,128)(2,1)S(1)} %sum_microbatches.1), channel_id=1, replica_groups=mesh['segment'=4,'chan'=16,'dp'=8] {'dp'}, dimensions={0} | all-to-all | bytes 1572864 | tf_op jit(solution)/shard_map/all_to_all | solution.py:579
  222.3 1.2 widen.1
  (17 shorter events, 0.1 us)
Async XLA Ops:
  7.2 23.9 %copy-start.21 = (f32[1,2,96]{2,1,0:T(2,128)S(1)}, f32[1,2,96]{2,1,0:T(2,128)}, u32[]{:S(2)}) copy-start(f32[1,2,96]{2,1,0:T(2,128)} %refs_17_.1) | copy-start | bytes 2308
  7.2 23.9 %copy-start.20 = (f32[1,2,96]{2,1,0:T(2,128)S(1)}, f32[1,2,96]{2,1,0:T(2,128)}, u32[]{:S(2)}) copy-start(f32[1,2,96]{2,1,0:T(2,128)} %refs_16_.1) | copy-start | bytes 2308
  7.2 23.9 %copy-start.2 = (bf16[1,2,96,1536]{3,2,1,0:T(8,128)(2,1)S(1)}, bf16[1,2,96,1536]{3,2,1,0:T(8,128)(2,1)}, u32[]{:S(2)}) copy-start(bf16[1,2,96,1536]{3,2,1,0:T(8,128)(2,1)} %refs_13_.1) | copy-start | bytes 1769476
  7.2 23.9 %copy-start.16 = (bf16[1,2,96,432]{3,2,1,0:T(8,128)(2,1)S(1)}, bf16[1,2,96,432]{3,2,1,0:T(8,128)(2,1)}, u32[]{:S(2)}) copy-start(bf16[1,2,96,432]{3,2,1,0:T(8,128)(2,1)} %wc_ref.5) | copy-start | bytes 497668
  7.2 47.0 %copy-start.17 = (bf16[1,1,96,256]{3,2,1,0:T(8,128)(2,1)S(1)}, bf16[1,1,96,256]{3,2,1,0:T(8,128)(2,1)}, u32[]{:S(2)}) copy-start(bf16[1,1,96,256]{3,2,1,0:T(8,128)(2,1)} %refs_14_.1) | copy-start | bytes 147460
  7.2 23.9 %copy-start.18 = (bf16[1,1,96,256]{3,2,1,0:T(8,128)(2,1)S(1)}, bf16[1,1,96,256]{3,2,1,0:T(8,128)(2,1)}, u32[]{:S(2)}) copy-start(bf16[1,1,96,256]{3,2,1,0:T(8,128)(2,1)} %refs_15_.1) | copy-start | bytes 147460
  7.2 72.4 %all-gather.5.cloned.1.call-start = ((), (), s32[]{:S(2)}) async-start(), calls=%async_computation.2 | async-start | bytes 3981312 | tf_op jit(solution)/shard_map/all_gather | solution.py:554
  10.0 117.9 %all-gather.7.cloned.1.call-start = ((), (), s32[]{:S(2)}) async-start(), calls=%async_computation.3 | async-start | bytes 3981312 | tf_op jit(solution)/shard_map/all_gather | solution.py:584
  31.0 56.7 %copy-start.9 = (bf16[1,1536,256]{2,1,0:T(8,128)(2,1)}, bf16[1,1536,256]{2,1,0:T(8,128)(2,1)S(1)}, u32[]{:S(2)}) copy-start(bf16[1,1536,256]{2,1,0:T(8,128)(2,1)S(1)} %copy.15) | copy-start | bytes 2359300
  31.1 124.2 %copy-start.19 = (s32[2]{0:T(128)}, s32[2]{0:T(128)S(1)}, u32[]{:S(2)}) copy-start(s32[2]{0:T(128)S(1)} %pad_add_fusion.flags_ref.refs_0_) | copy-start | bytes 28
  54.2 33.5 %copy-start.10 = (bf16[1536,256]{1,0:T(8,128)(2,1)}, bf16[1536,256]{1,0:T(8,128)(2,1)S(1)}, u32[]{:S(2)}) copy-start(bf16[1536,256]{1,0:T(8,128)(2,1)S(1)} %all_gather.43.g_ref) | copy-start | bytes 2359300
  79.7 11.9 %copy-start.4 = (bf16[1536,256]{1,0:T(8,128)(2,1)}, bf16[1536,256]{1,0:T(8,128)(2,1)S(1)}, u32[]{:S(2)}) copy-start(bf16[1536,256]{1,0:T(8,128)(2,1)S(1)} %all_gather.46) | copy-start | bytes 2359300
  79.7 2.3 copy-start
  87.7 34.6 %copy-start.12 = (f32[768,256]{1,0:T(8,128)}, f32[768,256]{1,0:T(8,128)S(1)}, u32[]{:S(2)}) copy-start(f32[768,256]{1,0:T(8,128)S(1)} %get-tuple-element.27.xhat_ref) | copy-start | bytes 2359300
  87.7 34.6 %copy-start.14 = (f32[768,256]{1,0:T(8,128)}, f32[768,256]{1,0:T(8,128)S(1)}, u32[]{:S(2)}) copy-start(f32[768,256]{1,0:T(8,128)S(1)} %get-tuple-element.28.rate_ref) | copy-start | bytes 2359300
  90.1 32.2 %copy-start.11 = (bf16[1536,256]{1,0:T(8,128)(2,1)}, bf16[1536,256]{1,0:T(8,128)(2,1)S(1)}, u32[]{:S(2)}) copy-start(bf16[1536,256]{1,0:T(8,128)(2,1)S(1)} %all_gather.47.g_ref) | copy-start | bytes 2359300
  118.9 6.0 %copy-start.5 = (bf16[1536,256]{1,0:T(8,128)(2,1)}, bf16[1536,256]{1,0:T(8,128)(2,1)S(1)}, u32[]{:S(2)}) copy-start(bf16[1536,256]{1,0:T(8,128)(2,1)S(1)} %all_gather.49.g_ref) | copy-start | bytes 2359300
  124.9 24.7 %copy-start.7 = (bf16[1536,256]{1,0:T(8,128)(2,1)}, bf16[1536,256]{1,0:T(8,128)(2,1)S(1)}, u32[]{:S(2)}) copy-start(bf16[1536,256]{1,0:T(8,128)(2,1)S(1)} %all_gather.50) | copy-start | bytes 2359300
  127.9 2.0 copy-start.3
  129.9 19.7 %copy-start.1 = (bf16[768,2304]{1,0:T(8,128)(2,1)S(1)}, bf16[768,2304]{1,0:T(8,128)(2,1)}, u32[]{:S(2)}) copy-start(bf16[768,2304]{1,0:T(8,128)(2,1)} %all-gather.5.cloned.1.call-done.pack_ref) | copy-start | bytes 10616836
  129.9 19.7 %copy-start.13 = (f32[768,256]{1,0:T(8,128)S(1)}, f32[768,256]{1,0:T(8,128)}, u32[]{:S(2)}) copy-start(f32[768,256]{1,0:T(8,128)} %copy-done.12) | copy-start | bytes 2359300
  129.9 19.7 %copy-start.15 = (f32[768,256]{1,0:T(8,128)S(1)}, f32[768,256]{1,0:T(8,128)}, u32[]{:S(2)}) copy-start(f32[768,256]{1,0:T(8,128)} %copy-done.14) | copy-start | bytes 2359300
  149.6 5.8 %copy-start.6 = (bf16[1536,256]{1,0:T(8,128)(2,1)}, bf16[1536,256]{1,0:T(8,128)(2,1)S(1)}, u32[]{:S(2)}) copy-start(bf16[1536,256]{1,0:T(8,128)(2,1)S(1)} %all_gather.53.g_ref) | copy-start | bytes 2359300
  155.3 5.9 %copy-start.8 = (bf16[1536,256]{1,0:T(8,128)(2,1)}, bf16[1536,256]{1,0:T(8,128)(2,1)S(1)}, u32[]{:S(2)}) copy-start(bf16[1536,256]{1,0:T(8,128)(2,1)S(1)} %all_gather.54.g_ref) | copy-start | bytes 2359300
Sparse Core Ops, SparseCore 0:
  10.1 61.8 all-gather.4
  74.2 53.6 all-gather.6

commit v8 on v7

--- a/solution.py
+++ b/solution.py
@@ -492,7 +492,7 @@
             pltpu.VMEM((2, chans, positions), BF16),
             pltpu.SemaphoreType.DMA((6,)),
         ],
-        compiler_params=vmem(56),
+        compiler_params=vmem(24),
         name="weight_grads",
     )(flags, *operands, proj_weight, h_one, h_two, gain, bias, *inputs)
 

time: 231 us -> 231 us (level)
    unnamed x44 -> x42, local copies, waits for them, and re-layouts: 4.37 us -> 5.88 us
where the time goes in v8:
time: 231 us; the launch traced here: 230 us
  blocking collectives  173 us (75%)
  Pallas kernels  33.6 us (15%)
  between operations  14.3 us (6%)
  local copies, waits for them, and re-layouts  6.18 us (3%)
  waiting for transfers between devices  3.08 us (1%)
    all_gather x11, blocking collectives, gather(): lax.all_gather(block_, axis, axis=0, tiled=True, axis_index_groups=groups)  95.7 us
    all_to_all x2, blocking collectives, exchange(): return lax.all_to_all(blocks, 'dp', split_axis=0, concat_axis=0, tiled=True)  57.3 us
    all_gather x1, blocking collectives, per_device(): g = lax.all_gather(grad_top[0], 'chan', axis=1, tiled=True)  20 us
    pallas_call x2, Pallas kernels, first_block(): pl.pallas_call(kernel, out_shape=(shape_of((chans, positions), BF16), ful...  11.4 us
    pallas_call x3, Pallas kernels, wide_block(): pl.pallas_call(kernel, out_shape=shape_of((chans, positions), BF16), in_s...  10.1 us
    unnamed x42, local copies, waits for them, and re-layouts  5.88 us
  transfers between devices with their start and end apart: 2, of which 1 were waited for; matrix products, arithmetic and copies ran while one was open for 0% of the time, Pallas kernels for 6%

profile of v8, /device:TPU:6, one launch (start us, length us, event | category | flops | bytes accessed | tf_op | source)
XLA Modules:
  0.0 230.2 jit_solution(1369256827780557465)
XLA Ops:
  7.2 0.0 copy-start.20
  7.2 0.0 copy-start.19
  7.2 0.0 copy-start.2
  7.2 0.0 copy-start.14
  7.2 0.0 copy-start.15
  7.2 0.0 copy-start.16
  7.2 0.0 all-gather.5.cloned.1.call-start
  7.3 2.7 %prepare.1 = (bf16[96,2304]{1,0:T(8,128)(2,1)}, bf16[96,2304]{1,0:T(8,128)(2,1)}) custom-call(bf16[1,2,96,1536]{3,2,1,0:T(8,128)(2,1)} %refs_13_.1, bf16[1,2,96,432]{3,2,1,0:T(8,128)(2,1)} %wc_ref.5, bf16[1,1,96,256]{3,2,1,0:T(8,128)(2,1)} %refs_14_.1, bf16[1,1,96,256]{3,2,1,0:T(8,128)(2,1)} %refs_15_.1, f32[1,2,96]{2,1,0:T(2,128)} %refs_16_.1, ...), custom_call_target="tpu_custom_call" | custom-call | tf_op jit(solution)/shard_map/prepare/pallas_call | solution.py:118
  10.0 0.0 all-gather.5.cloned.1.call-update
  10.0 0.0 all-gather.7.cloned.1.call-start
  10.0 0.7 all-gather.7.cloned.1.call-update
  10.8 20.0 %all-gather = bf16[1,1536,256]{1,2,0:T(8,128)(2,1)S(1)} all-gather(bf16[1,1536,16]{1,2,0:T(8,128)(2,1)} %param.9), channel_id=2, replica_groups=mesh['segment'=4,'chan'=16,'dp'=8] {'chan'}, dimensions={2}, use_global_device_ids=true | all-gather | bytes 835584 | tf_op jit(solution)/shard_map/all_gather | solution.py:594
  30.7 0.3 copy.15
  31.0 0.0 copy-start.4
  31.0 0.1 pad_add_fusion.flags_ref.refs_0_
  31.1 0.0 copy-done.20
  31.1 0.0 copy-done.19
  31.1 0.0 copy-done.2
  31.1 0.0 copy-done.14
  31.1 0.0 copy-done.16
  31.1 1.5 own_block.3
  32.6 21.6 %all_gather.43.g_ref = bf16[1536,256]{1,0:T(8,128)(2,1)S(1)} all-gather(bf16[96,256]{1,0:T(8,128)(2,1)S(1)} %own_block.3), channel_id=1, replica_groups=mesh['segment'=4,'chan'=16,'dp'=8] {'chan'}, dimensions={0}, use_global_device_ids=true | all-gather | bytes 835584 | tf_op jit(solution)/shard_map/all_gather | solution.py:554
  54.2 0.0 copy-done.15
  54.2 1.5 own_block.4
  55.7 0.0 copy-start.6
  55.7 0.9 copy-done.6
  56.6 4.8 %all_gather.45 = bf16[192,256]{1,0:T(8,128)(2,1)S(1)} all-gather(bf16[96,256]{1,0:T(8,128)(2,1)S(1)} %own_block.4), channel_id=1, replica_groups={{0,128},{256,384},{1,129},{257,385},{2,130},{258,386},{3,131},{259,387}..., dimensions={0}, use_global_device_ids=true | all-gather | bytes 147456 | tf_op jit(solution)/shard_map/all_gather | solution.py:554
  61.4 0.0 copy-done.4
  61.4 18.3 %all_gather.46 = bf16[1536,256]{1,0:T(8,128)(2,1)S(1)} all-gather(bf16[96,256]{1,0:T(8,128)(2,1)S(1)} %slice.12), channel_id=1, replica_groups=mesh['segment'=4,'chan'=16,'dp'=8] {'chan'}, dimensions={0}, use_global_device_ids=true | all-gather | bytes 835584 | tf_op jit(solution)/shard_map/all_gather | solution.py:554
  79.7 2.0 copy-done
  81.7 5.7 %first_block.2 = (bf16[768,256]{1,0:T(8,128)(2,1)S(1)}, f32[768,256]{1,0:T(8,128)S(1)}, f32[768,256]{1,0:T(8,128)S(1)}) custom-call(s32[2]{0:T(128)S(1)} %pad_add_fusion.flags_ref.refs_0_, bf16[8,2,96,256]{3,2,1,0:T(8,128)(2,1)S(1)} %bitcast.17, bf16[768,2304]{1,0:T(8,128)(2,1)S(1)} %copy-done), custom_call_target="tpu_custom_call" | custom-call | tf_op jit(solution)/shard_map/first_block/pallas_call | solution.py:298
  87.4 0.0 copy-start.10
  87.4 0.0 copy-start.12
  87.4 2.4 %all_gather.47.g_ref = bf16[1536,256]{1,0:T(8,128)(2,1)S(1)} all-gather(bf16[768,256]{1,0:T(8,128)(2,1)S(1)} %get-tuple-element.26), channel_id=1, replica_groups={{0,8},{16,24},{32,40},{48,56},{64,72},{80,88},{96,104},{112,120},{1,9},..., dimensions={0}, use_global_device_ids=true | all-gather | bytes 1179648 | tf_op jit(solution)/shard_map/all_gather | solution.py:554
  89.8 1.5 own_block.5
  91.3 0.0 copy-start.8
  91.3 0.9 copy-done.8
  92.2 6.0 %all_gather.48 = bf16[192,256]{1,0:T(8,128)(2,1)S(1)} all-gather(bf16[96,256]{1,0:T(8,128)(2,1)S(1)} %own_block.5), channel_id=1, replica_groups={{0,384},{128,256},{1,385},{129,257},{2,386},{130,258},{3,387},{131,259}..., dimensions={0}, use_global_device_ids=true | all-gather | bytes 147456 | tf_op jit(solution)/shard_map/all_gather | solution.py:554
  98.2 21.4 %all_gather.49.g_ref = bf16[1536,256]{1,0:T(8,128)(2,1)S(1)} all-gather(bf16[96,256]{1,0:T(8,128)(2,1)S(1)} %slice.13), channel_id=1, replica_groups=mesh['segment'=4,'chan'=16,'dp'=8] {'chan'}, dimensions={0}, use_global_device_ids=true | all-gather | bytes 835584 | tf_op jit(solution)/shard_map/all_gather | solution.py:554
  119.6 3.4 %wide_block.3 = bf16[768,256]{1,0:T(8,128)(2,1)S(1)} custom-call(s32[2]{0:T(128)S(1)} %pad_add_fusion.flags_ref.refs_0_, bf16[1536,256]{1,0:T(8,128)(2,1)S(1)} %all_gather.49.g_ref, bf16[768,2304]{1,0:T(8,128)(2,1)S(1)} %copy-done, f32[768,256]{1,0:T(8,128)S(1)} %get-tuple-element.27.xhat_ref, f32[768,256]{1,0:T(8,128)S(1)} %get-tuple-element.28.rate_ref), custom_call_target="tpu_custom_call" | custom-call | tf_op jit(solution)/shard_map/wide_block/pallas_call | solution.py:352
  123.0 0.0 copy-done.10
  123.0 0.0 copy-done.12
  123.0 2.5 %all_gather.50 = bf16[1536,256]{1,0:T(8,128)(2,1)S(1)} all-gather(bf16[768,256]{1,0:T(8,128)(2,1)S(1)} %wide_block.3), channel_id=1, replica_groups={{0,8},{16,24},{32,40},{48,56},{64,72},{80,88},{96,104},{112,120},{1,9},..., dimensions={0}, use_global_device_ids=true | all-gather | bytes 1179648 | tf_op jit(solution)/shard_map/all_gather | solution.py:554
  125.5 2.4 %all-gather.7.cloned.1.call-done.pack_ref = bf16[768,2304]{1,0:T(8,128)(2,1)} async-done(((bf16[96,2304]{1,0:T(8,128)(2,1)}), bf16[768,2304]{1,0:T(8,128)(2,1)}) %all-gather.7.cloned.1.call-update) | async-done | bytes 3538960 | tf_op jit(solution)/shard_map/all_gather | solution.py:584
  127.9 2.0 copy-done.3
  129.9 5.7 %first_block.3 = (bf16[768,256]{1,0:T(8,128)(2,1)S(1)}, f32[768,256]{1,0:T(8,128)S(1)}, f32[768,256]{1,0:T(8,128)S(1)}) custom-call(s32[2]{0:T(128)S(1)} %pad_add_fusion.flags_ref.refs_0_, bf16[2,8,96,256]{3,2,1,0:T(8,128)(2,1)S(1)} %bitcast.24, bf16[768,2304]{1,0:T(8,128)(2,1)S(1)} %copy-done.3), custom_call_target="tpu_custom_call" | custom-call | tf_op jit(solution)/shard_map/first_block/pallas_call | solution.py:298
  135.6 11.6 %all_gather.52 = bf16[1536,256]{1,0:T(8,128)(2,1)S(1)} all-gather(bf16[768,256]{1,0:T(8,128)(2,1)S(1)} %get-tuple-element.32), channel_id=1, replica_groups={{0,128},{256,384},{1,129},{257,385},{2,130},{258,386},{3,131},{259,387}..., dimensions={0}, use_global_device_ids=true | all-gather | bytes 1179648 | tf_op jit(solution)/shard_map/all_gather | solution.py:554
  147.2 2.4 %all_gather.53.g_ref = bf16[1536,256]{1,0:T(8,128)(2,1)S(1)} all-gather(bf16[768,256]{1,0:T(8,128)(2,1)S(1)} %slice.14), channel_id=1, replica_groups={{0,8},{16,24},{32,40},{48,56},{64,72},{80,88},{96,104},{112,120},{1,9},..., dimensions={0}, use_global_device_ids=true | all-gather | bytes 1179648 | tf_op jit(solution)/shard_map/all_gather | solution.py:554
  149.6 0.0 copy-done.1
  149.6 0.0 copy-done.11
  149.6 0.0 copy-done.13
  149.6 3.4 %wide_block.4 = bf16[768,256]{1,0:T(8,128)(2,1)S(1)} custom-call(s32[2]{0:T(128)S(1)} %pad_add_fusion.flags_ref.refs_0_, bf16[1536,256]{1,0:T(8,128)(2,1)S(1)} %all_gather.53.g_ref, bf16[768,2304]{1,0:T(8,128)(2,1)S(1)} %copy-done.1, f32[768,256]{1,0:T(8,128)S(1)} %copy-done.11, f32[768,256]{1,0:T(8,128)S(1)} %copy-done.13), custom_call_target="tpu_custom_call" | custom-call | tf_op jit(solution)/shard_map/wide_block/pallas_call | solution.py:352
  153.0 2.4 %all_gather.54.g_ref = bf16[1536,256]{1,0:T(8,128)(2,1)S(1)} all-gather(bf16[768,256]{1,0:T(8,128)(2,1)S(1)} %wide_block.4), channel_id=1, replica_groups={{0,8},{16,24},{32,40},{48,56},{64,72},{80,88},{96,104},{112,120},{1,9},..., dimensions={0}, use_global_device_ids=true | all-gather | bytes 1179648 | tf_op jit(solution)/shard_map/all_gather | solution.py:554
  155.3 0.0 copy-start.18
  155.4 3.4 %wide_block.5 = bf16[768,256]{1,0:T(8,128)(2,1)S(1)} custom-call(s32[2]{0:T(128)S(1)} %pad_add_fusion.flags_ref.refs_0_, bf16[1536,256]{1,0:T(8,128)(2,1)S(1)} %all_gather.54.g_ref, bf16[768,2304]{1,0:T(8,128)(2,1)S(1)} %copy-done.3, f32[768,256]{1,0:T(8,128)S(1)} %get-tuple-element.33.xhat_ref, f32[768,256]{1,0:T(8,128)S(1)} %get-tuple-element.34.rate_ref), custom_call_target="tpu_custom_call" | custom-call | tf_op jit(solution)/shard_map/wide_block/pallas_call | solution.py:352
  158.7 2.4 %all_gather.55 = bf16[1536,256]{1,0:T(8,128)(2,1)S(1)} all-gather(bf16[768,256]{1,0:T(8,128)(2,1)S(1)} %wide_block.5), channel_id=1, replica_groups={{0,8},{16,24},{32,40},{48,56},{64,72},{80,88},{96,104},{112,120},{1,9},..., dimensions={0}, use_global_device_ids=true | all-gather | bytes 1179648 | tf_op jit(solution)/shard_map/all_gather | solution.py:554
  161.1 0.0 copy-done.5
  161.1 0.0 copy-done.17
  161.1 0.0 copy-done.18
  161.1 3.7 %weight_grads.1 = (bf16[8,192,256]{2,1,0:T(8,128)(2,1)S(1)}, bf16[16,1536]{1,0:T(8,128)(2,1)}) custom-call(s32[2]{0:T(128)S(1)} %pad_add_fusion.flags_ref.refs_0_, bf16[8,2,96,256]{3,2,1,0:T(8,128)(2,1)S(1)} %bitcast.29, bf16[2,8,96,256]{3,2,1,0:T(8,128)(2,1)S(1)} %bitcast.30, bf16[2,8,96,256]{3,2,1,0:T(8,128)(2,1)S(1)} %bitcast.25, ...), custom_call_target="tpu_custom_call" | custom-call | tf_op jit(solution)/shard_map/weight_grads/pallas_call | solution.py:480
  164.8 32.6 %all_to_all.10.in_ref = bf16[8,192,256]{2,1,0:T(8,128)(2,1)S(1)} all-to-all(bf16[8,192,256]{2,1,0:T(8,128)(2,1)S(1)} %get-tuple-element.36), channel_id=1, replica_groups=mesh['segment'=4,'chan'=16,'dp'=8] {'dp'}, dimensions={0} | all-to-all | bytes 1572864 | tf_op jit(solution)/shard_map/all_to_all | solution.py:579
  197.4 0.1 sum_microbatches.1
  197.5 24.7 %all_to_all.11.in_ref = bf16[8,192,256]{2,1,0:T(8,128)(2,1)S(1)} all-to-all(bf16[8,192,256]{2,1,0:T(8,128)(2,1)S(1)} %sum_microbatches.1), channel_id=1, replica_groups=mesh['segment'=4,'chan'=16,'dp'=8] {'dp'}, dimensions={0} | all-to-all | bytes 1572864 | tf_op jit(solution)/shard_map/all_to_all | solution.py:579
  222.2 1.2 widen.1
  (15 shorter events, 0.1 us)
Async XLA Ops:
  7.2 23.9 %copy-start.20 = (f32[1,2,96]{2,1,0:T(2,128)S(1)}, f32[1,2,96]{2,1,0:T(2,128)}, u32[]{:S(2)}) copy-start(f32[1,2,96]{2,1,0:T(2,128)} %refs_17_.1) | copy-start | bytes 2308
  7.2 23.9 %copy-start.19 = (f32[1,2,96]{2,1,0:T(2,128)S(1)}, f32[1,2,96]{2,1,0:T(2,128)}, u32[]{:S(2)}) copy-start(f32[1,2,96]{2,1,0:T(2,128)} %refs_16_.1) | copy-start | bytes 2308
  7.2 23.9 %copy-start.2 = (bf16[1,2,96,1536]{3,2,1,0:T(8,128)(2,1)S(1)}, bf16[1,2,96,1536]{3,2,1,0:T(8,128)(2,1)}, u32[]{:S(2)}) copy-start(bf16[1,2,96,1536]{3,2,1,0:T(8,128)(2,1)} %refs_13_.1) | copy-start | bytes 1769476
  7.2 23.9 %copy-start.14 = (bf16[1,2,96,432]{3,2,1,0:T(8,128)(2,1)S(1)}, bf16[1,2,96,432]{3,2,1,0:T(8,128)(2,1)}, u32[]{:S(2)}) copy-start(bf16[1,2,96,432]{3,2,1,0:T(8,128)(2,1)} %wc_ref.5) | copy-start | bytes 497668
  7.2 47.0 %copy-start.15 = (bf16[1,1,96,256]{3,2,1,0:T(8,128)(2,1)S(1)}, bf16[1,1,96,256]{3,2,1,0:T(8,128)(2,1)}, u32[]{:S(2)}) copy-start(bf16[1,1,96,256]{3,2,1,0:T(8,128)(2,1)} %refs_14_.1) | copy-start | bytes 147460
  7.2 23.9 %copy-start.16 = (bf16[1,1,96,256]{3,2,1,0:T(8,128)(2,1)S(1)}, bf16[1,1,96,256]{3,2,1,0:T(8,128)(2,1)}, u32[]{:S(2)}) copy-start(bf16[1,1,96,256]{3,2,1,0:T(8,128)(2,1)} %refs_15_.1) | copy-start | bytes 147460
  7.2 72.5 %all-gather.5.cloned.1.call-start = ((), (), s32[]{:S(2)}) async-start(), calls=%async_computation.2 | async-start | bytes 3981312 | tf_op jit(solution)/shard_map/all_gather | solution.py:554
  10.0 117.9 %all-gather.7.cloned.1.call-start = ((), (), s32[]{:S(2)}) async-start(), calls=%async_computation.3 | async-start | bytes 3981312 | tf_op jit(solution)/shard_map/all_gather | solution.py:584
  31.0 30.4 %copy-start.4 = (bf16[1,1536,256]{2,1,0:T(8,128)(2,1)}, bf16[1,1536,256]{2,1,0:T(8,128)(2,1)S(1)}, u32[]{:S(2)}) copy-start(bf16[1,1536,256]{2,1,0:T(8,128)(2,1)S(1)} %copy.15) | copy-start | bytes 2359300
  55.7 0.9 copy-start.6
  79.7 2.0 copy-start
  87.4 35.6 %copy-start.10 = (f32[768,256]{1,0:T(8,128)}, f32[768,256]{1,0:T(8,128)S(1)}, u32[]{:S(2)}) copy-start(f32[768,256]{1,0:T(8,128)S(1)} %get-tuple-element.27.xhat_ref) | copy-start | bytes 2359300
  87.4 35.6 %copy-start.12 = (f32[768,256]{1,0:T(8,128)}, f32[768,256]{1,0:T(8,128)S(1)}, u32[]{:S(2)}) copy-start(f32[768,256]{1,0:T(8,128)S(1)} %get-tuple-element.28.rate_ref) | copy-start | bytes 2359300
  91.3 0.9 copy-start.8
  127.9 2.0 copy-start.3
  129.9 19.7 %copy-start.1 = (bf16[768,2304]{1,0:T(8,128)(2,1)S(1)}, bf16[768,2304]{1,0:T(8,128)(2,1)}, u32[]{:S(2)}) copy-start(bf16[768,2304]{1,0:T(8,128)(2,1)} %all-gather.5.cloned.1.call-done.pack_ref) | copy-start | bytes 10616836
  129.9 19.7 %copy-start.11 = (f32[768,256]{1,0:T(8,128)S(1)}, f32[768,256]{1,0:T(8,128)}, u32[]{:S(2)}) copy-start(f32[768,256]{1,0:T(8,128)} %copy-done.10) | copy-start | bytes 2359300
  129.9 19.7 %copy-start.13 = (f32[768,256]{1,0:T(8,128)S(1)}, f32[768,256]{1,0:T(8,128)}, u32[]{:S(2)}) copy-start(f32[768,256]{1,0:T(8,128)} %copy-done.12) | copy-start | bytes 2359300
  155.3 5.8 %copy-start.5 = (bf16[1,1536,256]{2,1,0:T(8,128)(2,1)S(1)}, bf16[1,1536,256]{2,1,0:T(8,128)(2,1)}, u32[]{:S(2)}) copy-start(bf16[1,1536,256]{2,1,0:T(8,128)(2,1)} %copy-done.4) | copy-start | bytes 2359300
  155.3 5.8 %copy-start.7 = (bf16[1536,256]{1,0:T(8,128)(2,1)S(1)}, bf16[1536,256]{1,0:T(8,128)(2,1)}, u32[]{:S(2)}) copy-start(bf16[1536,256]{1,0:T(8,128)(2,1)} %copy-done.6) | copy-start | bytes 2359300
  155.3 5.8 %copy-start.9 = (bf16[1536,256]{1,0:T(8,128)(2,1)S(1)}, bf16[1536,256]{1,0:T(8,128)(2,1)}, u32[]{:S(2)}) copy-start(bf16[1536,256]{1,0:T(8,128)(2,1)} %copy-done.8) | copy-start | bytes 2359300
  155.3 5.8 %copy-start.17 = (bf16[1,1,96,256]{3,2,1,0:T(8,128)(2,1)S(1)}, bf16[1,1,96,256]{3,2,1,0:T(8,128)(2,1)}, u32[]{:S(2)}) copy-start(bf16[1,1,96,256]{3,2,1,0:T(8,128)(2,1)} %refs_18_.1) | copy-start | bytes 147460
  155.3 5.8 %copy-start.18 = (bf16[1,1,96,256]{3,2,1,0:T(8,128)(2,1)S(1)}, bf16[1,1,96,256]{3,2,1,0:T(8,128)(2,1)}, u32[]{:S(2)}) copy-start(bf16[1,1,96,256]{3,2,1,0:T(8,128)(2,1)} %refs_19_.1) | copy-start | bytes 147460
Sparse Core Ops, SparseCore 0:
  10.1 61.3 all-gather.4
  73.6 54.2 all-gather.6

commit v9 on v8

--- a/solution.py
+++ b/solution.py
@@ -65,23 +65,32 @@
 
 def prepare_kernel(*refs):
     pack_refs = (refs[6], refs[7])
-    w_ref, wc_ref, h1_ref, h2_ref, gain_ref, bias_ref, sems = refs[8:]
+    w_ref, h_refs = refs[0], refs[2:4]
+    wc_ref, gain_ref, bias_ref, taps_ref, sems = refs[8:]
+    chans, width = w_ref.shape[2:]
     copies = [
-        pltpu.make_async_copy(refs[i], refs[8 + i], sems.at[i]) for i in range(6)
+        pltpu.make_async_copy(a, to, sems.at[i])
+        for i, (a, to) in enumerate(((refs[1], wc_ref), (refs[4], gain_ref), (refs[5], bias_ref)))
     ]
+    for b in (1, 0):
+        copies += [
+            pltpu.make_async_copy(
+                w_ref.at[0, b], pack_refs[b].at[:, :width], sems.at[3 + 3 * b]
+            ),
+            pltpu.make_async_copy(
+                h_refs[b].at[0, 0], pack_refs[b].at[:, width + TAIL :], sems.at[4 + 3 * b]
+            ),
+        ]
     for copy in copies:
         copy.start()
-    for copy in copies:
+    for copy in copies[:3]:
         copy.wait()
-    chans, width = w_ref.shape[2:]
     taps = wc_ref.shape[3]
     lane = lax.broadcasted_iota(jnp.int32, (chans, TAIL - 384), 1)
     down = lax.broadcasted_iota(jnp.int32, (GS, GS), 0)
     across = lax.broadcasted_iota(jnp.int32, (GS, GS), 1)
     same = jnp.where(down == across, 1.0, 0.0).astype(BF16)
-    for b, h_ref in ((1, h2_ref), (0, h1_ref)):
-        pack_ref = pack_refs[b]
-        pack_ref[:, :width] = w_ref[0, b]
+    for b in (1, 0):
         turned = []
         for q in range(0, chans, GS):
             taps_w = [
@@ -97,7 +106,7 @@
                 jnp.concatenate([*taps_w, jnp.zeros((GS, TAIL - taps), F32)], axis=1)
             )
         turned = jnp.concatenate(turned, axis=0)
-        pack_ref[:, width : width + 384] = turned[:, :384].astype(BF16)
+        taps_ref[b, :, :384] = turned[:, :384].astype(BF16)
         last = turned[:, 384:]
         at = taps - 384
         for whole in columns_of(gain_ref, bias_ref, b):
@@ -107,8 +116,15 @@
                 rest = rest - piece
                 last = jnp.where(lane == at, piece, last)
                 at += 1
-        pack_ref[:, width + 384 : width + TAIL] = last.astype(BF16)
-        pack_ref[:, width + TAIL :] = h_ref[0, 0]
+        taps_ref[b, :, 384:] = last.astype(BF16)
+        copies.append(
+            pltpu.make_async_copy(
+                taps_ref.at[b], pack_refs[b].at[:, width : width + TAIL], sems.at[5 + 3 * b]
+            )
+        )
+        copies[-1].start()
+    for copy in copies[3:]:
+        copy.wait()
 
 
 def prepare(*operands):
@@ -119,9 +135,9 @@
         prepare_kernel,
         out_shape=(pack, pack),
         in_specs=[ANY] * 6,
-        out_specs=[VMEM] * 2,
-        scratch_shapes=[pltpu.VMEM(x.shape, x.dtype) for x in operands]
-        + [pltpu.SemaphoreType.DMA((6,))],
+        out_specs=[ANY] * 2,
+        scratch_shapes=[pltpu.VMEM(operands[i].shape, operands[i].dtype) for i in (1, 4, 5)]
+        + [pltpu.VMEM((2, chans, TAIL), BF16), pltpu.SemaphoreType.DMA((9,))],
         compiler_params=vmem(56),
         name="prepare",
     )(*operands)

time: 231 us -> 250 us (1.082)
  Pallas kernels: 33.6 us -> 52.9 us
    pallas_call x1, Pallas kernels: 2.69 us -> 22 us  [prepare(): pl.pallas_call(prepare_kernel, out_shape=(pack, pack), in_specs=[ANY] * 6...]
  transfers between devices with their start and end apart: 2 -> 2, of which waited for: 1 -> 1; matrix products, arithmetic and copies ran while one was open for 0% -> 0% of each run, Pallas kernels for 6% -> 5%
where the time goes in v9:
time: 250 us
  blocking collectives  173 us (69%)
  Pallas kernels  52.9 us (21%)
  between operations  14.3 us (6%)
  local copies, waits for them, and re-layouts  6.18 us (2%)
  waiting for transfers between devices  3.08 us (1%)
    all_gather x11, blocking collectives, gather(): lax.all_gather(block_, axis, axis=0, tiled=True, axis_index_groups=groups)  95.6 us
    all_to_all x2, blocking collectives, exchange(): return lax.all_to_all(blocks, 'dp', split_axis=0, concat_axis=0, tiled=True)  57.3 us
    pallas_call x1, Pallas kernels, prepare(): pl.pallas_call(prepare_kernel, out_shape=(pack, pack), in_specs=[ANY] * 6...  22 us
    all_gather x1, blocking collectives, per_device(): g = lax.all_gather(grad_top[0], 'chan', axis=1, tiled=True)  20 us
    pallas_call x2, Pallas kernels, first_block(): pl.pallas_call(kernel, out_shape=(shape_of((chans, positions), BF16), ful...  11.4 us
    pallas_call x3, Pallas kernels, wide_block(): pl.pallas_call(kernel, out_shape=shape_of((chans, positions), BF16), in_s...  10.1 us
    unnamed x42, local copies, waits for them, and re-layouts  5.88 us
  transfers between devices with their start and end apart: 2, of which 1 were waited for; matrix products, arithmetic and copies ran while one was open for 0% of the time, Pallas kernels for 5%

profile of v9, /device:TPU:6, one launch (start us, length us, event | category | flops | bytes accessed | tf_op | source)
XLA Modules:
  0.0 249.6 jit_solution(11344846877528994503)
XLA Ops:
  7.2 0.0 copy-start.20
  7.2 0.0 copy-start.19
  7.2 0.0 copy-start.2
  7.2 0.0 copy-start.14
  7.2 0.0 copy-start.15
  7.2 0.0 copy-start.16
  7.2 0.0 all-gather.5.cloned.1.call-start
  7.3 22.0 %prepare.1 = (bf16[96,2304]{1,0:T(8,128)(2,1)}, bf16[96,2304]{1,0:T(8,128)(2,1)}) custom-call(bf16[1,2,96,1536]{3,2,1,0:T(8,128)(2,1)} %refs_13_.1, bf16[1,2,96,432]{3,2,1,0:T(8,128)(2,1)} %wc_ref.5, bf16[1,1,96,256]{3,2,1,0:T(8,128)(2,1)} %refs_14_.1, bf16[1,1,96,256]{3,2,1,0:T(8,128)(2,1)} %refs_15_.1, f32[1,2,96]{2,1,0:T(2,128)} %refs_16_.1, ...), custom_call_target="tpu_custom_call" | custom-call | tf_op jit(solution)/shard_map/prepare/pallas_call | solution.py:134
  29.3 0.0 all-gather.5.cloned.1.call-update
  29.3 0.0 all-gather.7.cloned.1.call-start
  29.4 0.7 all-gather.7.cloned.1.call-update
  30.1 20.0 %all-gather = bf16[1,1536,256]{1,2,0:T(8,128)(2,1)S(1)} all-gather(bf16[1,1536,16]{1,2,0:T(8,128)(2,1)} %param.9), channel_id=2, replica_groups=mesh['segment'=4,'chan'=16,'dp'=8] {'chan'}, dimensions={2}, use_global_device_ids=true | all-gather | bytes 835584 | tf_op jit(solution)/shard_map/all_gather | solution.py:610
  50.1 0.3 copy.15
  50.4 0.0 copy-start.4
  50.4 0.1 pad_add_fusion.flags_ref.refs_0_
  50.5 0.0 copy-done.20
  50.5 0.0 copy-done.19
  50.5 0.0 copy-done.2
  50.5 0.0 copy-done.14
  50.5 0.0 copy-done.16
  50.5 1.5 own_block.3
  52.0 21.6 %all_gather.43.g_ref = bf16[1536,256]{1,0:T(8,128)(2,1)S(1)} all-gather(bf16[96,256]{1,0:T(8,128)(2,1)S(1)} %own_block.3), channel_id=1, replica_groups=mesh['segment'=4,'chan'=16,'dp'=8] {'chan'}, dimensions={0}, use_global_device_ids=true | all-gather | bytes 835584 | tf_op jit(solution)/shard_map/all_gather | solution.py:570
  73.6 0.0 copy-done.15
  73.6 1.5 own_block.4
  75.1 0.0 copy-start.6
  75.1 0.9 copy-done.6
  76.0 4.8 %all_gather.45 = bf16[192,256]{1,0:T(8,128)(2,1)S(1)} all-gather(bf16[96,256]{1,0:T(8,128)(2,1)S(1)} %own_block.4), channel_id=1, replica_groups={{0,128},{256,384},{1,129},{257,385},{2,130},{258,386},{3,131},{259,387}..., dimensions={0}, use_global_device_ids=true | all-gather | bytes 147456 | tf_op jit(solution)/shard_map/all_gather | solution.py:570
  80.7 0.0 copy-done.4
  80.7 18.3 %all_gather.46 = bf16[1536,256]{1,0:T(8,128)(2,1)S(1)} all-gather(bf16[96,256]{1,0:T(8,128)(2,1)S(1)} %slice.12), channel_id=1, replica_groups=mesh['segment'=4,'chan'=16,'dp'=8] {'chan'}, dimensions={0}, use_global_device_ids=true | all-gather | bytes 835584 | tf_op jit(solution)/shard_map/all_gather | solution.py:570
  99.1 2.0 copy-done
  101.1 5.7 %first_block.2 = (bf16[768,256]{1,0:T(8,128)(2,1)S(1)}, f32[768,256]{1,0:T(8,128)S(1)}, f32[768,256]{1,0:T(8,128)S(1)}) custom-call(s32[2]{0:T(128)S(1)} %pad_add_fusion.flags_ref.refs_0_, bf16[8,2,96,256]{3,2,1,0:T(8,128)(2,1)S(1)} %bitcast.17, bf16[768,2304]{1,0:T(8,128)(2,1)S(1)} %copy-done), custom_call_target="tpu_custom_call" | custom-call | tf_op jit(solution)/shard_map/first_block/pallas_call | solution.py:314
  106.8 0.0 copy-start.10
  106.8 0.0 copy-start.12
  106.8 2.4 all_gather.47.g_ref
  109.1 1.5 own_block.5
  110.6 0.0 copy-start.8
  110.6 0.9 copy-done.8
  111.6 6.0 %all_gather.48 = bf16[192,256]{1,0:T(8,128)(2,1)S(1)} all-gather(bf16[96,256]{1,0:T(8,128)(2,1)S(1)} %own_block.5), channel_id=1, replica_groups={{0,384},{128,256},{1,385},{129,257},{2,386},{130,258},{3,387},{131,259}..., dimensions={0}, use_global_device_ids=true | all-gather | bytes 147456 | tf_op jit(solution)/shard_map/all_gather | solution.py:570
  117.5 21.4 %all_gather.49.g_ref = bf16[1536,256]{1,0:T(8,128)(2,1)S(1)} all-gather(bf16[96,256]{1,0:T(8,128)(2,1)S(1)} %slice.13), channel_id=1, replica_groups=mesh['segment'=4,'chan'=16,'dp'=8] {'chan'}, dimensions={0}, use_global_device_ids=true | all-gather | bytes 835584 | tf_op jit(solution)/shard_map/all_gather | solution.py:570
  138.9 3.4 %wide_block.3 = bf16[768,256]{1,0:T(8,128)(2,1)S(1)} custom-call(s32[2]{0:T(128)S(1)} %pad_add_fusion.flags_ref.refs_0_, bf16[1536,256]{1,0:T(8,128)(2,1)S(1)} %all_gather.49.g_ref, bf16[768,2304]{1,0:T(8,128)(2,1)S(1)} %copy-done, f32[768,256]{1,0:T(8,128)S(1)} %get-tuple-element.27.xhat_ref, f32[768,256]{1,0:T(8,128)S(1)} %get-tuple-element.28.rate_ref), custom_call_target="tpu_custom_call" | custom-call | tf_op jit(solution)/shard_map/wide_block/pallas_call | solution.py:368
  142.3 0.0 copy-done.10
  142.3 0.0 copy-done.12
  142.3 2.5 %all_gather.50 = bf16[1536,256]{1,0:T(8,128)(2,1)S(1)} all-gather(bf16[768,256]{1,0:T(8,128)(2,1)S(1)} %wide_block.3), channel_id=1, replica_groups={{0,8},{16,24},{32,40},{48,56},{64,72},{80,88},{96,104},{112,120},{1,9},..., dimensions={0}, use_global_device_ids=true | all-gather | bytes 1179648 | tf_op jit(solution)/shard_map/all_gather | solution.py:570
  144.9 2.4 all-gather.7.cloned.1.call-done.pack_ref
  147.2 2.0 copy-done.3
  149.2 5.7 %first_block.3 = (bf16[768,256]{1,0:T(8,128)(2,1)S(1)}, f32[768,256]{1,0:T(8,128)S(1)}, f32[768,256]{1,0:T(8,128)S(1)}) custom-call(s32[2]{0:T(128)S(1)} %pad_add_fusion.flags_ref.refs_0_, bf16[2,8,96,256]{3,2,1,0:T(8,128)(2,1)S(1)} %bitcast.24, bf16[768,2304]{1,0:T(8,128)(2,1)S(1)} %copy-done.3), custom_call_target="tpu_custom_call" | custom-call | tf_op jit(solution)/shard_map/first_block/pallas_call | solution.py:314
  154.9 11.6 %all_gather.52 = bf16[1536,256]{1,0:T(8,128)(2,1)S(1)} all-gather(bf16[768,256]{1,0:T(8,128)(2,1)S(1)} %get-tuple-element.32), channel_id=1, replica_groups={{0,128},{256,384},{1,129},{257,385},{2,130},{258,386},{3,131},{259,387}..., dimensions={0}, use_global_device_ids=true | all-gather | bytes 1179648 | tf_op jit(solution)/shard_map/all_gather | solution.py:570
  166.5 2.4 all_gather.53.g_ref
  168.9 0.0 copy-done.1
  168.9 0.0 copy-done.11
  168.9 0.0 copy-done.13
  168.9 3.4 %wide_block.4 = bf16[768,256]{1,0:T(8,128)(2,1)S(1)} custom-call(s32[2]{0:T(128)S(1)} %pad_add_fusion.flags_ref.refs_0_, bf16[1536,256]{1,0:T(8,128)(2,1)S(1)} %all_gather.53.g_ref, bf16[768,2304]{1,0:T(8,128)(2,1)S(1)} %copy-done.1, f32[768,256]{1,0:T(8,128)S(1)} %copy-done.11, f32[768,256]{1,0:T(8,128)S(1)} %copy-done.13), custom_call_target="tpu_custom_call" | custom-call | tf_op jit(solution)/shard_map/wide_block/pallas_call | solution.py:368
  172.3 2.4 all_gather.54.g_ref
  174.7 0.0 copy-start.18
  174.7 3.4 %wide_block.5 = bf16[768,256]{1,0:T(8,128)(2,1)S(1)} custom-call(s32[2]{0:T(128)S(1)} %pad_add_fusion.flags_ref.refs_0_, bf16[1536,256]{1,0:T(8,128)(2,1)S(1)} %all_gather.54.g_ref, bf16[768,2304]{1,0:T(8,128)(2,1)S(1)} %copy-done.3, f32[768,256]{1,0:T(8,128)S(1)} %get-tuple-element.33.xhat_ref, f32[768,256]{1,0:T(8,128)S(1)} %get-tuple-element.34.rate_ref), custom_call_target="tpu_custom_call" | custom-call | tf_op jit(solution)/shard_map/wide_block/pallas_call | solution.py:368
  178.0 2.4 all_gather.55
  180.4 0.0 copy-done.5
  180.4 0.0 copy-done.7
  180.4 0.0 copy-done.9
  180.4 3.6 %weight_grads.1 = (bf16[8,192,256]{2,1,0:T(8,128)(2,1)S(1)}, bf16[16,1536]{1,0:T(8,128)(2,1)}) custom-call(s32[2]{0:T(128)S(1)} %pad_add_fusion.flags_ref.refs_0_, bf16[8,2,96,256]{3,2,1,0:T(8,128)(2,1)S(1)} %bitcast.29, bf16[2,8,96,256]{3,2,1,0:T(8,128)(2,1)S(1)} %bitcast.30, bf16[2,8,96,256]{3,2,1,0:T(8,128)(2,1)S(1)} %bitcast.25, ...), custom_call_target="tpu_custom_call" | custom-call | tf_op jit(solution)/shard_map/weight_grads/pallas_call | solution.py:496
  184.1 32.6 %all_to_all.10.in_ref = bf16[8,192,256]{2,1,0:T(8,128)(2,1)S(1)} all-to-all(bf16[8,192,256]{2,1,0:T(8,128)(2,1)S(1)} %get-tuple-element.36), channel_id=1, replica_groups=mesh['segment'=4,'chan'=16,'dp'=8] {'dp'}, dimensions={0} | all-to-all | bytes 1572864 | tf_op jit(solution)/shard_map/all_to_all | solution.py:595
  216.8 0.1 sum_microbatches.1
  216.9 24.7 %all_to_all.11.in_ref = bf16[8,192,256]{2,1,0:T(8,128)(2,1)S(1)} all-to-all(bf16[8,192,256]{2,1,0:T(8,128)(2,1)S(1)} %sum_microbatches.1), channel_id=1, replica_groups=mesh['segment'=4,'chan'=16,'dp'=8] {'dp'}, dimensions={0} | all-to-all | bytes 1572864 | tf_op jit(solution)/shard_map/all_to_all | solution.py:595
  241.6 1.2 widen.1
  (15 shorter events, 0.1 us)
Async XLA Ops:
  7.2 43.3 %copy-start.20 = (f32[1,2,96]{2,1,0:T(2,128)S(1)}, f32[1,2,96]{2,1,0:T(2,128)}, u32[]{:S(2)}) copy-start(f32[1,2,96]{2,1,0:T(2,128)} %refs_17_.1) | copy-start | bytes 2308
  7.2 43.3 %copy-start.19 = (f32[1,2,96]{2,1,0:T(2,128)S(1)}, f32[1,2,96]{2,1,0:T(2,128)}, u32[]{:S(2)}) copy-start(f32[1,2,96]{2,1,0:T(2,128)} %refs_16_.1) | copy-start | bytes 2308
  7.2 43.3 %copy-start.2 = (bf16[1,2,96,1536]{3,2,1,0:T(8,128)(2,1)S(1)}, bf16[1,2,96,1536]{3,2,1,0:T(8,128)(2,1)}, u32[]{:S(2)}) copy-start(bf16[1,2,96,1536]{3,2,1,0:T(8,128)(2,1)} %refs_13_.1) | copy-start | bytes 1769476
  7.2 43.3 %copy-start.14 = (bf16[1,2,96,432]{3,2,1,0:T(8,128)(2,1)S(1)}, bf16[1,2,96,432]{3,2,1,0:T(8,128)(2,1)}, u32[]{:S(2)}) copy-start(bf16[1,2,96,432]{3,2,1,0:T(8,128)(2,1)} %wc_ref.5) | copy-start | bytes 497668
  7.2 66.4 %copy-start.15 = (bf16[1,1,96,256]{3,2,1,0:T(8,128)(2,1)S(1)}, bf16[1,1,96,256]{3,2,1,0:T(8,128)(2,1)}, u32[]{:S(2)}) copy-start(bf16[1,1,96,256]{3,2,1,0:T(8,128)(2,1)} %refs_14_.1) | copy-start | bytes 147460
  7.2 43.3 %copy-start.16 = (bf16[1,1,96,256]{3,2,1,0:T(8,128)(2,1)S(1)}, bf16[1,1,96,256]{3,2,1,0:T(8,128)(2,1)}, u32[]{:S(2)}) copy-start(bf16[1,1,96,256]{3,2,1,0:T(8,128)(2,1)} %refs_15_.1) | copy-start | bytes 147460
  7.2 91.8 %all-gather.5.cloned.1.call-start = ((), (), s32[]{:S(2)}) async-start(), calls=%async_computation.2 | async-start | bytes 3981312 | tf_op jit(solution)/shard_map/all_gather | solution.py:570
  29.3 117.9 %all-gather.7.cloned.1.call-start = ((), (), s32[]{:S(2)}) async-start(), calls=%async_computation.3 | async-start | bytes 3981312 | tf_op jit(solution)/shard_map/all_gather | solution.py:600
  50.4 30.4 %copy-start.4 = (bf16[1,1536,256]{2,1,0:T(8,128)(2,1)}, bf16[1,1536,256]{2,1,0:T(8,128)(2,1)S(1)}, u32[]{:S(2)}) copy-start(bf16[1,1536,256]{2,1,0:T(8,128)(2,1)S(1)} %copy.15) | copy-start | bytes 2359300
  75.1 0.9 copy-start.6
  99.1 2.0 copy-start
  106.8 35.5 %copy-start.10 = (f32[768,256]{1,0:T(8,128)}, f32[768,256]{1,0:T(8,128)S(1)}, u32[]{:S(2)}) copy-start(f32[768,256]{1,0:T(8,128)S(1)} %get-tuple-element.27.xhat_ref) | copy-start | bytes 2359300
  106.8 35.5 %copy-start.12 = (f32[768,256]{1,0:T(8,128)}, f32[768,256]{1,0:T(8,128)S(1)}, u32[]{:S(2)}) copy-start(f32[768,256]{1,0:T(8,128)S(1)} %get-tuple-element.28.rate_ref) | copy-start | bytes 2359300
  110.6 0.9 copy-start.8
  147.2 2.0 copy-start.3
  149.2 19.7 %copy-start.1 = (bf16[768,2304]{1,0:T(8,128)(2,1)S(1)}, bf16[768,2304]{1,0:T(8,128)(2,1)}, u32[]{:S(2)}) copy-start(bf16[768,2304]{1,0:T(8,128)(2,1)} %all-gather.5.cloned.1.call-done.pack_ref) | copy-start | bytes 10616836
  149.2 19.7 %copy-start.11 = (f32[768,256]{1,0:T(8,128)S(1)}, f32[768,256]{1,0:T(8,128)}, u32[]{:S(2)}) copy-start(f32[768,256]{1,0:T(8,128)} %copy-done.10) | copy-start | bytes 2359300
  149.2 19.7 %copy-start.13 = (f32[768,256]{1,0:T(8,128)S(1)}, f32[768,256]{1,0:T(8,128)}, u32[]{:S(2)}) copy-start(f32[768,256]{1,0:T(8,128)} %copy-done.12) | copy-start | bytes 2359300
  174.6 5.8 %copy-start.5 = (bf16[1,1536,256]{2,1,0:T(8,128)(2,1)S(1)}, bf16[1,1536,256]{2,1,0:T(8,128)(2,1)}, u32[]{:S(2)}) copy-start(bf16[1,1536,256]{2,1,0:T(8,128)(2,1)} %copy-done.4) | copy-start | bytes 2359300
  174.7 5.8 %copy-start.7 = (bf16[1536,256]{1,0:T(8,128)(2,1)S(1)}, bf16[1536,256]{1,0:T(8,128)(2,1)}, u32[]{:S(2)}) copy-start(bf16[1536,256]{1,0:T(8,128)(2,1)} %copy-done.6) | copy-start | bytes 2359300
  174.7 5.8 %copy-start.9 = (bf16[1536,256]{1,0:T(8,128)(2,1)S(1)}, bf16[1536,256]{1,0:T(8,128)(2,1)}, u32[]{:S(2)}) copy-start(bf16[1536,256]{1,0:T(8,128)(2,1)} %copy-done.8) | copy-start | bytes 2359300
  174.7 5.8 %copy-start.17 = (bf16[1,1,96,256]{3,2,1,0:T(8,128)(2,1)S(1)}, bf16[1,1,96,256]{3,2,1,0:T(8,128)(2,1)}, u32[]{:S(2)}) copy-start(bf16[1,1,96,256]{3,2,1,0:T(8,128)(2,1)} %refs_18_.1) | copy-start | bytes 147460
  174.7 5.8 %copy-start.18 = (bf16[1,1,96,256]{3,2,1,0:T(8,128)(2,1)S(1)}, bf16[1,1,96,256]{3,2,1,0:T(8,128)(2,1)}, u32[]{:S(2)}) copy-start(bf16[1,1,96,256]{3,2,1,0:T(8,128)(2,1)} %refs_19_.1) | copy-start | bytes 147460
Sparse Core Ops, SparseCore 0:
  29.5 61.3 all-gather.4
  92.9 54.2 all-gather.6
